TPU v7x, 256 devices: a whole 4x4x8 slice. The times are simulated.
256 devices in a mesh: row: 128 (over y_hi, x, z, core), col: 2 (over y_lo).
Axes of the slice: x: 4, y: 4 (y_hi: 2, y_lo: 2; y = y_hi * 2 + y_lo), z: 8, core: 2. Of those that a mesh axis runs over, the one named last changes fastest.
Arguments:
- activations: bfloat16 [1024, 2048], P('row', 'col'), may hold values from -6 to 6
- out_grad: bfloat16 [1024, 2048], P('row', 'col'), may hold values from -6 to 6
- gate_blocks: bfloat16 [128, 2, 48, 128, 128], P('row', 'col'), may hold values from -0.09375 to 0.09375
- up_blocks: bfloat16 [128, 2, 48, 128, 128], P('row', 'col'), may hold values from -0.09375 to 0.09375
- down_blocks: bfloat16 [128, 2, 48, 128, 128], P('row', 'col'), may hold values from -0.046875 to 0.046875
- block_index: int32 [3, 128, 2, 48], replicated, may hold values from 0 to 56, as said below
- block_dest: int32 [3, 128, 2, 48], P(None, None, 'col'), may hold values from 0 to 192, as said below
Outputs:
- mixed_rows: bfloat16 [1024, 2048], P('row', 'col')
- input_grad: bfloat16 [1024, 2048], P('row', 'col')
- weight_grads: bfloat16 [3, 128, 2, 48, 128, 128], P(None, 'row', 'col')
Inputs may be any that keep to these rules, and one draw needn't show every extreme that they name: `block_index`: entries below 56 are live slots; within one list (m, r, c) they are distinct. The value 56 marks an unused slot, placed anywhere in the list. Each list has 8 to 48 live slots; for each matrix some list has exactly 8, and all four lists of some group g and column c have 48. `block_dest`: for a live slot the value is o * 48 + s: its gradient goes to row g * 4 + o of the same group and column, at place s; no two live slots of a group and column share a value; unused slots hold 192. For each matrix some owner's places 0 to 47 are all taken.
All inputs are finite; a program needn't handle non-finite values.
Results may differ from a plain program's by a relative error of at most 0.0049.
Values may be sent and summed in bfloat16 or wider, within the bound.
No kernel may reach another device: no remote copies, remote signals or barrier semaphores. Data moves between devices by JAX's collectives and lax.ppermute only.
A program may use at most 192 MiB of HBM per device.

v0:
```python
import jax
import jax.numpy as jnp
from jax import lax
from jax.sharding import PartitionSpec as P

FF = 28672
BLK = 128
QUARTERS = 4


def from_partner(value, axis, stride):
    mask = 2**stride
    pairs = [(source, source ^ mask) for source in range(lax.axis_size(axis))]
    return lax.ppermute(value, axis, pairs)


def shifted(value, axis, by):
    devices = lax.axis_size(axis)
    return lax.ppermute(value, axis, [(i, (i + by) % devices) for i in range(devices)])


def bit_value(row_index, bit_pos):
    return row_index // (1 << bit_pos) % 2


def collect_rows(values, first_bit, last_bit, axis_dim, row_index):
    for bit_pos in range(first_bit, last_bit):
        partner = from_partner(values, "row", bit_pos)
        high_side = bit_value(row_index, bit_pos) == 1
        values = jnp.where(
            high_side,
            jnp.concatenate([partner, values], axis_dim),
            jnp.concatenate([values, partner], axis_dim),
        )
    return values


def halve_sums(values, first_bit, last_bit, axis_dim, row_index):
    for bit_pos in reversed(range(first_bit, last_bit)):
        half_size = values.shape[axis_dim] // 2
        lower_half = lax.slice_in_dim(values, 0, half_size, axis=axis_dim)
        upper_half = lax.slice_in_dim(values, half_size, 2 * half_size, axis=axis_dim)
        high_side = bit_value(row_index, bit_pos) == 1
        kept_half = jnp.where(high_side, upper_half, lower_half)
        sent_half = jnp.where(high_side, lower_half, upper_half)
        values = kept_half + from_partner(sent_half, "row", bit_pos)
    return values


def group_sums(values, quarter_bits, row_index):
    values = halve_sums(values, 0, quarter_bits, 1, row_index)
    return lax.psum_scatter(values, "col", scatter_dimension=1, tiled=True)


def group_rows(values, quarter_bits, row_index):
    values = lax.all_gather(values, "col", axis=1, tiled=True)
    return collect_rows(values, 0, quarter_bits, 1, row_index)


def gate_slab(blocks, positions, slot_count, hidden_count):
    filled = jnp.zeros((slot_count, BLK, BLK), blocks.dtype).at[positions].set(blocks, mode="drop")
    feature_count = slot_count // hidden_count
    block_grid = filled.reshape(hidden_count, feature_count, BLK, BLK)
    return block_grid.transpose(1, 2, 0, 3).reshape(feature_count * BLK, hidden_count * BLK)


def down_slab(blocks, positions, slot_count, hidden_count):
    filled = jnp.zeros((slot_count, BLK, BLK), blocks.dtype).at[positions].set(blocks, mode="drop")
    feature_count = slot_count // hidden_count
    block_grid = filled.reshape(hidden_count, feature_count, BLK, BLK)
    return block_grid.transpose(0, 2, 1, 3).reshape(hidden_count * BLK, feature_count * BLK)


def gate_pieces(dense_slab, hidden_count):
    feature_count = dense_slab.shape[0] // BLK
    shaped = dense_slab.reshape(feature_count, BLK, hidden_count, BLK)
    return shaped.transpose(2, 0, 1, 3).reshape(hidden_count * feature_count, BLK, BLK)


def down_pieces(dense_slab, hidden_count):
    feature_count = dense_slab.shape[1] // BLK
    shaped = dense_slab.reshape(hidden_count, BLK, feature_count, BLK)
    return shaped.transpose(0, 2, 1, 3).reshape(hidden_count * feature_count, BLK, BLK)


def body(activations, out_grad, gate_blocks, up_blocks, down_blocks, block_index, block_dest):
    row_count = lax.axis_size("row")
    row_index = lax.axis_index("row")
    col_index = lax.axis_index("col")
    row_bits = row_count.bit_length() - 1
    quarter_bits = QUARTERS.bit_length() - 1
    group_count = row_count // QUARTERS
    group_index = row_index // QUARTERS
    quarter_index = row_index % QUARTERS
    group_tokens = activations.shape[0]
    feature_width = activations.shape[1]
    hidden_width = FF // group_count
    hidden_count = hidden_width // BLK
    feature_count = feature_width // BLK
    slot_count = hidden_count * feature_count
    capacity = gate_blocks.shape[2]
    all_index = lax.dynamic_index_in_dim(block_index, col_index, axis=2, keepdims=False)
    all_dest = block_dest[:, :, 0, :]
    own_index = lax.dynamic_index_in_dim(all_index, row_index, axis=1, keepdims=False)
    gathered = collect_rows(
        jnp.stack([activations, out_grad]), quarter_bits, row_bits, 1, row_index
    )
    inputs = gathered[0]
    upstream = gathered[1]
    w_gate = gate_slab(
        gate_blocks.reshape(capacity, BLK, BLK), own_index[0], slot_count, hidden_count
    )
    w_up = gate_slab(up_blocks.reshape(capacity, BLK, BLK), own_index[1], slot_count, hidden_count)
    w_down = down_slab(
        down_blocks.reshape(capacity, BLK, BLK), own_index[2], slot_count, hidden_count
    )
    partial_value = jnp.stack(
        [
            jnp.dot(inputs, w_gate, preferred_element_type=jnp.float32),
            jnp.dot(inputs, w_up, preferred_element_type=jnp.float32),
        ]
    )
    shares = group_sums(partial_value, quarter_bits, row_index)
    gate_share = shares[0]
    up_share = shares[1]
    sigmoid_gate = jax.nn.sigmoid(gate_share)
    silu_gate = gate_share * sigmoid_gate
    hidden_share = (silu_gate * up_share).astype(jnp.bfloat16)
    hidden = group_rows(hidden_share[None], quarter_bits, row_index)[0]
    down_part = jnp.dot(hidden, w_down, preferred_element_type=jnp.float32)

    def cycle_piece(offset):
        start_row = (group_index - offset + 2 * group_count) % group_count * group_tokens
        return lax.dynamic_slice_in_dim(down_part, start_row, group_tokens, 0)

    def cycle_turn(turn_index, carried):
        moved_sum = shifted(carried, "row", QUARTERS)
        return moved_sum + cycle_piece(turn_index + 1)

    mixed_rows = lax.fori_loop(1, group_count, cycle_turn, cycle_piece(1)).astype(jnp.bfloat16)
    contract_last = (((1,), (1,)), ((), ()))
    hidden_part = lax.dot_general(
        upstream, w_down, contract_last, preferred_element_type=jnp.float32
    )
    hidden_grad = group_sums(hidden_part[None], quarter_bits, row_index)[0]
    gate_grad_share = (
        hidden_grad * up_share * sigmoid_gate * (1.0 + gate_share * (1.0 - sigmoid_gate))
    ).astype(jnp.bfloat16)
    up_grad_share = (hidden_grad * silu_gate).astype(jnp.bfloat16)
    grad_pair = group_rows(jnp.stack([gate_grad_share, up_grad_share]), quarter_bits, row_index)
    gate_grad = grad_pair[0]
    up_grad = grad_pair[1]
    input_part = lax.dot_general(
        gate_grad, w_gate, contract_last, preferred_element_type=jnp.float32
    )
    input_part = input_part + lax.dot_general(
        up_grad, w_up, contract_last, preferred_element_type=jnp.float32
    )
    input_grad = halve_sums(input_part, quarter_bits, row_bits, 0, row_index).astype(jnp.bfloat16)
    group_dest = lax.dynamic_slice_in_dim(all_dest, group_index * QUARTERS, QUARTERS, axis=1)
    group_dest = group_dest.reshape(3, QUARTERS * capacity)
    targets = quarter_index * capacity + jnp.arange(capacity, dtype=jnp.int32)
    matches = group_dest[:, None, :] == targets[None, :, None]
    found_slot = jnp.any(matches, axis=2)
    source = jnp.argmax(matches, axis=2)
    contract_tokens = (((0,), (0,)), ((), ()))
    dense_gate = lax.dot_general(
        inputs, gate_grad, contract_tokens, preferred_element_type=jnp.float32
    ).astype(jnp.bfloat16)
    dense_up = lax.dot_general(
        inputs, up_grad, contract_tokens, preferred_element_type=jnp.float32
    ).astype(jnp.bfloat16)
    dense_down = lax.dot_general(
        hidden, upstream, contract_tokens, preferred_element_type=jnp.float32
    ).astype(jnp.bfloat16)
    safe_index = jnp.minimum(own_index, slot_count - 1)
    pieces = jnp.stack(
        [
            jnp.take(gate_pieces(dense_gate, hidden_count), safe_index[0], axis=0),
            jnp.take(gate_pieces(dense_up, hidden_count), safe_index[1], axis=0),
            jnp.take(down_pieces(dense_down, hidden_count), safe_index[2], axis=0),
        ]
    )
    group_pieces = collect_rows(pieces, 0, quarter_bits, 1, row_index)
    picked = jnp.take_along_axis(group_pieces, source[:, :, None, None], axis=1)
    owned_blocks = jnp.where(found_slot[:, :, None, None], picked, jnp.zeros_like(picked))
    weight_grads = owned_blocks.reshape(3, 1, 1, capacity, BLK, BLK)
    return (mixed_rows, input_grad, weight_grads)


def solution(mesh):
    return jax.shard_map(
        body,
        mesh=mesh,
        in_specs=(
            P("row", "col"),
            P("row", "col"),
            P("row", "col", None, None, None),
            P("row", "col", None, None, None),
            P("row", "col", None, None, None),
            P(),
            P(None, None, "col", None),
        ),
        out_specs=(P("row", "col"), P("row", "col"), P(None, "row", "col", None, None, None)),
        check_vma=False,
    )
```

profile of v0, /device:TPU:32, one launch (start us, length us, event | category | flops | bytes accessed | tf_op | source)
XLA Modules:
  0.0 840.0 jit_solution(12002372146149603347)
XLA Ops:
  82.2 13.1 %collective-permute-done.6 = f32[2,128,896]{2,1,0:T(8,128)} collective-permute-done((f32[2,128,896]{2,1,0:T(8,128)}, f32[2,128,896]{2,1,0:T(8,128)}, u32[]{:S(2)}, u32[]{:S(2)}) %collective-permute-start.6) | collective-permute-done | bytes 917536 | tf_op jit(solution)/shard_map/ppermute | solution.py:14
  99.6 13.2 %reduce-scatter.5.cloned.1.call-done = f32[1,32,896]{2,1,0:T(8,128)} async-done(((f32[1,64,896]{2,1,0:T(8,128)}), f32[1,32,896]{2,1,0:T(8,128)}) %reduce-scatter.5.cloned.1.call-update) | async-done | bytes 114704 | tf_op jit(solution)/shard_map/reduce_scatter | solution.py:52
  112.7 22.5 %reduce-scatter.3.cloned.1.call-done = f32[2,32,896]{2,1,0:T(8,128)} async-done(((f32[2,64,896]{2,1,0:T(8,128)}), f32[2,32,896]{2,1,0:T(8,128)}) %reduce-scatter.3.cloned.1.call-update) | async-done | bytes 229392 | tf_op jit(solution)/shard_map/reduce_scatter | solution.py:52
  202.8 12.3 %collective-permute-done.14 = f32[128,1024]{1,0:T(8,128)S(1)} collective-permute-done((f32[128,1024]{1,0:T(8,128)S(1)}, f32[128,1024]{1,0:T(8,128)S(1)}, u32[]{:S(2)}, u32[]{:S(2)}) %collective-permute-start.14) | collective-permute-done | bytes 524320 | tf_op jit(solution)/shard_map/ppermute | solution.py:14
  245.5 189.2 %collective-permute-done.17 = f32[16,1024]{1,0:T(8,128)S(1)} collective-permute-done((f32[16,1024]{1,0:T(8,128)S(1)}, f32[16,1024]{1,0:T(8,128)S(1)}, u32[]{:S(2)}, u32[]{:S(2)}) %collective-permute-start.17) | collective-permute-done | bytes 65568 | tf_op jit(solution)/shard_map/ppermute | solution.py:14
  436.3 351.5 %while.17 = (s32[]{:T(128)}, f32[8,1024]{1,0:T(8,128)S(1)}, s32[]{:T(128)}, f32[256,1024]{1,0:T(8,128)}, s32[]{:T(128)}, /*index=5*/s32[]{:T(128)}, s32[]{:T(128...) while((s32[]{:T(128)}, f32[8,1024]{1,0:T(8,128)S(1)}, s32[]{:T(128)}, ...), condition=%wide.region_5.6_spmd, body=%wide.region_4.5_spmd.sunk | while | flops 8212 | bytes 229728 | solution.py:140
  447.6 10.5 %collective-permute-done = f32[8,1024]{1,0:T(8,128)S(1)} collective-permute-done((f32[8,1024]{1,0:T(8,128)S(1)}, f32[8,1024]{1,0:T(8,128)S(1)}, u32[]{:S(2)}, u32[]{:S(2)}) %collective-permute-start) | collective-permute-done | bytes 32800 | tf_op jit(solution)/shard_map/while/body/eval_jaxpr/ppermute | solution.py:19
  458.9 10.5 %collective-permute-done = f32[8,1024]{1,0:T(8,128)S(1)} collective-permute-done((f32[8,1024]{1,0:T(8,128)S(1)}, f32[8,1024]{1,0:T(8,128)S(1)}, u32[]{:S(2)}, u32[]{:S(2)}) %collective-permute-start) | collective-permute-done | bytes 32800 | tf_op jit(solution)/shard_map/while/body/eval_jaxpr/ppermute | solution.py:19
  470.2 10.5 %collective-permute-done = f32[8,1024]{1,0:T(8,128)S(1)} collective-permute-done((f32[8,1024]{1,0:T(8,128)S(1)}, f32[8,1024]{1,0:T(8,128)S(1)}, u32[]{:S(2)}, u32[]{:S(2)}) %collective-permute-start) | collective-permute-done | bytes 32800 | tf_op jit(solution)/shard_map/while/body/eval_jaxpr/ppermute | solution.py:19
  481.5 10.5 %collective-permute-done = f32[8,1024]{1,0:T(8,128)S(1)} collective-permute-done((f32[8,1024]{1,0:T(8,128)S(1)}, f32[8,1024]{1,0:T(8,128)S(1)}, u32[]{:S(2)}, u32[]{:S(2)}) %collective-permute-start) | collective-permute-done | bytes 32800 | tf_op jit(solution)/shard_map/while/body/eval_jaxpr/ppermute | solution.py:19
  492.8 10.5 %collective-permute-done = f32[8,1024]{1,0:T(8,128)S(1)} collective-permute-done((f32[8,1024]{1,0:T(8,128)S(1)}, f32[8,1024]{1,0:T(8,128)S(1)}, u32[]{:S(2)}, u32[]{:S(2)}) %collective-permute-start) | collective-permute-done | bytes 32800 | tf_op jit(solution)/shard_map/while/body/eval_jaxpr/ppermute | solution.py:19
  504.1 10.6 %collective-permute-done = f32[8,1024]{1,0:T(8,128)S(1)} collective-permute-done((f32[8,1024]{1,0:T(8,128)S(1)}, f32[8,1024]{1,0:T(8,128)S(1)}, u32[]{:S(2)}, u32[]{:S(2)}) %collective-permute-start) | collective-permute-done | bytes 32800 | tf_op jit(solution)/shard_map/while/body/eval_jaxpr/ppermute | solution.py:19
  515.5 10.6 %collective-permute-done = f32[8,1024]{1,0:T(8,128)S(1)} collective-permute-done((f32[8,1024]{1,0:T(8,128)S(1)}, f32[8,1024]{1,0:T(8,128)S(1)}, u32[]{:S(2)}, u32[]{:S(2)}) %collective-permute-start) | collective-permute-done | bytes 32800 | tf_op jit(solution)/shard_map/while/body/eval_jaxpr/ppermute | solution.py:19
  526.8 10.5 %collective-permute-done = f32[8,1024]{1,0:T(8,128)S(1)} collective-permute-done((f32[8,1024]{1,0:T(8,128)S(1)}, f32[8,1024]{1,0:T(8,128)S(1)}, u32[]{:S(2)}, u32[]{:S(2)}) %collective-permute-start) | collective-permute-done | bytes 32800 | tf_op jit(solution)/shard_map/while/body/eval_jaxpr/ppermute | solution.py:19
  538.1 10.5 %collective-permute-done = f32[8,1024]{1,0:T(8,128)S(1)} collective-permute-done((f32[8,1024]{1,0:T(8,128)S(1)}, f32[8,1024]{1,0:T(8,128)S(1)}, u32[]{:S(2)}, u32[]{:S(2)}) %collective-permute-start) | collective-permute-done | bytes 32800 | tf_op jit(solution)/shard_map/while/body/eval_jaxpr/ppermute | solution.py:19
  549.4 10.7 %collective-permute-done = f32[8,1024]{1,0:T(8,128)S(1)} collective-permute-done((f32[8,1024]{1,0:T(8,128)S(1)}, f32[8,1024]{1,0:T(8,128)S(1)}, u32[]{:S(2)}, u32[]{:S(2)}) %collective-permute-start) | collective-permute-done | bytes 32800 | tf_op jit(solution)/shard_map/while/body/eval_jaxpr/ppermute | solution.py:19
  560.9 10.8 %collective-permute-done = f32[8,1024]{1,0:T(8,128)S(1)} collective-permute-done((f32[8,1024]{1,0:T(8,128)S(1)}, f32[8,1024]{1,0:T(8,128)S(1)}, u32[]{:S(2)}, u32[]{:S(2)}) %collective-permute-start) | collective-permute-done | bytes 32800 | tf_op jit(solution)/shard_map/while/body/eval_jaxpr/ppermute | solution.py:19
  572.5 10.6 %collective-permute-done = f32[8,1024]{1,0:T(8,128)S(1)} collective-permute-done((f32[8,1024]{1,0:T(8,128)S(1)}, f32[8,1024]{1,0:T(8,128)S(1)}, u32[]{:S(2)}, u32[]{:S(2)}) %collective-permute-start) | collective-permute-done | bytes 32800 | tf_op jit(solution)/shard_map/while/body/eval_jaxpr/ppermute | solution.py:19
  583.8 10.5 %collective-permute-done = f32[8,1024]{1,0:T(8,128)S(1)} collective-permute-done((f32[8,1024]{1,0:T(8,128)S(1)}, f32[8,1024]{1,0:T(8,128)S(1)}, u32[]{:S(2)}, u32[]{:S(2)}) %collective-permute-start) | collective-permute-done | bytes 32800 | tf_op jit(solution)/shard_map/while/body/eval_jaxpr/ppermute | solution.py:19
  595.1 10.5 %collective-permute-done = f32[8,1024]{1,0:T(8,128)S(1)} collective-permute-done((f32[8,1024]{1,0:T(8,128)S(1)}, f32[8,1024]{1,0:T(8,128)S(1)}, u32[]{:S(2)}, u32[]{:S(2)}) %collective-permute-start) | collective-permute-done | bytes 32800 | tf_op jit(solution)/shard_map/while/body/eval_jaxpr/ppermute | solution.py:19
  606.4 10.9 %collective-permute-done = f32[8,1024]{1,0:T(8,128)S(1)} collective-permute-done((f32[8,1024]{1,0:T(8,128)S(1)}, f32[8,1024]{1,0:T(8,128)S(1)}, u32[]{:S(2)}, u32[]{:S(2)}) %collective-permute-start) | collective-permute-done | bytes 32800 | tf_op jit(solution)/shard_map/while/body/eval_jaxpr/ppermute | solution.py:19
  618.1 10.5 %collective-permute-done = f32[8,1024]{1,0:T(8,128)S(1)} collective-permute-done((f32[8,1024]{1,0:T(8,128)S(1)}, f32[8,1024]{1,0:T(8,128)S(1)}, u32[]{:S(2)}, u32[]{:S(2)}) %collective-permute-start) | collective-permute-done | bytes 32800 | tf_op jit(solution)/shard_map/while/body/eval_jaxpr/ppermute | solution.py:19
  629.4 10.5 %collective-permute-done = f32[8,1024]{1,0:T(8,128)S(1)} collective-permute-done((f32[8,1024]{1,0:T(8,128)S(1)}, f32[8,1024]{1,0:T(8,128)S(1)}, u32[]{:S(2)}, u32[]{:S(2)}) %collective-permute-start) | collective-permute-done | bytes 32800 | tf_op jit(solution)/shard_map/while/body/eval_jaxpr/ppermute | solution.py:19
  640.7 10.5 %collective-permute-done = f32[8,1024]{1,0:T(8,128)S(1)} collective-permute-done((f32[8,1024]{1,0:T(8,128)S(1)}, f32[8,1024]{1,0:T(8,128)S(1)}, u32[]{:S(2)}, u32[]{:S(2)}) %collective-permute-start) | collective-permute-done | bytes 32800 | tf_op jit(solution)/shard_map/while/body/eval_jaxpr/ppermute | solution.py:19
  674.6 10.6 %collective-permute-done = f32[8,1024]{1,0:T(8,128)S(1)} collective-permute-done((f32[8,1024]{1,0:T(8,128)S(1)}, f32[8,1024]{1,0:T(8,128)S(1)}, u32[]{:S(2)}, u32[]{:S(2)}) %collective-permute-start) | collective-permute-done | bytes 32800 | tf_op jit(solution)/shard_map/while/body/eval_jaxpr/ppermute | solution.py:19
  686.0 10.5 %collective-permute-done = f32[8,1024]{1,0:T(8,128)S(1)} collective-permute-done((f32[8,1024]{1,0:T(8,128)S(1)}, f32[8,1024]{1,0:T(8,128)S(1)}, u32[]{:S(2)}, u32[]{:S(2)}) %collective-permute-start) | collective-permute-done | bytes 32800 | tf_op jit(solution)/shard_map/while/body/eval_jaxpr/ppermute | solution.py:19
  697.3 10.6 %collective-permute-done = f32[8,1024]{1,0:T(8,128)S(1)} collective-permute-done((f32[8,1024]{1,0:T(8,128)S(1)}, f32[8,1024]{1,0:T(8,128)S(1)}, u32[]{:S(2)}, u32[]{:S(2)}) %collective-permute-start) | collective-permute-done | bytes 32800 | tf_op jit(solution)/shard_map/while/body/eval_jaxpr/ppermute | solution.py:19
  708.6 10.6 %collective-permute-done = f32[8,1024]{1,0:T(8,128)S(1)} collective-permute-done((f32[8,1024]{1,0:T(8,128)S(1)}, f32[8,1024]{1,0:T(8,128)S(1)}, u32[]{:S(2)}, u32[]{:S(2)}) %collective-permute-start) | collective-permute-done | bytes 32800 | tf_op jit(solution)/shard_map/while/body/eval_jaxpr/ppermute | solution.py:19
  720.0 10.5 %collective-permute-done = f32[8,1024]{1,0:T(8,128)S(1)} collective-permute-done((f32[8,1024]{1,0:T(8,128)S(1)}, f32[8,1024]{1,0:T(8,128)S(1)}, u32[]{:S(2)}, u32[]{:S(2)}) %collective-permute-start) | collective-permute-done | bytes 32800 | tf_op jit(solution)/shard_map/while/body/eval_jaxpr/ppermute | solution.py:19
  753.9 10.5 %collective-permute-done = f32[8,1024]{1,0:T(8,128)S(1)} collective-permute-done((f32[8,1024]{1,0:T(8,128)S(1)}, f32[8,1024]{1,0:T(8,128)S(1)}, u32[]{:S(2)}, u32[]{:S(2)}) %collective-permute-start) | collective-permute-done | bytes 32800 | tf_op jit(solution)/shard_map/while/body/eval_jaxpr/ppermute | solution.py:19
  789.1 21.3 %maximum_select_fusion = bf16[3,192,128,128]{3,2,1,0:T(8,128)(2,1)} fusion(bf16[3,96,128,128]{3,2,1,0:T(8,128)(2,1)} %maximum_select_fusion.1, bf16[3,96,128,128]{3,2,1,0:T(8,128)(2,1)} %collective-permute-done.20, pred[]{:T(512)S(6)} %eq.81), kind=kLoop, calls=%fused_computation.8 | loop fusion | flops 28311552 | bytes 37748736 | tf_op jit(solution)/shard_map/jit(_where)/select_n | solution.py:30
  810.4 18.4 %gather_fusion = bf16[144,128,128]{2,1,0:T(8,128)(2,1)} fusion(bf16[3,192,128,128]{3,2,1,0:T(8,128)(2,1)} %maximum_select_fusion, s32[144]{0:T(256)S(1)} %reshape.314), kind=kCustom, calls=%fused_computation.3 | custom fusion | bytes 9438336 | tf_op jit(solution)/shard_map/jit(take_along_axis)/gather | solution.py:185
  (244 shorter events, 281.3 us)
Async XLA Ops:
  7.2 105.5 %reduce-scatter.5.cloned.1.call-start = ((), (), s32[]{:S(2)}) async-start(), calls=%async_computation.3 | async-start | bytes 344064 | tf_op jit(solution)/shard_map/reduce_scatter | solution.py:52
  36.5 28.2 %collective-permute-start.5 = (bf16[2,128,1024]{2,1,0:T(8,128)(2,1)S(1)}, bf16[2,128,1024]{2,1,0:T(8,128)(2,1)S(1)}, u32[]{:S(2)}, u32[]{:S(2)}) collective-permute-start(bf16[2,128,1024]{2,1,0:T(8,128)(2,1)S(1)} %maximum_select_fusion.4), channel_id=1, source_target_pairs={{0,128},{2,130},{4,132},{6,134},{8,136},{10,138},{12,140},{14,142}... | collective-permute-start | bytes 1572872 | tf_op jit(solution)/shard_map/ppermute | solution.py:14
  67.1 13.6 %collective-permute-start.10 = (f32[1,128,896]{2,1,0:T(8,128)S(1)}, f32[1,128,896]{2,1,0:T(8,128)}, u32[]{:S(2)}, u32[]{:S(2)}) collective-permute-start(f32[1,128,896]{2,1,0:T(8,128)S(1)} %slice_select_fusion.1), channel_id=1, source_target_pairs={{0,4},{2,6},{4,0},{6,2},{8,12},{10,14},{12,8},{14,10},{16,20},{18,... | collective-permute-start | bytes 1376264 | tf_op jit(solution)/shard_map/ppermute | solution.py:14
  72.0 23.3 %collective-permute-start.6 = (f32[2,128,896]{2,1,0:T(8,128)}, f32[2,128,896]{2,1,0:T(8,128)}, u32[]{:S(2)}, u32[]{:S(2)}) collective-permute-start(f32[2,128,896]{2,1,0:T(8,128)} %broadcast_select_fusion), channel_id=1, source_target_pairs={{0,4},{2,6},{4,0},{6,2},{8,12},{10,14},{12,8},{14,10},{16,20},{18,... | collective-permute-start | bytes 2752520 | tf_op jit(solution)/shard_map/ppermute | solution.py:14
  81.9 14.9 %collective-permute-start.11 = (f32[1,64,896]{2,1,0:T(8,128)S(1)}, f32[1,64,896]{2,1,0:T(8,128)S(1)}, u32[]{:S(2)}, u32[]{:S(2)}) collective-permute-start(f32[1,64,896]{2,1,0:T(8,128)S(1)} %slice_select_fusion.4), channel_id=1, source_target_pairs={{0,2},{2,0},{4,6},{6,4},{8,10},{10,8},{12,14},{14,12},{16,18},{18,... | collective-permute-start | bytes 688136 | tf_op jit(solution)/shard_map/ppermute | solution.py:14
  97.6 37.6 %reduce-scatter.3.cloned.1.call-start = ((), (), s32[]{:S(2)}) async-start(), calls=%async_computation.2 | async-start | bytes 688128 | tf_op jit(solution)/shard_map/reduce_scatter | solution.py:52
  149.8 15.7 %collective-permute-start.13 = (bf16[2,128,896]{2,1,0:T(8,128)(2,1)}, bf16[2,128,896]{2,1,0:T(8,128)(2,1)}, u32[]{:S(2)}, u32[]{:S(2)}) collective-permute-start(bf16[2,128,896]{2,1,0:T(8,128)(2,1)} %maximum_select_fusion.6), channel_id=1, source_target_pairs={{0,4},{2,6},{4,0},{6,2},{8,12},{10,14},{12,8},{14,10},{16,20},{18,... | collective-permute-start | bytes 1376264 | tf_op jit(solution)/shard_map/ppermute | solution.py:14
  195.6 19.7 %collective-permute-start.19 = (bf16[3,48,128,128]{3,2,1,0:T(8,128)(2,1)}, bf16[3,48,128,128]{3,2,1,0:T(8,128)(2,1)}, u32[]{:S(2)}, u32[]{:S(2)}) collective-permute-start(bf16[3,48,128,128]{3,2,1,0:T(8,128)(2,1)} %pad_maximum_fusion), channel_id=1, source_target_pairs={{0,2},{2,0},{4,6},{6,4},{8,10},{10,8},{12,14},{14,12},{16,18},{18,... | collective-permute-start | bytes 14155784 | tf_op jit(solution)/shard_map/ppermute | solution.py:14
  199.2 15.9 %collective-permute-start.14 = (f32[128,1024]{1,0:T(8,128)S(1)}, f32[128,1024]{1,0:T(8,128)S(1)}, u32[]{:S(2)}, u32[]{:S(2)}) collective-permute-start(f32[128,1024]{1,0:T(8,128)S(1)} %slice_select_fusion), channel_id=1, source_target_pairs={{0,128},{2,130},{4,132},{6,134},{8,136},{10,138},{12,140},{14,142}... | collective-permute-start | bytes 1572872 | tf_op jit(solution)/shard_map/ppermute | solution.py:14
  223.7 565.4 %collective-permute-start.20 = (bf16[3,96,128,128]{3,2,1,0:T(8,128)(2,1)}, bf16[3,96,128,128]{3,2,1,0:T(8,128)(2,1)}, u32[]{:S(2)}, u32[]{:S(2)}) collective-permute-start(bf16[3,96,128,128]{3,2,1,0:T(8,128)(2,1)} %maximum_select_fusion.1), channel_id=1, source_target_pairs={{0,4},{2,6},{4,0},{6,2},{8,12},{10,14},{12,8},{14,10},{16,20},{18,... | collective-permute-start | bytes 28311560 | tf_op jit(solution)/shard_map/ppermute | solution.py:14
  239.7 195.1 %collective-permute-start.17 = (f32[16,1024]{1,0:T(8,128)S(1)}, f32[16,1024]{1,0:T(8,128)S(1)}, u32[]{:S(2)}, u32[]{:S(2)}) collective-permute-start(f32[16,1024]{1,0:T(8,128)S(1)} %slice_select_fusion.6), channel_id=1, source_target_pairs={{0,16},{2,18},{4,20},{6,22},{8,24},{10,26},{12,28},{14,30},{16,0},... | collective-permute-start | bytes 196616 | tf_op jit(solution)/shard_map/ppermute | solution.py:14
  434.8 353.7 %collective-permute-start.18 = (f32[8,1024]{1,0:T(8,128)S(1)}, f32[8,1024]{1,0:T(8,128)S(1)}, u32[]{:S(2)}, u32[]{:S(2)}) collective-permute-start(f32[8,1024]{1,0:T(8,128)S(1)} %slice_select_fusion.7), channel_id=1, source_target_pairs={{0,8},{2,10},{4,12},{6,14},{8,0},{10,2},{12,4},{14,6},{16,24},{18,... | collective-permute-start | bytes 98312 | tf_op jit(solution)/shard_map/ppermute | solution.py:14
  436.3 10.5 %collective-permute-start = (f32[8,1024]{1,0:T(8,128)S(1)}, f32[8,1024]{1,0:T(8,128)S(1)}, u32[]{:S(2)}, u32[]{:S(2)}) collective-permute-start(f32[8,1024]{1,0:T(8,128)S(1)} %get-tuple-element.210), channel_id=1, source_target_pairs={{0,8},{2,10},{4,12},{6,14},{8,16},{10,18},{12,20},{14,22},{16,24},... | collective-permute-start | bytes 98312 | tf_op jit(solution)/shard_map/while/body/eval_jaxpr/ppermute | solution.py:19
  447.6 10.5 %collective-permute-start = (f32[8,1024]{1,0:T(8,128)S(1)}, f32[8,1024]{1,0:T(8,128)S(1)}, u32[]{:S(2)}, u32[]{:S(2)}) collective-permute-start(f32[8,1024]{1,0:T(8,128)S(1)} %get-tuple-element.210), channel_id=1, source_target_pairs={{0,8},{2,10},{4,12},{6,14},{8,16},{10,18},{12,20},{14,22},{16,24},... | collective-permute-start | bytes 98312 | tf_op jit(solution)/shard_map/while/body/eval_jaxpr/ppermute | solution.py:19
  458.9 10.5 %collective-permute-start = (f32[8,1024]{1,0:T(8,128)S(1)}, f32[8,1024]{1,0:T(8,128)S(1)}, u32[]{:S(2)}, u32[]{:S(2)}) collective-permute-start(f32[8,1024]{1,0:T(8,128)S(1)} %get-tuple-element.210), channel_id=1, source_target_pairs={{0,8},{2,10},{4,12},{6,14},{8,16},{10,18},{12,20},{14,22},{16,24},... | collective-permute-start | bytes 98312 | tf_op jit(solution)/shard_map/while/body/eval_jaxpr/ppermute | solution.py:19
  470.2 10.5 %collective-permute-start = (f32[8,1024]{1,0:T(8,128)S(1)}, f32[8,1024]{1,0:T(8,128)S(1)}, u32[]{:S(2)}, u32[]{:S(2)}) collective-permute-start(f32[8,1024]{1,0:T(8,128)S(1)} %get-tuple-element.210), channel_id=1, source_target_pairs={{0,8},{2,10},{4,12},{6,14},{8,16},{10,18},{12,20},{14,22},{16,24},... | collective-permute-start | bytes 98312 | tf_op jit(solution)/shard_map/while/body/eval_jaxpr/ppermute | solution.py:19
  481.5 10.5 %collective-permute-start = (f32[8,1024]{1,0:T(8,128)S(1)}, f32[8,1024]{1,0:T(8,128)S(1)}, u32[]{:S(2)}, u32[]{:S(2)}) collective-permute-start(f32[8,1024]{1,0:T(8,128)S(1)} %get-tuple-element.210), channel_id=1, source_target_pairs={{0,8},{2,10},{4,12},{6,14},{8,16},{10,18},{12,20},{14,22},{16,24},... | collective-permute-start | bytes 98312 | tf_op jit(solution)/shard_map/while/body/eval_jaxpr/ppermute | solution.py:19
  492.8 10.5 %collective-permute-start = (f32[8,1024]{1,0:T(8,128)S(1)}, f32[8,1024]{1,0:T(8,128)S(1)}, u32[]{:S(2)}, u32[]{:S(2)}) collective-permute-start(f32[8,1024]{1,0:T(8,128)S(1)} %get-tuple-element.210), channel_id=1, source_target_pairs={{0,8},{2,10},{4,12},{6,14},{8,16},{10,18},{12,20},{14,22},{16,24},... | collective-permute-start | bytes 98312 | tf_op jit(solution)/shard_map/while/body/eval_jaxpr/ppermute | solution.py:19
  504.1 10.6 %collective-permute-start = (f32[8,1024]{1,0:T(8,128)S(1)}, f32[8,1024]{1,0:T(8,128)S(1)}, u32[]{:S(2)}, u32[]{:S(2)}) collective-permute-start(f32[8,1024]{1,0:T(8,128)S(1)} %get-tuple-element.210), channel_id=1, source_target_pairs={{0,8},{2,10},{4,12},{6,14},{8,16},{10,18},{12,20},{14,22},{16,24},... | collective-permute-start | bytes 98312 | tf_op jit(solution)/shard_map/while/body/eval_jaxpr/ppermute | solution.py:19
  515.4 10.6 %collective-permute-start = (f32[8,1024]{1,0:T(8,128)S(1)}, f32[8,1024]{1,0:T(8,128)S(1)}, u32[]{:S(2)}, u32[]{:S(2)}) collective-permute-start(f32[8,1024]{1,0:T(8,128)S(1)} %get-tuple-element.210), channel_id=1, source_target_pairs={{0,8},{2,10},{4,12},{6,14},{8,16},{10,18},{12,20},{14,22},{16,24},... | collective-permute-start | bytes 98312 | tf_op jit(solution)/shard_map/while/body/eval_jaxpr/ppermute | solution.py:19
  526.8 10.5 %collective-permute-start = (f32[8,1024]{1,0:T(8,128)S(1)}, f32[8,1024]{1,0:T(8,128)S(1)}, u32[]{:S(2)}, u32[]{:S(2)}) collective-permute-start(f32[8,1024]{1,0:T(8,128)S(1)} %get-tuple-element.210), channel_id=1, source_target_pairs={{0,8},{2,10},{4,12},{6,14},{8,16},{10,18},{12,20},{14,22},{16,24},... | collective-permute-start | bytes 98312 | tf_op jit(solution)/shard_map/while/body/eval_jaxpr/ppermute | solution.py:19
  538.1 10.5 %collective-permute-start = (f32[8,1024]{1,0:T(8,128)S(1)}, f32[8,1024]{1,0:T(8,128)S(1)}, u32[]{:S(2)}, u32[]{:S(2)}) collective-permute-start(f32[8,1024]{1,0:T(8,128)S(1)} %get-tuple-element.210), channel_id=1, source_target_pairs={{0,8},{2,10},{4,12},{6,14},{8,16},{10,18},{12,20},{14,22},{16,24},... | collective-permute-start | bytes 98312 | tf_op jit(solution)/shard_map/while/body/eval_jaxpr/ppermute | solution.py:19
  549.4 10.7 %collective-permute-start = (f32[8,1024]{1,0:T(8,128)S(1)}, f32[8,1024]{1,0:T(8,128)S(1)}, u32[]{:S(2)}, u32[]{:S(2)}) collective-permute-start(f32[8,1024]{1,0:T(8,128)S(1)} %get-tuple-element.210), channel_id=1, source_target_pairs={{0,8},{2,10},{4,12},{6,14},{8,16},{10,18},{12,20},{14,22},{16,24},... | collective-permute-start | bytes 98312 | tf_op jit(solution)/shard_map/while/body/eval_jaxpr/ppermute | solution.py:19
  560.9 10.8 %collective-permute-start = (f32[8,1024]{1,0:T(8,128)S(1)}, f32[8,1024]{1,0:T(8,128)S(1)}, u32[]{:S(2)}, u32[]{:S(2)}) collective-permute-start(f32[8,1024]{1,0:T(8,128)S(1)} %get-tuple-element.210), channel_id=1, source_target_pairs={{0,8},{2,10},{4,12},{6,14},{8,16},{10,18},{12,20},{14,22},{16,24},... | collective-permute-start | bytes 98312 | tf_op jit(solution)/shard_map/while/body/eval_jaxpr/ppermute | solution.py:19
  572.5 10.6 %collective-permute-start = (f32[8,1024]{1,0:T(8,128)S(1)}, f32[8,1024]{1,0:T(8,128)S(1)}, u32[]{:S(2)}, u32[]{:S(2)}) collective-permute-start(f32[8,1024]{1,0:T(8,128)S(1)} %get-tuple-element.210), channel_id=1, source_target_pairs={{0,8},{2,10},{4,12},{6,14},{8,16},{10,18},{12,20},{14,22},{16,24},... | collective-permute-start | bytes 98312 | tf_op jit(solution)/shard_map/while/body/eval_jaxpr/ppermute | solution.py:19
  583.8 10.5 %collective-permute-start = (f32[8,1024]{1,0:T(8,128)S(1)}, f32[8,1024]{1,0:T(8,128)S(1)}, u32[]{:S(2)}, u32[]{:S(2)}) collective-permute-start(f32[8,1024]{1,0:T(8,128)S(1)} %get-tuple-element.210), channel_id=1, source_target_pairs={{0,8},{2,10},{4,12},{6,14},{8,16},{10,18},{12,20},{14,22},{16,24},... | collective-permute-start | bytes 98312 | tf_op jit(solution)/shard_map/while/body/eval_jaxpr/ppermute | solution.py:19
  595.1 10.5 %collective-permute-start = (f32[8,1024]{1,0:T(8,128)S(1)}, f32[8,1024]{1,0:T(8,128)S(1)}, u32[]{:S(2)}, u32[]{:S(2)}) collective-permute-start(f32[8,1024]{1,0:T(8,128)S(1)} %get-tuple-element.210), channel_id=1, source_target_pairs={{0,8},{2,10},{4,12},{6,14},{8,16},{10,18},{12,20},{14,22},{16,24},... | collective-permute-start | bytes 98312 | tf_op jit(solution)/shard_map/while/body/eval_jaxpr/ppermute | solution.py:19
  606.4 10.9 %collective-permute-start = (f32[8,1024]{1,0:T(8,128)S(1)}, f32[8,1024]{1,0:T(8,128)S(1)}, u32[]{:S(2)}, u32[]{:S(2)}) collective-permute-start(f32[8,1024]{1,0:T(8,128)S(1)} %get-tuple-element.210), channel_id=1, source_target_pairs={{0,8},{2,10},{4,12},{6,14},{8,16},{10,18},{12,20},{14,22},{16,24},... | collective-permute-start | bytes 98312 | tf_op jit(solution)/shard_map/while/body/eval_jaxpr/ppermute | solution.py:19
  618.1 10.5 %collective-permute-start = (f32[8,1024]{1,0:T(8,128)S(1)}, f32[8,1024]{1,0:T(8,128)S(1)}, u32[]{:S(2)}, u32[]{:S(2)}) collective-permute-start(f32[8,1024]{1,0:T(8,128)S(1)} %get-tuple-element.210), channel_id=1, source_target_pairs={{0,8},{2,10},{4,12},{6,14},{8,16},{10,18},{12,20},{14,22},{16,24},... | collective-permute-start | bytes 98312 | tf_op jit(solution)/shard_map/while/body/eval_jaxpr/ppermute | solution.py:19
  674.6 10.6 %collective-permute-start = (f32[8,1024]{1,0:T(8,128)S(1)}, f32[8,1024]{1,0:T(8,128)S(1)}, u32[]{:S(2)}, u32[]{:S(2)}) collective-permute-start(f32[8,1024]{1,0:T(8,128)S(1)} %get-tuple-element.210), channel_id=1, source_target_pairs={{0,8},{2,10},{4,12},{6,14},{8,16},{10,18},{12,20},{14,22},{16,24},... | collective-permute-start | bytes 98312 | tf_op jit(solution)/shard_map/while/body/eval_jaxpr/ppermute | solution.py:19
  697.3 10.6 %collective-permute-start = (f32[8,1024]{1,0:T(8,128)S(1)}, f32[8,1024]{1,0:T(8,128)S(1)}, u32[]{:S(2)}, u32[]{:S(2)}) collective-permute-start(f32[8,1024]{1,0:T(8,128)S(1)} %get-tuple-element.210), channel_id=1, source_target_pairs={{0,8},{2,10},{4,12},{6,14},{8,16},{10,18},{12,20},{14,22},{16,24},... | collective-permute-start | bytes 98312 | tf_op jit(solution)/shard_map/while/body/eval_jaxpr/ppermute | solution.py:19
  708.6 10.6 %collective-permute-start = (f32[8,1024]{1,0:T(8,128)S(1)}, f32[8,1024]{1,0:T(8,128)S(1)}, u32[]{:S(2)}, u32[]{:S(2)}) collective-permute-start(f32[8,1024]{1,0:T(8,128)S(1)} %get-tuple-element.210), channel_id=1, source_target_pairs={{0,8},{2,10},{4,12},{6,14},{8,16},{10,18},{12,20},{14,22},{16,24},... | collective-permute-start | bytes 98312 | tf_op jit(solution)/shard_map/while/body/eval_jaxpr/ppermute | solution.py:19
  (44 other events, 820.4 us)
Sparse Core Ops, SparseCore 0:
  97.7 14.9 reduce-scatter.4
  115.2 19.8 reduce-scatter.2
where the time goes:
time: 843 us; the launch traced here: 840 us
  waiting for transfers between devices  618 us (73%)
  other arithmetic  79.6 us (9%)
  local copies, waits for them, and re-layouts  68.8 us (8%)
  starting transfers between devices  38.2 us (5%)
  between operations  14.6 us (2%)
  blocking collectives  11.1 us (1%)
  matrix products  9.59 us (1%)
    ppermute x31, waiting for transfers between devices, shifted(): lax.ppermute(value, axis, [(i, (i + by) % devices) for i in range(devices)])  326 us
    ppermute x20, waiting for transfers between devices, from_partner(): return lax.ppermute(value, axis, pairs)  256 us
    ppermute x20, starting transfers between devices, from_partner(): return lax.ppermute(value, axis, pairs)  36.6 us
    reduce_scatter x2, waiting for transfers between devices, group_sums(): return lax.psum_scatter(values, 'col', scatter_dimension=1, tiled=True)  35.6 us
    select_n x11, other arithmetic, collect_rows(): jnp.where(high_side, jnp.concatenate([partner, values], axis_dim), jnp.co...  33.8 us
    add x31, other arithmetic, cycle_turn(): return moved_sum + cycle_piece(turn_index + 1)  23.6 us
    gather x2, local copies, waits for them, and re-layouts, body(): picked = jnp.take_along_axis(group_pieces, source[:, :, None, None], axis=1)  18.5 us
  transfers between devices with their start and end apart: 53, of which 47 were waited for; matrix products, arithmetic and copies ran while one was open for 8% of the time, Pallas kernels for 0%

commit v1 on v0

v1 whole, which is shorter than its diff:
```python
import functools

import jax
import jax.numpy as jnp
from jax import lax
from jax.experimental import pallas as pl
from jax.experimental.pallas import tpu as pltpu
from jax.sharding import PartitionSpec as P

BLK = 128
QUARTERS = 4
FB = 7
DB = 8
SLOTS = 56
CAP = 48
DQ = 1024
HB = 896
TG = 8
GROUPS = 32
TOKENS = 256
BF = jnp.bfloat16
F32 = jnp.float32
NT = (((1,), (1,)), ((), ()))
VMEM = pl.BlockSpec(memory_space=pltpu.VMEM)
SMEM = pl.BlockSpec(memory_space=pltpu.SMEM)
ANY = pl.BlockSpec(memory_space=pl.ANY)


def row_swap(value, mask):
    return lax.ppermute(value, "row", [(i, i ^ mask) for i in range(128)])


def square_swap(value, step):
    mask = (step >> 1) * 4 | (step & 1)
    return lax.ppermute(value, ("row", "col"), [(i, i ^ mask) for i in range(256)])


def deep_mask(step):
    return (step & 3) << 2 | (step >> 2) << 6


def x_mask(step):
    return step << 4


def sds(shape, dtype):
    return jax.ShapeDtypeStruct(shape, dtype)


def call(kernel, out_shape, in_specs, out_specs=None, scratch=(), limit=40, cost=None):
    many = isinstance(out_shape, (tuple, list))
    if out_specs is None:
        out_specs = [VMEM] * len(out_shape) if many else VMEM
    return pl.pallas_call(
        kernel,
        out_shape=out_shape,
        in_specs=in_specs,
        out_specs=out_specs,
        scratch_shapes=list(scratch),
        compiler_params=pltpu.CompilerParams(vmem_limit_bytes=limit * 2**20),
        cost_estimate=cost,
    )


def dense_kernel(index_ref, gate_ref, up_ref, down_ref, wg_ref, wu_ref, wd_ref, sems):
    wg_ref[...] = jnp.zeros_like(wg_ref)
    wu_ref[...] = jnp.zeros_like(wu_ref)
    wd_ref[...] = jnp.zeros_like(wd_ref)

    def each(act):
        def one(slot, carry):
            for m, (blocks, dense) in enumerate(
                ((gate_ref, wg_ref), (up_ref, wu_ref), (down_ref, wd_ref))
            ):
                place = index_ref[m, slot]

                @pl.when(place < SLOTS)
                def _():
                    hid = pl.multiple_of(place // DB * BLK, BLK)
                    feat = pl.multiple_of(place % DB * BLK, BLK)
                    first, second = (hid, feat) if m == 2 else (feat, hid)
                    act(
                        pltpu.make_async_copy(
                            blocks.at[slot],
                            dense.at[pl.ds(first, BLK), pl.ds(second, BLK)],
                            sems.at[m, slot],
                        )
                    )

            return carry

        lax.fori_loop(0, CAP, one, 0)

    each(lambda copy: copy.start())
    each(lambda copy: copy.wait())


def partial_kernel(place_ref, p0, p1, p2, p3, wg_ref, wu_ref, wd_ref, keep_ref, send_ref, rows):
    core = place_ref[0]
    first = pl.multiple_of(core * 128, 128)
    second = pl.multiple_of((1 - core) * 128, 128)
    rows[pl.ds(first, 64), :] = p0[...]
    rows[pl.ds(first + 64, 64), :] = p1[...]
    rows[pl.ds(second, 64), :] = p2[...]
    rows[pl.ds(second + 64, 64), :] = p3[...]
    x = rows[:, :DQ]
    dy = rows[:, DQ:]
    for at, value in (
        (0, lambda: jnp.dot(x, wg_ref[...], preferred_element_type=F32)),
        (1, lambda: jnp.dot(x, wu_ref[...], preferred_element_type=F32)),
        (2, lambda: lax.dot_general(dy, wd_ref[...], NT, preferred_element_type=F32)),
    ):
        part = value()
        keep_ref[:, at * HB : (at + 1) * HB] = part[:128]
        send_ref[:, at * HB : (at + 1) * HB] = part[128:]


def pair_kernel(place_ref, keep_ref, got_ref, o0, o1, o2, o3):
    me = place_ref[1]
    for step, out in enumerate((o0, o1, o2, o3)):
        at = pl.ds(pl.multiple_of((me ^ step) * 32, 32), 32)
        out[...] = keep_ref[at, :] + got_ref[at, :]


def act_kernel(a0, a1, a2, a3, out_ref):
    def total(at):
        part = slice(at * HB, (at + 1) * HB)
        return (a0[:, part] + a1[:, part]) + (a2[:, part] + a3[:, part])

    gate, up, dh = total(0), total(1), total(2)
    sig = jax.nn.sigmoid(gate)
    silu = gate * sig
    out_ref[:, :HB] = (silu * up).astype(BF)
    out_ref[:, HB : 2 * HB] = (dh * up * sig * (1.0 + gate * (1.0 - sig))).astype(BF)
    out_ref[:, 2 * HB :] = (dh * silu).astype(BF)


def spread(place_ref, mine, theirs, rows):
    core, me = place_ref[0], place_ref[1]
    for step in range(4):
        at = pl.multiple_of(core * 128 + (me ^ step) * 32, 32)
        rows[pl.ds(at, 32), :] = mine[step * 32 : (step + 1) * 32, :]
        at = pl.multiple_of((1 - core) * 128 + (me ^ step) * 32, 32)
        rows[pl.ds(at, 32), :] = theirs[step * 32 : (step + 1) * 32, :]


def out_kernel(place_ref, mine, theirs, wg_ref, wu_ref, wd_ref, t0, t1, t2, t3, full_ref):
    spread(place_ref, mine, theirs, full_ref)
    mixed = jnp.dot(full_ref[:, :HB], wd_ref[...], preferred_element_type=F32)
    for step, out in enumerate((t0, t1, t2, t3)):
        out[:, :DQ] = mixed[step * 64 : (step + 1) * 64].astype(out.dtype)
    grad = lax.dot_general(full_ref[:, HB : 2 * HB], wg_ref[...], NT, preferred_element_type=F32)
    grad += lax.dot_general(full_ref[:, 2 * HB :], wu_ref[...], NT, preferred_element_type=F32)
    for step, out in enumerate((t0, t1, t2, t3)):
        out[:, DQ:] = grad[step * 64 : (step + 1) * 64].astype(out.dtype)


def prep_kernel(p0, p1, p2, p3, xt_ref, dy_ref, rows):
    for step, piece in enumerate((p0, p1, p2, p3)):
        rows[step * 64 : (step + 1) * 64, :] = piece[...]
    for b in range(DB):
        xt_ref[b] = rows[:, b * BLK : (b + 1) * BLK].T
        dy_ref[b] = rows[:, DQ + b * BLK : DQ + (b + 1) * BLK]


def grad_kernel(code_ref, full_ref, x0, x1, x2, x3, y0, y1, y2, y3, out_ref, xt, dy, ht, dg, du):
    for j, (x, y) in enumerate(((x0, y0), (x1, y1), (x2, y2), (x3, y3))):
        xt[j * DB : (j + 1) * DB] = x[...]
        dy[j * DB : (j + 1) * DB] = y[...]
    for a in range(FB):
        ht[a] = full_ref[:, a * BLK : (a + 1) * BLK].T
        dg[a] = full_ref[:, HB + a * BLK : HB + (a + 1) * BLK]
        du[a] = full_ref[:, 2 * HB + a * BLK : 2 * HB + (a + 1) * BLK]

    def one(slot, carry):
        for m in range(3):
            code = code_ref[m, slot]

            @pl.when(code > 0)
            def _():
                where = code - 1
                feat = where // 64 * DB + where % 8
                hid = where % 64 // 8
                left, right = ((xt.at[feat], dg.at[hid]), (xt.at[feat], du.at[hid]), (ht.at[hid], dy.at[feat]))[m]
                out_ref[m, slot] = jnp.dot(left[...], right[...], preferred_element_type=F32).astype(BF)

            @pl.when(code == 0)
            def _():
                out_ref[m, slot] = jnp.zeros((BLK, BLK), BF)

        return carry

    lax.fori_loop(0, CAP, one, 0)


def body(activations, out_grad, gate_blocks, up_blocks, down_blocks, block_index, block_dest):
    row = lax.axis_index("row")
    col = lax.axis_index("col")
    group = row // QUARTERS
    quarter = row % QUARTERS
    place = jnp.stack([row % 2, row // 2 % 2 * 2 + col]).astype(jnp.int32)
    all_index = lax.dynamic_index_in_dim(block_index, col, axis=2, keepdims=False)
    own_index = lax.dynamic_index_in_dim(all_index, row, axis=1, keepdims=False)

    shard = jnp.concatenate([activations, out_grad], axis=1)
    near = jnp.concatenate([shard] + [row_swap(shard, deep_mask(i)) for i in range(1, 8)], axis=0)
    pieces = [near] + [row_swap(near, x_mask(i)) for i in range(1, 4)]
    wide = [sds((DQ, HB), BF), sds((DQ, HB), BF), sds((HB, DQ), BF)]
    wg, wu, wd = call(
        dense_kernel, wide, [SMEM, ANY, ANY, ANY], scratch=[pltpu.SemaphoreType.DMA((3, CAP))], limit=24
    )(
        own_index,
        gate_blocks.reshape(CAP, BLK, BLK),
        up_blocks.reshape(CAP, BLK, BLK),
        down_blocks.reshape(CAP, BLK, BLK),
    )

    half = sds((128, 3 * HB), F32)
    keep, send = call(
        partial_kernel, [half, half], [SMEM] + [VMEM] * 7, scratch=[pltpu.VMEM((TOKENS, 2 * DQ), BF)]
    )(place, *pieces, wg, wu, wd)
    got = row_swap(send, 1)
    fours = call(pair_kernel, [sds((32, 3 * HB), F32)] * 4, [SMEM, VMEM, VMEM])(place, keep, got)
    sums = [fours[0]] + [square_swap(fours[i], i) for i in range(1, 4)]
    share = call(act_kernel, sds((32, 3 * HB), BF), [VMEM] * 4)(*sums)
    mine = jnp.concatenate([share] + [square_swap(share, i) for i in range(1, 4)], axis=0)
    theirs = row_swap(mine, 1)
    outs = call(
        out_kernel,
        [sds((64, 2 * DQ), F32)] + [sds((64, 2 * DQ), BF)] * 3 + [sds((TOKENS, 3 * HB), BF)],
        [SMEM] + [VMEM] * 5,
    )(place, mine, theirs, wg, wu, wd)
    full = outs[4]
    far = outs[0]
    for i in range(1, 4):
        far = far + row_swap(outs[i], x_mask(i)).astype(F32)
    last = far[:TG]
    for i in range(1, 8):
        last = last + row_swap(far[i * TG : (i + 1) * TG].astype(BF), deep_mask(i)).astype(F32)
    last = last.astype(BF)

    mirror = row_swap(near, 2)
    mirrors = [mirror] + [row_swap(mirror, x_mask(i)) for i in range(1, 4)]
    prepped = [sds((DB, BLK, TOKENS), BF), sds((DB, TOKENS, BLK), BF)]
    prep = call(prep_kernel, prepped, [VMEM] * 4, scratch=[pltpu.VMEM((TOKENS, 2 * DQ), BF)])
    x0, y0 = prep(*pieces)
    x2, y2 = prep(*mirrors)
    x1, y1, x3, y3 = [row_swap(v, 1) for v in (x0, y0, x2, y2)]

    dest = lax.dynamic_slice_in_dim(block_dest[:, :, 0, :], group * QUARTERS, QUARTERS, axis=1)
    index = lax.dynamic_slice_in_dim(all_index, group * QUARTERS, QUARTERS, axis=1)
    swap = (jnp.arange(QUARTERS, dtype=jnp.int32) ^ quarter)[None, :, None]
    value = (swap * 64 + index + 1).reshape(3, 1, QUARTERS * CAP)
    targets = quarter * CAP + jnp.arange(CAP, dtype=jnp.int32)
    hits = dest.reshape(3, 1, QUARTERS * CAP) == targets[None, :, None]
    code = jnp.sum(jnp.where(hits, value, 0), axis=2, dtype=jnp.int32)

    grads = call(
        grad_kernel,
        sds((3, CAP, BLK, BLK), BF),
        [SMEM] + [VMEM] * 9,
        scratch=[
            pltpu.VMEM((QUARTERS * DB, BLK, TOKENS), BF),
            pltpu.VMEM((QUARTERS * DB, TOKENS, BLK), BF),
            pltpu.VMEM((FB, BLK, TOKENS), BF),
            pltpu.VMEM((FB, TOKENS, BLK), BF),
            pltpu.VMEM((FB, TOKENS, BLK), BF),
        ],
    )(code, full, x0, x1, x2, x3, y0, y1, y2, y3)
    return last[:, :DQ], last[:, DQ:], grads.reshape(3, 1, 1, CAP, BLK, BLK)


def solution(mesh):
    return jax.shard_map(
        body,
        mesh=mesh,
        in_specs=(
            P("row", "col"),
            P("row", "col"),
            P("row", "col", None, None, None),
            P("row", "col", None, None, None),
            P("row", "col", None, None, None),
            P(),
            P(None, None, "col", None),
        ),
        out_specs=(P("row", "col"), P("row", "col"), P(None, "row", "col", None, None, None)),
        check_vma=False,
    )
```

time: 843 us -> 167 us (0.20)
  waiting for transfers between devices: 618 us -> 48.1 us
  other arithmetic: 79.6 us -> 3.25 us
  local copies, waits for them, and re-layouts: 68.8 us -> 15.5 us
  Pallas kernels: 0 us -> 36.6 us
  starting transfers between devices: 38.2 us -> 61 us
  between operations: 14.6 us -> 0.93 us
  blocking collectives: 11.1 us -> 0 us
  matrix products: 9.59 us -> 0 us
    ppermute x51 -> x36, waiting for transfers between devices: 582 us -> 48.1 us  [the longest x30 26.6 us: row_swap(): return lax.ppermute(value, 'row', [(i, i ^ mask) for i in range(128)])]
    select_n x25 -> x0, other arithmetic: 39.5 us -> none  [the longest x11 33.8 us: collect_rows(): jnp.where(high_side, jnp.concatenate([partner, values], axis_dim), jnp.co...]
    pallas_call x0 -> x8, Pallas kernels: none -> 36.6 us  [the longest x1 21 us: body(): call(grad_kernel, sds((3, CAP, BLK, BLK), BF), [SMEM] + [VMEM] * 9, scrat...]
    reduce_scatter x2 -> x0, waiting for transfers between devices: 35.6 us -> none  [group_sums(): return lax.psum_scatter(values, 'col', scatter_dimension=1, tiled=True)]
    add x40 -> x2, other arithmetic: 29 us -> 0.01 us  [the longest x1 0.01 us: body(): value = (swap * 64 + index + 1).reshape(3, 1, QUARTERS * CAP)]
    gather x5 -> x0, local copies, waits for them, and re-layouts: 24.7 us -> none  [the longest x2 18.5 us: body(): picked = jnp.take_along_axis(group_pieces, source[:, :, None, None], axis=1)]
    ppermute x51 -> x36, starting transfers between devices: 38.1 us -> 61 us  [the longest x30 53.8 us: row_swap(): return lax.ppermute(value, 'row', [(i, i ^ mask) for i in range(128)])]
    scatter x3 -> x0, local copies, waits for them, and re-layouts: 15.4 us -> none  [the longest x2 10.2 us: gate_slab(): jnp.zeros((slot_count, BLK, BLK), blocks.dtype).at[positions]]
  transfers between devices with their start and end apart: 53 -> 36, of which waited for: 47 -> 13; matrix products, arithmetic and copies ran while one was open for 8% -> 3% of each run, Pallas kernels for 0% -> 20%
where the time goes in v1:
time: 167 us; the launch traced here: 165 us
  starting transfers between devices  61 us (37%)
  waiting for transfers between devices  48.1 us (29%)
  Pallas kernels  36.6 us (22%)
  local copies, waits for them, and re-layouts  15.5 us (9%)
  other arithmetic  3.25 us (2%)
    ppermute x30, starting transfers between devices, row_swap(): return lax.ppermute(value, 'row', [(i, i ^ mask) for i in range(128)])  53.8 us
    ppermute x30, waiting for transfers between devices, row_swap(): return lax.ppermute(value, 'row', [(i, i ^ mask) for i in range(128)])  26.6 us
    ppermute x6, waiting for transfers between devices, square_swap(): lax.ppermute(value, ('row', 'col'), [(i, i ^ mask) for i in range(256)])  21.5 us
    pallas_call x1, Pallas kernels, body(): call(grad_kernel, sds((3, CAP, BLK, BLK), BF), [SMEM] + [VMEM] * 9, scrat...  21 us
    unnamed x35, local copies, waits for them, and re-layouts  10.9 us
    ppermute x6, starting transfers between devices, square_swap(): lax.ppermute(value, ('row', 'col'), [(i, i ^ mask) for i in range(256)])  7.15 us
    pallas_call x1, Pallas kernels, body(): call(dense_kernel, wide, [SMEM, ANY, ANY, ANY], scratch=[pltpu.SemaphoreT...  5.88 us
    pallas_call x1, Pallas kernels, body(): call(out_kernel, [sds((64, 2 * DQ), F32)] + [sds((64, 2 * DQ), BF)] * 3 +...  3.86 us
  transfers between devices with their start and end apart: 36, of which 13 were waited for; matrix products, arithmetic and copies ran while one was open for 3% of the time, Pallas kernels for 20%

profile of v1, /device:TPU:32, one launch (start us, length us, event | category | flops | bytes accessed | tf_op | source)
XLA Modules:
  0.0 165.4 jit_solution(94794611021499037)
XLA Ops:
  2.1 3.3 %collective-permute-start = (bf16[8,2048]{1,0:T(8,128)(2,1)S(1)}, bf16[8,2048]{1,0:T(8,128)(2,1)S(1)}, u32[]{:S(2)}, u32[]{:S(2)}) collective-permute-start(bf16[8,2048]{1,0:T(8,128)(2,1)S(1)} %get-tuple-element.59), channel_id=1, source_target_pairs={{0,8},{2,10},{4,12},{6,14},{8,0},{10,2},{12,4},{14,6},{16,24},{18,... | collective-permute-start | bytes 98312 | tf_op jit(solution)/shard_map/ppermute | solution.py:30
  5.4 4.5 %collective-permute-start.1 = (bf16[8,2048]{1,0:T(8,128)(2,1)S(1)}, bf16[8,2048]{1,0:T(8,128)(2,1)S(1)}, u32[]{:S(2)}, u32[]{:S(2)}) collective-permute-start(bf16[8,2048]{1,0:T(8,128)(2,1)S(1)} %get-tuple-element.59), channel_id=1, source_target_pairs={{0,16},{2,18},{4,20},{6,22},{8,24},{10,26},{12,28},{14,30},{16,0},... | collective-permute-start | bytes 98312 | tf_op jit(solution)/shard_map/ppermute | solution.py:30
  9.9 3.2 %collective-permute-start.3 = (bf16[8,2048]{1,0:T(8,128)(2,1)S(1)}, bf16[8,2048]{1,0:T(8,128)(2,1)S(1)}, u32[]{:S(2)}, u32[]{:S(2)}) collective-permute-start(bf16[8,2048]{1,0:T(8,128)(2,1)S(1)} %get-tuple-element.59), channel_id=1, source_target_pairs={{0,128},{2,130},{4,132},{6,134},{8,136},{10,138},{12,140},{14,142}... | collective-permute-start | bytes 98312 | tf_op jit(solution)/shard_map/ppermute | solution.py:30
  13.1 1.8 %collective-permute-start.4 = (bf16[8,2048]{1,0:T(8,128)(2,1)S(1)}, bf16[8,2048]{1,0:T(8,128)(2,1)S(1)}, u32[]{:S(2)}, u32[]{:S(2)}) collective-permute-start(bf16[8,2048]{1,0:T(8,128)(2,1)S(1)} %get-tuple-element.59), channel_id=1, source_target_pairs={{0,136},{2,138},{4,140},{6,142},{8,128},{10,130},{12,132},{14,134}... | collective-permute-start | bytes 98312 | tf_op jit(solution)/shard_map/ppermute | solution.py:30
  14.9 7.1 %collective-permute-start.5 = (bf16[8,2048]{1,0:T(8,128)(2,1)S(1)}, bf16[8,2048]{1,0:T(8,128)(2,1)S(1)}, u32[]{:S(2)}, u32[]{:S(2)}) collective-permute-start(bf16[8,2048]{1,0:T(8,128)(2,1)S(1)} %get-tuple-element.59), channel_id=1, source_target_pairs={{0,144},{2,146},{4,148},{6,150},{8,152},{10,154},{12,156},{14,158}... | collective-permute-start | bytes 98312 | tf_op jit(solution)/shard_map/ppermute | solution.py:30
  22.1 3.0 %collective-permute-done.5 = bf16[8,2048]{1,0:T(8,128)(2,1)S(1)} collective-permute-done((bf16[8,2048]{1,0:T(8,128)(2,1)S(1)}, bf16[8,2048]{1,0:T(8,128)(2,1)S(1)}, u32[]{:S(2)}, u32[]{:S(2)}) %collective-permute-start.5) | collective-permute-done | bytes 32800 | tf_op jit(solution)/shard_map/ppermute | solution.py:30
  25.1 5.3 %collective-permute-done.6 = bf16[8,2048]{1,0:T(8,128)(2,1)S(1)} collective-permute-done((bf16[8,2048]{1,0:T(8,128)(2,1)S(1)}, bf16[8,2048]{1,0:T(8,128)(2,1)S(1)}, u32[]{:S(2)}, u32[]{:S(2)}) %collective-permute-start.6) | collective-permute-done | bytes 32800 | tf_op jit(solution)/shard_map/ppermute | solution.py:30
  31.9 2.7 %collective-permute-start.8 = (bf16[64,2048]{1,0:T(8,128)(2,1)S(1)}, bf16[64,2048]{1,0:T(8,128)(2,1)S(1)}, u32[]{:S(2)}, u32[]{:S(2)}) collective-permute-start(bf16[64,2048]{1,0:T(8,128)(2,1)S(1)} %constant_dynamic-update-slice_fusion.2.p0), channel_id=1, source_target_pairs={{0,64},{2,66},{4,68},{6,70},{8,72},{10,74},{12,76},{14,78},{16,80}... | collective-permute-start | bytes 786440 | tf_op jit(solution)/shard_map/ppermute | solution.py:30
  39.6 5.9 %shard_map.94 = (bf16[1024,896]{1,0:T(8,128)(2,1)S(1)}, bf16[1024,896]{1,0:T(8,128)(2,1)S(1)}, bf16[896,1024]{1,0:T(8,128)(2,1)S(1)}) custom-call(s32[3,48]{1,0:T(4,128)S(1)} %dynamic-slice_reduce_fusion.index_ref, bf16[48,128,128]{2,1,0:T(8,128)(2,1)S(1)} %bitcast.12, bf16[48,128,128]{2,1,0:T(8,128)(2,1)S(1)} %bitcast.13, bf16[48,128,128]{2,1,0:T(8,128)(2,1)S(1)} %bitcast.14), custom_call_target="tpu_custom_call" | custom-call | tf_op jit(solution)/shard_map/pallas_call | solution.py:209
  46.1 2.4 %shard_map.95 = (f32[128,2688]{1,0:T(8,128)S(1)}, f32[128,2688]{1,0:T(8,128)S(1)}) custom-call(s32[2]{0:T(128)S(1)} %pad_add_fusion.place_ref, bf16[64,2048]{1,0:T(8,128)(2,1)S(1)} %constant_dynamic-update-slice_fusion.2.p0, bf16[64,2048]{1,0:T(8,128)(2,1)S(1)} %collective-permute-done.7.p1, bf16[64,2048]{1,0:T(8,128)(2,1)S(1)} %collective-permute-done.8.p2, ...), custom_call_target="tpu_custom_call" | custom-call | tf_op jit(solution)/shard_map/pallas_call | solution.py:219
  48.6 3.1 %collective-permute-done.10.got_ref = f32[128,2688]{1,0:T(8,128)S(1)} collective-permute-done((f32[128,2688]{1,0:T(8,128)S(1)}, f32[128,2688]{1,0:T(8,128)S(1)}, u32[]{:S(2)}, u32[]{:S(2)}) %collective-permute-start.10) | collective-permute-done | bytes 1376288 | tf_op jit(solution)/shard_map/ppermute | solution.py:30
  54.2 1.8 %collective-permute-start.13 = (f32[32,2688]{1,0:T(8,128)S(1)}, f32[32,2688]{1,0:T(8,128)S(1)}, u32[]{:S(2)}, u32[]{:S(2)}) collective-permute-start(f32[32,2688]{1,0:T(8,128)S(1)} %get-tuple-element.29), channel_id=1, source_target_pairs={{0,5},{1,4},{2,7},{3,6},{4,1},{5,0},{6,3},{7,2},{8,13},{9,12},{10,... | collective-permute-start | bytes 1032200 | tf_op jit(solution)/shard_map/ppermute | solution.py:35
  56.0 6.6 %collective-permute-done.11.a1 = f32[32,2688]{1,0:T(8,128)S(1)} collective-permute-done((f32[32,2688]{1,0:T(8,128)S(1)}, f32[32,2688]{1,0:T(8,128)S(1)}, u32[]{:S(2)}, u32[]{:S(2)}) %collective-permute-start.11) | collective-permute-done | bytes 344096 | tf_op jit(solution)/shard_map/ppermute | solution.py:35
  62.6 1.5 collective-permute-done.12.a2
  64.2 7.0 %collective-permute-done.13.a3 = f32[32,2688]{1,0:T(8,128)S(1)} collective-permute-done((f32[32,2688]{1,0:T(8,128)S(1)}, f32[32,2688]{1,0:T(8,128)S(1)}, u32[]{:S(2)}, u32[]{:S(2)}) %collective-permute-start.13) | collective-permute-done | bytes 344096 | tf_op jit(solution)/shard_map/ppermute | solution.py:35
  74.9 4.5 %collective-permute-done.16 = bf16[32,2688]{1,0:T(8,128)(2,1)S(1)} collective-permute-done((bf16[32,2688]{1,0:T(8,128)(2,1)S(1)}, bf16[32,2688]{1,0:T(8,128)(2,1)S(1)}, u32[]{:S(2)}, u32[]{:S(2)}) %collective-permute-start.16) | collective-permute-done | bytes 172064 | tf_op jit(solution)/shard_map/ppermute | solution.py:35
  82.5 7.7 %collective-permute-done.29.p0 = bf16[64,2048]{1,0:T(8,128)(2,1)} collective-permute-done((bf16[64,2048]{1,0:T(8,128)(2,1)S(1)}, bf16[64,2048]{1,0:T(8,128)(2,1)}, u32[]{:S(2)}, u32[]{:S(2)}) %collective-permute-start.29) | collective-permute-done | bytes 262176 | tf_op jit(solution)/shard_map/ppermute | solution.py:30
  91.9 3.9 %collective-permute-start.31 = (bf16[64,2048]{1,0:T(8,128)(2,1)}, bf16[64,2048]{1,0:T(8,128)(2,1)}, u32[]{:S(2)}, u32[]{:S(2)}) collective-permute-start(bf16[64,2048]{1,0:T(8,128)(2,1)} %collective-permute-done.29.p0), channel_id=1, source_target_pairs={{0,64},{2,66},{4,68},{6,70},{8,72},{10,74},{12,76},{14,78},{16,80}... | collective-permute-start | bytes 786440 | tf_op jit(solution)/shard_map/ppermute | solution.py:30
  96.7 1.5 copy-done.2
  99.7 3.9 %shard_map.98 = (f32[64,2048]{1,0:T(8,128)S(1)}, bf16[64,2048]{1,0:T(8,128)(2,1)}, bf16[64,2048]{1,0:T(8,128)(2,1)}, bf16[64,2048]{1,0:T(8,128)(2,1)}, bf16[256,2688]{1,0:T(8,128)(2,1)S(1)}) custom-call(s32[2]{0:T(128)S(1)} %pad_add_fusion.place_ref, bf16[128,2688]{1,0:T(8,128)(2,1)S(1)} %pad_maximum_fusion.mine, ...), custom_call_target="tpu_custom_call" | custom-call | tf_op jit(solution)/shard_map/pallas_call | solution.py:228
  105.4 2.4 %collective-permute-start.20 = (bf16[64,2048]{1,0:T(8,128)(2,1)}, bf16[64,2048]{1,0:T(8,128)(2,1)}, u32[]{:S(2)}, u32[]{:S(2)}) collective-permute-start(bf16[64,2048]{1,0:T(8,128)(2,1)} %get-tuple-element.33), channel_id=1, source_target_pairs={{0,96},{2,98},{4,100},{6,102},{8,104},{10,106},{12,108},{14,110},{... | collective-permute-start | bytes 786440 | tf_op jit(solution)/shard_map/ppermute | solution.py:30
  107.8 1.7 %collective-permute-start.18 = (bf16[64,2048]{1,0:T(8,128)(2,1)}, bf16[64,2048]{1,0:T(8,128)(2,1)}, u32[]{:S(2)}, u32[]{:S(2)}) collective-permute-start(bf16[64,2048]{1,0:T(8,128)(2,1)} %get-tuple-element.31), channel_id=1, source_target_pairs={{0,32},{2,34},{4,36},{6,38},{8,40},{10,42},{12,44},{14,46},{16,48}... | collective-permute-start | bytes 786440 | tf_op jit(solution)/shard_map/ppermute | solution.py:30
  112.1 2.6 %collective-permute-done.32.p3 = bf16[64,2048]{1,0:T(8,128)(2,1)} collective-permute-done((bf16[64,2048]{1,0:T(8,128)(2,1)}, bf16[64,2048]{1,0:T(8,128)(2,1)}, u32[]{:S(2)}, u32[]{:S(2)}) %collective-permute-start.32) | collective-permute-done | bytes 262176 | tf_op jit(solution)/shard_map/ppermute | solution.py:30
  114.7 2.5 %shard_map.100 = (bf16[8,128,256]{2,1,0:T(8,128)(2,1)}, bf16[8,256,128]{2,1,0:T(8,128)(2,1)}) custom-call(bf16[64,2048]{1,0:T(8,128)(2,1)} %collective-permute-done.29.p0, bf16[64,2048]{1,0:T(8,128)(2,1)} %collective-permute-done.30.p1, bf16[64,2048]{1,0:T(8,128)(2,1)} %collective-permute-done.31.p2, bf16[64,2048]{1,0:T(8,128)(2,1)} %collective-permute-done.32.p3), custom_call_target="tpu_custom_call" | custom-call | tf_op jit(solution)/shard_map/pallas_call | solution.py:247
  117.2 4.2 %collective-permute-done.20 = bf16[64,2048]{1,0:T(8,128)(2,1)} collective-permute-done((bf16[64,2048]{1,0:T(8,128)(2,1)}, bf16[64,2048]{1,0:T(8,128)(2,1)}, u32[]{:S(2)}, u32[]{:S(2)}) %collective-permute-start.20) | collective-permute-done | bytes 262176 | tf_op jit(solution)/shard_map/ppermute | solution.py:30
  121.9 2.0 %fusion.7 = (bf16[64,2048]{1,0:T(8,128)(2,1)S(1)}, f32[64,2048]{1,0:T(8,128)}) fusion(bf16[64,2048]{1,0:T(8,128)(2,1)} %collective-permute-done.20, bf16[64,2048]{1,0:T(8,128)(2,1)} %collective-permute-done.19, f32[64,2048]{1,0:T(8,128)S(1)} %copy-done.13, bf16[64,2048]{1,0:T(8,128)(2,1)} %collective-permute-done.18), kind=kLoop, calls=%fused_computation.29 | loop fusion | flops 917504 | bytes 2097152 | tf_op jit(solution)/shard_map/convert.6
  125.1 6.0 %collective-permute-start.26 = (bf16[8,2048]{1,0:T(8,128)(2,1)S(1)}, bf16[8,2048]{1,0:T(8,128)(2,1)S(1)}, u32[]{:S(2)}, u32[]{:S(2)}) collective-permute-start(bf16[8,2048]{1,0:T(8,128)(2,1)S(1)} %get-tuple-element.52), channel_id=1, source_target_pairs={{0,144},{2,146},{4,148},{6,150},{8,152},{10,154},{12,156},{14,158}... | collective-permute-start | bytes 98312 | tf_op jit(solution)/shard_map/ppermute | solution.py:30
  131.3 2.7 %collective-permute-start.25 = (bf16[8,2048]{1,0:T(8,128)(2,1)S(1)}, bf16[8,2048]{1,0:T(8,128)(2,1)S(1)}, u32[]{:S(2)}, u32[]{:S(2)}) collective-permute-start(bf16[8,2048]{1,0:T(8,128)(2,1)S(1)} %get-tuple-element.53), channel_id=1, source_target_pairs={{0,136},{2,138},{4,140},{6,142},{8,128},{10,130},{12,132},{14,134}... | collective-permute-start | bytes 98312 | tf_op jit(solution)/shard_map/ppermute | solution.py:30
  133.9 2.3 %collective-permute-start.24 = (bf16[8,2048]{1,0:T(8,128)(2,1)S(1)}, bf16[8,2048]{1,0:T(8,128)(2,1)S(1)}, u32[]{:S(2)}, u32[]{:S(2)}) collective-permute-start(bf16[8,2048]{1,0:T(8,128)(2,1)S(1)} %get-tuple-element.54), channel_id=1, source_target_pairs={{0,128},{2,130},{4,132},{6,134},{8,136},{10,138},{12,140},{14,142}... | collective-permute-start | bytes 98312 | tf_op jit(solution)/shard_map/ppermute | solution.py:30
  136.2 4.6 %collective-permute-start.22 = (bf16[8,2048]{1,0:T(8,128)(2,1)S(1)}, bf16[8,2048]{1,0:T(8,128)(2,1)S(1)}, u32[]{:S(2)}, u32[]{:S(2)}) collective-permute-start(bf16[8,2048]{1,0:T(8,128)(2,1)S(1)} %get-tuple-element.56), channel_id=1, source_target_pairs={{0,16},{2,18},{4,20},{6,22},{8,24},{10,26},{12,28},{14,30},{16,0},... | collective-permute-start | bytes 98312 | tf_op jit(solution)/shard_map/ppermute | solution.py:30
  140.8 1.9 %collective-permute-start.21 = (bf16[8,2048]{1,0:T(8,128)(2,1)S(1)}, bf16[8,2048]{1,0:T(8,128)(2,1)S(1)}, u32[]{:S(2)}, u32[]{:S(2)}) collective-permute-start(bf16[8,2048]{1,0:T(8,128)(2,1)S(1)} %get-tuple-element.50), channel_id=1, source_target_pairs={{0,8},{2,10},{4,12},{6,14},{8,0},{10,2},{12,4},{14,6},{16,24},{18,... | collective-permute-start | bytes 98312 | tf_op jit(solution)/shard_map/ppermute | solution.py:30
  142.9 21.0 %shard_map.101 = bf16[3,48,128,128]{3,2,1,0:T(8,128)(2,1)} custom-call(s32[3,48]{1,0:T(4,128)S(1)} %select_reduce_fusion.code_ref, bf16[256,2688]{1,0:T(8,128)(2,1)S(1)} %copy-done.9, bf16[8,128,256]{2,1,0:T(8,128)(2,1)S(1)} %get-tuple-element.35.x0, bf16[8,128,256]{2,1,0:T(8,128)(2,1)S(1)} %collective-permute-done.28.x1, ...), custom_call_target="tpu_custom_call" | custom-call | tf_op jit(solution)/shard_map/pallas_call | solution.py:258
  (104 shorter events, 29.9 us)
Async XLA Ops:
  2.1 12.7 %collective-permute-start = (bf16[8,2048]{1,0:T(8,128)(2,1)S(1)}, bf16[8,2048]{1,0:T(8,128)(2,1)S(1)}, u32[]{:S(2)}, u32[]{:S(2)}) collective-permute-start(bf16[8,2048]{1,0:T(8,128)(2,1)S(1)} %get-tuple-element.59), channel_id=1, source_target_pairs={{0,8},{2,10},{4,12},{6,14},{8,0},{10,2},{12,4},{14,6},{16,24},{18,... | collective-permute-start | bytes 98312 | tf_op jit(solution)/shard_map/ppermute | solution.py:30
  5.4 16.6 %collective-permute-start.1 = (bf16[8,2048]{1,0:T(8,128)(2,1)S(1)}, bf16[8,2048]{1,0:T(8,128)(2,1)S(1)}, u32[]{:S(2)}, u32[]{:S(2)}) collective-permute-start(bf16[8,2048]{1,0:T(8,128)(2,1)S(1)} %get-tuple-element.59), channel_id=1, source_target_pairs={{0,16},{2,18},{4,20},{6,22},{8,24},{10,26},{12,28},{14,30},{16,0},... | collective-permute-start | bytes 98312 | tf_op jit(solution)/shard_map/ppermute | solution.py:30
  9.9 12.1 %collective-permute-start.2 = (bf16[8,2048]{1,0:T(8,128)(2,1)S(1)}, bf16[8,2048]{1,0:T(8,128)(2,1)S(1)}, u32[]{:S(2)}, u32[]{:S(2)}) collective-permute-start(bf16[8,2048]{1,0:T(8,128)(2,1)S(1)} %get-tuple-element.59), channel_id=1, source_target_pairs={{0,24},{2,26},{4,28},{6,30},{8,16},{10,18},{12,20},{14,22},{16,8},... | collective-permute-start | bytes 98312 | tf_op jit(solution)/shard_map/ppermute | solution.py:30
  9.9 12.2 %collective-permute-start.3 = (bf16[8,2048]{1,0:T(8,128)(2,1)S(1)}, bf16[8,2048]{1,0:T(8,128)(2,1)S(1)}, u32[]{:S(2)}, u32[]{:S(2)}) collective-permute-start(bf16[8,2048]{1,0:T(8,128)(2,1)S(1)} %get-tuple-element.59), channel_id=1, source_target_pairs={{0,128},{2,130},{4,132},{6,134},{8,136},{10,138},{12,140},{14,142}... | collective-permute-start | bytes 98312 | tf_op jit(solution)/shard_map/ppermute | solution.py:30
  13.1 9.0 %collective-permute-start.4 = (bf16[8,2048]{1,0:T(8,128)(2,1)S(1)}, bf16[8,2048]{1,0:T(8,128)(2,1)S(1)}, u32[]{:S(2)}, u32[]{:S(2)}) collective-permute-start(bf16[8,2048]{1,0:T(8,128)(2,1)S(1)} %get-tuple-element.59), channel_id=1, source_target_pairs={{0,136},{2,138},{4,140},{6,142},{8,128},{10,130},{12,132},{14,134}... | collective-permute-start | bytes 98312 | tf_op jit(solution)/shard_map/ppermute | solution.py:30
  14.9 10.3 %collective-permute-start.5 = (bf16[8,2048]{1,0:T(8,128)(2,1)S(1)}, bf16[8,2048]{1,0:T(8,128)(2,1)S(1)}, u32[]{:S(2)}, u32[]{:S(2)}) collective-permute-start(bf16[8,2048]{1,0:T(8,128)(2,1)S(1)} %get-tuple-element.59), channel_id=1, source_target_pairs={{0,144},{2,146},{4,148},{6,150},{8,152},{10,154},{12,156},{14,158}... | collective-permute-start | bytes 98312 | tf_op jit(solution)/shard_map/ppermute | solution.py:30
  22.0 8.4 %collective-permute-start.6 = (bf16[8,2048]{1,0:T(8,128)(2,1)S(1)}, bf16[8,2048]{1,0:T(8,128)(2,1)S(1)}, u32[]{:S(2)}, u32[]{:S(2)}) collective-permute-start(bf16[8,2048]{1,0:T(8,128)(2,1)S(1)} %get-tuple-element.59), channel_id=1, source_target_pairs={{0,152},{2,154},{4,156},{6,158},{8,144},{10,146},{12,148},{14,150}... | collective-permute-start | bytes 98312 | tf_op jit(solution)/shard_map/ppermute | solution.py:30
  30.4 15.1 %collective-permute-start.7 = (bf16[64,2048]{1,0:T(8,128)(2,1)S(1)}, bf16[64,2048]{1,0:T(8,128)(2,1)S(1)}, u32[]{:S(2)}, u32[]{:S(2)}) collective-permute-start(bf16[64,2048]{1,0:T(8,128)(2,1)S(1)} %constant_dynamic-update-slice_fusion.2.p0), channel_id=1, source_target_pairs={{0,32},{2,34},{4,36},{6,38},{8,40},{10,42},{12,44},{14,46},{16,48}... | collective-permute-start | bytes 786440 | tf_op jit(solution)/shard_map/ppermute | solution.py:30
  31.9 13.7 %collective-permute-start.8 = (bf16[64,2048]{1,0:T(8,128)(2,1)S(1)}, bf16[64,2048]{1,0:T(8,128)(2,1)S(1)}, u32[]{:S(2)}, u32[]{:S(2)}) collective-permute-start(bf16[64,2048]{1,0:T(8,128)(2,1)S(1)} %constant_dynamic-update-slice_fusion.2.p0), channel_id=1, source_target_pairs={{0,64},{2,66},{4,68},{6,70},{8,72},{10,74},{12,76},{14,78},{16,80}... | collective-permute-start | bytes 786440 | tf_op jit(solution)/shard_map/ppermute | solution.py:30
  34.6 11.5 %collective-permute-start.9 = (bf16[64,2048]{1,0:T(8,128)(2,1)S(1)}, bf16[64,2048]{1,0:T(8,128)(2,1)S(1)}, u32[]{:S(2)}, u32[]{:S(2)}) collective-permute-start(bf16[64,2048]{1,0:T(8,128)(2,1)S(1)} %constant_dynamic-update-slice_fusion.2.p0), channel_id=1, source_target_pairs={{0,96},{2,98},{4,100},{6,102},{8,104},{10,106},{12,108},{14,110},{... | collective-permute-start | bytes 786440 | tf_op jit(solution)/shard_map/ppermute | solution.py:30
  52.5 10.2 %collective-permute-start.11 = (f32[32,2688]{1,0:T(8,128)S(1)}, f32[32,2688]{1,0:T(8,128)S(1)}, u32[]{:S(2)}, u32[]{:S(2)}) collective-permute-start(f32[32,2688]{1,0:T(8,128)S(1)} %get-tuple-element.27), channel_id=1, source_target_pairs={{0,1},{1,0},{2,3},{3,2},{4,5},{5,4},{6,7},{7,6},{8,9},{9,8},{10,11... | collective-permute-start | bytes 1032200 | tf_op jit(solution)/shard_map/ppermute | solution.py:35
  53.2 10.9 %collective-permute-start.12 = (f32[32,2688]{1,0:T(8,128)S(1)}, f32[32,2688]{1,0:T(8,128)S(1)}, u32[]{:S(2)}, u32[]{:S(2)}) collective-permute-start(f32[32,2688]{1,0:T(8,128)S(1)} %get-tuple-element.28), channel_id=1, source_target_pairs={{0,4},{1,5},{2,6},{3,7},{4,0},{5,1},{6,2},{7,3},{8,12},{9,13},{10,... | collective-permute-start | bytes 1032200 | tf_op jit(solution)/shard_map/ppermute | solution.py:35
  54.2 17.0 %collective-permute-start.13 = (f32[32,2688]{1,0:T(8,128)S(1)}, f32[32,2688]{1,0:T(8,128)S(1)}, u32[]{:S(2)}, u32[]{:S(2)}) collective-permute-start(f32[32,2688]{1,0:T(8,128)S(1)} %get-tuple-element.29), channel_id=1, source_target_pairs={{0,5},{1,4},{2,7},{3,6},{4,1},{5,0},{6,3},{7,2},{8,13},{9,12},{10,... | collective-permute-start | bytes 1032200 | tf_op jit(solution)/shard_map/ppermute | solution.py:35
  81.3 15.4 %collective-permute-start.17 = (bf16[128,2688]{1,0:T(8,128)(2,1)S(1)}, bf16[128,2688]{1,0:T(8,128)(2,1)}, u32[]{:S(2)}, u32[]{:S(2)}) collective-permute-start(bf16[128,2688]{1,0:T(8,128)(2,1)S(1)} %pad_maximum_fusion.mine), channel_id=1, source_target_pairs={{0,2},{2,0},{4,6},{6,4},{8,10},{10,8},{12,14},{14,12},{16,18},{18,... | collective-permute-start | bytes 2064392 | tf_op jit(solution)/shard_map/ppermute | solution.py:30
  81.4 8.8 %collective-permute-start.29 = (bf16[64,2048]{1,0:T(8,128)(2,1)S(1)}, bf16[64,2048]{1,0:T(8,128)(2,1)}, u32[]{:S(2)}, u32[]{:S(2)}) collective-permute-start(bf16[64,2048]{1,0:T(8,128)(2,1)S(1)} %constant_dynamic-update-slice_fusion.2.p0), channel_id=1, source_target_pairs={{0,4},{2,6},{4,0},{6,2},{8,12},{10,14},{12,8},{14,10},{16,20},{18,... | collective-permute-start | bytes 786440 | tf_op jit(solution)/shard_map/ppermute | solution.py:30
  90.2 17.6 %collective-permute-start.30 = (bf16[64,2048]{1,0:T(8,128)(2,1)}, bf16[64,2048]{1,0:T(8,128)(2,1)}, u32[]{:S(2)}, u32[]{:S(2)}) collective-permute-start(bf16[64,2048]{1,0:T(8,128)(2,1)} %collective-permute-done.29.p0), channel_id=1, source_target_pairs={{0,32},{2,34},{4,36},{6,38},{8,40},{10,42},{12,44},{14,46},{16,48}... | collective-permute-start | bytes 786440 | tf_op jit(solution)/shard_map/ppermute | solution.py:30
  91.9 20.1 %collective-permute-start.31 = (bf16[64,2048]{1,0:T(8,128)(2,1)}, bf16[64,2048]{1,0:T(8,128)(2,1)}, u32[]{:S(2)}, u32[]{:S(2)}) collective-permute-start(bf16[64,2048]{1,0:T(8,128)(2,1)} %collective-permute-done.29.p0), channel_id=1, source_target_pairs={{0,64},{2,66},{4,68},{6,70},{8,72},{10,74},{12,76},{14,78},{16,80}... | collective-permute-start | bytes 786440 | tf_op jit(solution)/shard_map/ppermute | solution.py:30
  95.9 18.9 %collective-permute-start.32 = (bf16[64,2048]{1,0:T(8,128)(2,1)}, bf16[64,2048]{1,0:T(8,128)(2,1)}, u32[]{:S(2)}, u32[]{:S(2)}) collective-permute-start(bf16[64,2048]{1,0:T(8,128)(2,1)} %collective-permute-done.29.p0), channel_id=1, source_target_pairs={{0,96},{2,98},{4,100},{6,102},{8,104},{10,106},{12,108},{14,110},{... | collective-permute-start | bytes 786440 | tf_op jit(solution)/shard_map/ppermute | solution.py:30
  105.4 16.0 %collective-permute-start.20 = (bf16[64,2048]{1,0:T(8,128)(2,1)}, bf16[64,2048]{1,0:T(8,128)(2,1)}, u32[]{:S(2)}, u32[]{:S(2)}) collective-permute-start(bf16[64,2048]{1,0:T(8,128)(2,1)} %get-tuple-element.33), channel_id=1, source_target_pairs={{0,96},{2,98},{4,100},{6,102},{8,104},{10,106},{12,108},{14,110},{... | collective-permute-start | bytes 786440 | tf_op jit(solution)/shard_map/ppermute | solution.py:30
  107.8 13.6 %collective-permute-start.19 = (bf16[64,2048]{1,0:T(8,128)(2,1)}, bf16[64,2048]{1,0:T(8,128)(2,1)}, u32[]{:S(2)}, u32[]{:S(2)}) collective-permute-start(bf16[64,2048]{1,0:T(8,128)(2,1)} %get-tuple-element.32), channel_id=1, source_target_pairs={{0,64},{2,66},{4,68},{6,70},{8,72},{10,74},{12,76},{14,78},{16,80}... | collective-permute-start | bytes 786440 | tf_op jit(solution)/shard_map/ppermute | solution.py:30
  107.8 14.1 %collective-permute-start.18 = (bf16[64,2048]{1,0:T(8,128)(2,1)}, bf16[64,2048]{1,0:T(8,128)(2,1)}, u32[]{:S(2)}, u32[]{:S(2)}) collective-permute-start(bf16[64,2048]{1,0:T(8,128)(2,1)} %get-tuple-element.31), channel_id=1, source_target_pairs={{0,32},{2,34},{4,36},{6,38},{8,40},{10,42},{12,44},{14,46},{16,48}... | collective-permute-start | bytes 786440 | tf_op jit(solution)/shard_map/ppermute | solution.py:30
  112.0 13.0 %collective-permute-start.28 = (bf16[8,128,256]{2,1,0:T(8,128)(2,1)S(1)}, bf16[8,128,256]{2,1,0:T(8,128)(2,1)S(1)}, u32[]{:S(2)}, u32[]{:S(2)}) collective-permute-start(bf16[8,128,256]{2,1,0:T(8,128)(2,1)S(1)} %get-tuple-element.35.x0), channel_id=1, source_target_pairs={{0,2},{2,0},{4,6},{6,4},{8,10},{10,8},{12,14},{14,12},{16,18},{18,... | collective-permute-start | bytes 1572872 | tf_op jit(solution)/shard_map/ppermute | solution.py:30
  114.7 16.5 %collective-permute-start.34 = (bf16[8,256,128]{2,1,0:T(8,128)(2,1)S(1)}, bf16[8,256,128]{2,1,0:T(8,128)(2,1)}, u32[]{:S(2)}, u32[]{:S(2)}) collective-permute-start(bf16[8,256,128]{2,1,0:T(8,128)(2,1)S(1)} %get-tuple-element.37.y0), channel_id=1, source_target_pairs={{0,2},{2,0},{4,6},{6,4},{8,10},{10,8},{12,14},{14,12},{16,18},{18,... | collective-permute-start | bytes 1572872 | tf_op jit(solution)/shard_map/ppermute | solution.py:30
  121.4 12.5 %collective-permute-start.33 = (bf16[8,128,256]{2,1,0:T(8,128)(2,1)}, bf16[8,128,256]{2,1,0:T(8,128)(2,1)}, u32[]{:S(2)}, u32[]{:S(2)}) collective-permute-start(bf16[8,128,256]{2,1,0:T(8,128)(2,1)} %get-tuple-element.36.x2), channel_id=1, source_target_pairs={{0,2},{2,0},{4,6},{6,4},{8,10},{10,8},{12,14},{14,12},{16,18},{18,... | collective-permute-start | bytes 1572872 | tf_op jit(solution)/shard_map/ppermute | solution.py:30
  121.4 14.8 %collective-permute-start.35 = (bf16[8,256,128]{2,1,0:T(8,128)(2,1)}, bf16[8,256,128]{2,1,0:T(8,128)(2,1)}, u32[]{:S(2)}, u32[]{:S(2)}) collective-permute-start(bf16[8,256,128]{2,1,0:T(8,128)(2,1)} %get-tuple-element.38.y2), channel_id=1, source_target_pairs={{0,2},{2,0},{4,6},{6,4},{8,10},{10,8},{12,14},{14,12},{16,18},{18,... | collective-permute-start | bytes 1572872 | tf_op jit(solution)/shard_map/ppermute | solution.py:30
  124.0 12.2 %collective-permute-start.27 = (bf16[8,2048]{1,0:T(8,128)(2,1)S(1)}, bf16[8,2048]{1,0:T(8,128)(2,1)S(1)}, u32[]{:S(2)}, u32[]{:S(2)}) collective-permute-start(bf16[8,2048]{1,0:T(8,128)(2,1)S(1)} %get-tuple-element.51), channel_id=1, source_target_pairs={{0,152},{2,154},{4,156},{6,158},{8,144},{10,146},{12,148},{14,150}... | collective-permute-start | bytes 98312 | tf_op jit(solution)/shard_map/ppermute | solution.py:30
  125.1 15.7 %collective-permute-start.26 = (bf16[8,2048]{1,0:T(8,128)(2,1)S(1)}, bf16[8,2048]{1,0:T(8,128)(2,1)S(1)}, u32[]{:S(2)}, u32[]{:S(2)}) collective-permute-start(bf16[8,2048]{1,0:T(8,128)(2,1)S(1)} %get-tuple-element.52), channel_id=1, source_target_pairs={{0,144},{2,146},{4,148},{6,150},{8,152},{10,154},{12,156},{14,158}... | collective-permute-start | bytes 98312 | tf_op jit(solution)/shard_map/ppermute | solution.py:30
  131.3 32.6 %collective-permute-start.25 = (bf16[8,2048]{1,0:T(8,128)(2,1)S(1)}, bf16[8,2048]{1,0:T(8,128)(2,1)S(1)}, u32[]{:S(2)}, u32[]{:S(2)}) collective-permute-start(bf16[8,2048]{1,0:T(8,128)(2,1)S(1)} %get-tuple-element.53), channel_id=1, source_target_pairs={{0,136},{2,138},{4,140},{6,142},{8,128},{10,130},{12,132},{14,134}... | collective-permute-start | bytes 98312 | tf_op jit(solution)/shard_map/ppermute | solution.py:30
  133.9 30.0 %collective-permute-start.24 = (bf16[8,2048]{1,0:T(8,128)(2,1)S(1)}, bf16[8,2048]{1,0:T(8,128)(2,1)S(1)}, u32[]{:S(2)}, u32[]{:S(2)}) collective-permute-start(bf16[8,2048]{1,0:T(8,128)(2,1)S(1)} %get-tuple-element.54), channel_id=1, source_target_pairs={{0,128},{2,130},{4,132},{6,134},{8,136},{10,138},{12,140},{14,142}... | collective-permute-start | bytes 98312 | tf_op jit(solution)/shard_map/ppermute | solution.py:30
  136.2 27.7 %collective-permute-start.23 = (bf16[8,2048]{1,0:T(8,128)(2,1)S(1)}, bf16[8,2048]{1,0:T(8,128)(2,1)S(1)}, u32[]{:S(2)}, u32[]{:S(2)}) collective-permute-start(bf16[8,2048]{1,0:T(8,128)(2,1)S(1)} %get-tuple-element.55), channel_id=1, source_target_pairs={{0,24},{2,26},{4,28},{6,30},{8,16},{10,18},{12,20},{14,22},{16,8},... | collective-permute-start | bytes 98312 | tf_op jit(solution)/shard_map/ppermute | solution.py:30
  136.2 27.7 %collective-permute-start.22 = (bf16[8,2048]{1,0:T(8,128)(2,1)S(1)}, bf16[8,2048]{1,0:T(8,128)(2,1)S(1)}, u32[]{:S(2)}, u32[]{:S(2)}) collective-permute-start(bf16[8,2048]{1,0:T(8,128)(2,1)S(1)} %get-tuple-element.56), channel_id=1, source_target_pairs={{0,16},{2,18},{4,20},{6,22},{8,24},{10,26},{12,28},{14,30},{16,0},... | collective-permute-start | bytes 98312 | tf_op jit(solution)/shard_map/ppermute | solution.py:30
  140.8 23.1 %collective-permute-start.21 = (bf16[8,2048]{1,0:T(8,128)(2,1)S(1)}, bf16[8,2048]{1,0:T(8,128)(2,1)S(1)}, u32[]{:S(2)}, u32[]{:S(2)}) collective-permute-start(bf16[8,2048]{1,0:T(8,128)(2,1)S(1)} %get-tuple-element.50), channel_id=1, source_target_pairs={{0,8},{2,10},{4,12},{6,14},{8,0},{10,2},{12,4},{14,6},{16,24},{18,... | collective-permute-start | bytes 98312 | tf_op jit(solution)/shard_map/ppermute | solution.py:30
  (18 other events, 116.0 us)

commit v2 on v1

--- a/solution.py
+++ b/solution.py
@@ -16,14 +16,13 @@
 DQ = 1024
 HB = 896
 TG = 8
-GROUPS = 32
+STEP = 8
 TOKENS = 256
 BF = jnp.bfloat16
 F32 = jnp.float32
 NT = (((1,), (1,)), ((), ()))
 VMEM = pl.BlockSpec(memory_space=pltpu.VMEM)
 SMEM = pl.BlockSpec(memory_space=pltpu.SMEM)
-ANY = pl.BlockSpec(memory_space=pl.ANY)
 
 
 def row_swap(value, mask):
@@ -35,8 +34,11 @@
     return lax.ppermute(value, ("row", "col"), [(i, i ^ mask) for i in range(256)])
 
 
-def deep_mask(step):
-    return (step & 3) << 2 | (step >> 2) << 6
+def z_mask(step):
+    return step << 2
+
+
+Y_MASK = 64
 
 
 def x_mask(step):
@@ -47,7 +49,7 @@
     return jax.ShapeDtypeStruct(shape, dtype)
 
 
-def call(kernel, out_shape, in_specs, out_specs=None, scratch=(), limit=40, cost=None):
+def call(kernel, out_shape, in_specs, out_specs=None, scratch=(), limit=16, grid=()):
     many = isinstance(out_shape, (tuple, list))
     if out_specs is None:
         out_specs = [VMEM] * len(out_shape) if many else VMEM
@@ -56,43 +58,31 @@
         out_shape=out_shape,
         in_specs=in_specs,
         out_specs=out_specs,
+        grid=grid,
         scratch_shapes=list(scratch),
         compiler_params=pltpu.CompilerParams(vmem_limit_bytes=limit * 2**20),
-        cost_estimate=cost,
     )
 
 
-def dense_kernel(index_ref, gate_ref, up_ref, down_ref, wg_ref, wu_ref, wd_ref, sems):
+def dense_kernel(index_ref, gate_ref, up_ref, down_ref, wg_ref, wu_ref, wd_ref):
     wg_ref[...] = jnp.zeros_like(wg_ref)
     wu_ref[...] = jnp.zeros_like(wu_ref)
     wd_ref[...] = jnp.zeros_like(wd_ref)
 
-    def each(act):
-        def one(slot, carry):
-            for m, (blocks, dense) in enumerate(
-                ((gate_ref, wg_ref), (up_ref, wu_ref), (down_ref, wd_ref))
-            ):
-                place = index_ref[m, slot]
-
-                @pl.when(place < SLOTS)
-                def _():
-                    hid = pl.multiple_of(place // DB * BLK, BLK)
-                    feat = pl.multiple_of(place % DB * BLK, BLK)
-                    first, second = (hid, feat) if m == 2 else (feat, hid)
-                    act(
-                        pltpu.make_async_copy(
-                            blocks.at[slot],
-                            dense.at[pl.ds(first, BLK), pl.ds(second, BLK)],
-                            sems.at[m, slot],
-                        )
-                    )
-
-            return carry
-
-        lax.fori_loop(0, CAP, one, 0)
-
-    each(lambda copy: copy.start())
-    each(lambda copy: copy.wait())
+    def one(slot, carry):
+        for m, (blocks, dense) in enumerate(((gate_ref, wg_ref), (up_ref, wu_ref), (down_ref, wd_ref))):
+            place = index_ref[m, slot]
+
+            @pl.when(place < SLOTS)
+            def _():
+                hid = pl.multiple_of(place // DB * BLK, BLK)
+                feat = pl.multiple_of(place % DB * BLK, BLK)
+                first, second = (hid, feat) if m == 2 else (feat, hid)
+                dense[pl.ds(first, BLK), pl.ds(second, BLK)] = blocks[slot]
+
+        return carry
+
+    lax.fori_loop(0, CAP, one, 0)
 
 
 def partial_kernel(place_ref, p0, p1, p2, p3, wg_ref, wu_ref, wd_ref, keep_ref, send_ref, rows):
@@ -164,33 +154,27 @@
 
 
 def grad_kernel(code_ref, full_ref, x0, x1, x2, x3, y0, y1, y2, y3, out_ref, xt, dy, ht, dg, du):
-    for j, (x, y) in enumerate(((x0, y0), (x1, y1), (x2, y2), (x3, y3))):
-        xt[j * DB : (j + 1) * DB] = x[...]
-        dy[j * DB : (j + 1) * DB] = y[...]
-    for a in range(FB):
-        ht[a] = full_ref[:, a * BLK : (a + 1) * BLK].T
-        dg[a] = full_ref[:, HB + a * BLK : HB + (a + 1) * BLK]
-        du[a] = full_ref[:, 2 * HB + a * BLK : 2 * HB + (a + 1) * BLK]
-
-    def one(slot, carry):
+    turn = pl.program_id(0)
+
+    @pl.when(turn == 0)
+    def _():
+        for j, (x, y) in enumerate(((x0, y0), (x1, y1), (x2, y2), (x3, y3))):
+            xt[j * DB : (j + 1) * DB] = x[...]
+            dy[j * DB : (j + 1) * DB] = y[...]
+        for a in range(FB):
+            ht[a] = full_ref[:, a * BLK : (a + 1) * BLK].T
+            dg[a] = full_ref[:, HB + a * BLK : HB + (a + 1) * BLK]
+            du[a] = full_ref[:, 2 * HB + a * BLK : 2 * HB + (a + 1) * BLK]
+
+    for near in range(STEP):
         for m in range(3):
-            code = code_ref[m, slot]
-
-            @pl.when(code > 0)
-            def _():
-                where = code - 1
-                feat = where // 64 * DB + where % 8
-                hid = where % 64 // 8
-                left, right = ((xt.at[feat], dg.at[hid]), (xt.at[feat], du.at[hid]), (ht.at[hid], dy.at[feat]))[m]
-                out_ref[m, slot] = jnp.dot(left[...], right[...], preferred_element_type=F32).astype(BF)
-
-            @pl.when(code == 0)
-            def _():
-                out_ref[m, slot] = jnp.zeros((BLK, BLK), BF)
-
-        return carry
-
-    lax.fori_loop(0, CAP, one, 0)
+            code = code_ref[m, turn * STEP + near]
+            where = jnp.maximum(code - 1, 0)
+            feat = where // 64 * DB + where % 8
+            hid = where % 64 // 8
+            left, right = ((xt.at[feat], dg.at[hid]), (xt.at[feat], du.at[hid]), (ht.at[hid], dy.at[feat]))[m]
+            value = jnp.dot(left[...], right[...], preferred_element_type=F32)
+            out_ref[m, near] = jnp.where(code > 0, value, 0.0).astype(BF)
 
 
 def body(activations, out_grad, gate_blocks, up_blocks, down_blocks, block_index, block_dest):
@@ -202,18 +186,28 @@
     all_index = lax.dynamic_index_in_dim(block_index, col, axis=2, keepdims=False)
     own_index = lax.dynamic_index_in_dim(all_index, row, axis=1, keepdims=False)
 
+    tie = lax.optimization_barrier
     shard = jnp.concatenate([activations, out_grad], axis=1)
-    near = jnp.concatenate([shard] + [row_swap(shard, deep_mask(i)) for i in range(1, 8)], axis=0)
+    pair = jnp.concatenate([shard, row_swap(shard, Y_MASK)], axis=0)
+    near = jnp.concatenate([pair] + [row_swap(pair, z_mask(i)) for i in range(1, 4)], axis=0)
     pieces = [near] + [row_swap(near, x_mask(i)) for i in range(1, 4)]
+    mirror = row_swap(near, 2)
+
     wide = [sds((DQ, HB), BF), sds((DQ, HB), BF), sds((HB, DQ), BF)]
-    wg, wu, wd = call(
-        dense_kernel, wide, [SMEM, ANY, ANY, ANY], scratch=[pltpu.SemaphoreType.DMA((3, CAP))], limit=24
-    )(
+    wg, wu, wd = call(dense_kernel, wide, [SMEM] + [VMEM] * 3)(
         own_index,
         gate_blocks.reshape(CAP, BLK, BLK),
         up_blocks.reshape(CAP, BLK, BLK),
         down_blocks.reshape(CAP, BLK, BLK),
     )
+    dest = lax.dynamic_slice_in_dim(block_dest[:, :, 0, :], group * QUARTERS, QUARTERS, axis=1)
+    index = lax.dynamic_slice_in_dim(all_index, group * QUARTERS, QUARTERS, axis=1)
+    swap = (jnp.arange(QUARTERS, dtype=jnp.int32) ^ quarter)[None, :, None]
+    value = (swap * 64 + index + 1).reshape(3, 1, QUARTERS * CAP)
+    targets = quarter * CAP + jnp.arange(CAP, dtype=jnp.int32)
+    hits = dest.reshape(3, 1, QUARTERS * CAP) == targets[None, :, None]
+    code = jnp.sum(jnp.where(hits, value, 0), axis=2, dtype=jnp.int32)
+    pieces, mirror, code = tie((pieces, mirror, code))
 
     half = sds((128, 3 * HB), F32)
     keep, send = call(
@@ -222,8 +216,20 @@
     got = row_swap(send, 1)
     fours = call(pair_kernel, [sds((32, 3 * HB), F32)] * 4, [SMEM, VMEM, VMEM])(place, keep, got)
     sums = [fours[0]] + [square_swap(fours[i], i) for i in range(1, 4)]
+
+    pieces, mirror, keep = tie((pieces, mirror, keep))
+    mirrors = [mirror] + [row_swap(mirror, x_mask(i)) for i in range(1, 4)]
+    prepped = [sds((DB, BLK, TOKENS), BF), sds((DB, TOKENS, BLK), BF)]
+    prep = call(prep_kernel, prepped, [VMEM] * 4, scratch=[pltpu.VMEM((TOKENS, 2 * DQ), BF)])
+    x0, y0 = prep(*pieces)
+    sums, mirrors, x0, y0 = tie((sums, mirrors, x0, y0))
+
     share = call(act_kernel, sds((32, 3 * HB), BF), [VMEM] * 4)(*sums)
-    mine = jnp.concatenate([share] + [square_swap(share, i) for i in range(1, 4)], axis=0)
+    mine = [share] + [square_swap(share, i) for i in range(1, 4)]
+    x2, y2 = prep(*tie((mirrors, share))[0])
+    x1, y1 = [row_swap(v, 1) for v in (x0, y0)]
+    mine, x1, y1, x2, y2 = tie((mine, x1, y1, x2, y2))
+    mine = jnp.concatenate(mine, axis=0)
     theirs = row_swap(mine, 1)
     outs = call(
         out_kernel,
@@ -231,34 +237,14 @@
         [SMEM] + [VMEM] * 5,
     )(place, mine, theirs, wg, wu, wd)
     full = outs[4]
-    far = outs[0]
-    for i in range(1, 4):
-        far = far + row_swap(outs[i], x_mask(i)).astype(F32)
-    last = far[:TG]
-    for i in range(1, 8):
-        last = last + row_swap(far[i * TG : (i + 1) * TG].astype(BF), deep_mask(i)).astype(F32)
-    last = last.astype(BF)
-
-    mirror = row_swap(near, 2)
-    mirrors = [mirror] + [row_swap(mirror, x_mask(i)) for i in range(1, 4)]
-    prepped = [sds((DB, BLK, TOKENS), BF), sds((DB, TOKENS, BLK), BF)]
-    prep = call(prep_kernel, prepped, [VMEM] * 4, scratch=[pltpu.VMEM((TOKENS, 2 * DQ), BF)])
-    x0, y0 = prep(*pieces)
-    x2, y2 = prep(*mirrors)
-    x1, y1, x3, y3 = [row_swap(v, 1) for v in (x0, y0, x2, y2)]
-
-    dest = lax.dynamic_slice_in_dim(block_dest[:, :, 0, :], group * QUARTERS, QUARTERS, axis=1)
-    index = lax.dynamic_slice_in_dim(all_index, group * QUARTERS, QUARTERS, axis=1)
-    swap = (jnp.arange(QUARTERS, dtype=jnp.int32) ^ quarter)[None, :, None]
-    value = (swap * 64 + index + 1).reshape(3, 1, QUARTERS * CAP)
-    targets = quarter * CAP + jnp.arange(CAP, dtype=jnp.int32)
-    hits = dest.reshape(3, 1, QUARTERS * CAP) == targets[None, :, None]
-    code = jnp.sum(jnp.where(hits, value, 0), axis=2, dtype=jnp.int32)
+    x3, y3 = [row_swap(v, 1) for v in tie((x2, y2, mine))[:2]]
+    far = [row_swap(outs[i], x_mask(i)) for i in range(1, 4)]
 
     grads = call(
         grad_kernel,
         sds((3, CAP, BLK, BLK), BF),
         [SMEM] + [VMEM] * 9,
+        out_specs=pl.BlockSpec((3, STEP, BLK, BLK), lambda i: (0, i, 0, 0)),
         scratch=[
             pltpu.VMEM((QUARTERS * DB, BLK, TOKENS), BF),
             pltpu.VMEM((QUARTERS * DB, TOKENS, BLK), BF),
@@ -266,7 +252,15 @@
             pltpu.VMEM((FB, TOKENS, BLK), BF),
             pltpu.VMEM((FB, TOKENS, BLK), BF),
         ],
+        grid=(CAP // STEP,),
+        limit=24,
     )(code, full, x0, x1, x2, x3, y0, y1, y2, y3)
+    far, grads = tie((far, grads))
+    total = outs[0] + far[0].astype(F32) + far[1].astype(F32) + far[2].astype(F32)
+    last = total[: 2 * TG]
+    for i in range(1, 4):
+        last = last + row_swap(total[i * 2 * TG : (i + 1) * 2 * TG].astype(BF), z_mask(i)).astype(F32)
+    last = (last[:TG] + row_swap(last[TG:].astype(BF), Y_MASK).astype(F32)).astype(BF)
     return last[:, :DQ], last[:, DQ:], grads.reshape(3, 1, 1, CAP, BLK, BLK)
 
 

time: 167 us -> 118 us (0.71)
  starting transfers between devices: 61 us -> 38.6 us
  Pallas kernels: 36.6 us -> 16.3 us
  local copies, waits for them, and re-layouts: 15.5 us -> 8.23 us
  waiting for transfers between devices: 48.1 us -> 51.1 us
  other arithmetic: 3.25 us -> 0.47 us
    ppermute x30 -> x24, starting transfers between devices: 53.8 us -> 31.4 us  [row_swap(): return lax.ppermute(value, 'row', [(i, i ^ mask) for i in range(128)])]
    pallas_call x3, Pallas kernels: 29.3 us -> 10.3 us  [the longest x1 6.18 us: body(): call(grad_kernel, sds((3, CAP, BLK, BLK), BF), [SMEM] + [VMEM] * 9, out_s...]
    ppermute x30 -> x24, waiting for transfers between devices: 26.6 us -> 43.2 us  [row_swap(): return lax.ppermute(value, 'row', [(i, i ^ mask) for i in range(128)])]
    ppermute x6, waiting for transfers between devices: 21.5 us -> 7.91 us  [square_swap(): lax.ppermute(value, ('row', 'col'), [(i, i ^ mask) for i in range(256)])]
    unnamed x35 -> x15, local copies, waits for them, and re-layouts: 10.9 us -> 5.06 us
    another operation x1, other arithmetic: 2.01 us -> 0.12 us
  transfers between devices with their start and end apart: 36 -> 30, of which waited for: 13 -> 19; matrix products, arithmetic and copies ran while one was open for 3% -> 2% of each run, Pallas kernels for 20% -> 12%
where the time goes in v2:
time: 118 us; the launch traced here: 115 us
  waiting for transfers between devices  51.1 us (43%)
  starting transfers between devices  38.6 us (33%)
  Pallas kernels  16.3 us (14%)
  local copies, waits for them, and re-layouts  8.23 us (7%)
    ppermute x24, waiting for transfers between devices, row_swap(): return lax.ppermute(value, 'row', [(i, i ^ mask) for i in range(128)])  43.2 us
    ppermute x24, starting transfers between devices, row_swap(): return lax.ppermute(value, 'row', [(i, i ^ mask) for i in range(128)])  31.4 us
    ppermute x6, waiting for transfers between devices, square_swap(): lax.ppermute(value, ('row', 'col'), [(i, i ^ mask) for i in range(256)])  7.91 us
    ppermute x6, starting transfers between devices, square_swap(): lax.ppermute(value, ('row', 'col'), [(i, i ^ mask) for i in range(256)])  7.15 us
    pallas_call x1, Pallas kernels, body(): call(grad_kernel, sds((3, CAP, BLK, BLK), BF), [SMEM] + [VMEM] * 9, out_s...  6.18 us
    unnamed x15, local copies, waits for them, and re-layouts  5.06 us
    pallas_call x1, Pallas kernels, body(): call(dense_kernel, wide, [SMEM] + [VMEM] * 3)  3.83 us
    pallas_call x1, Pallas kernels, body(): call(out_kernel, [sds((64, 2 * DQ), F32)] + [sds((64, 2 * DQ), BF)] * 3 +...  2.45 us
  transfers between devices with their start and end apart: 30, of which 19 were waited for; matrix products, arithmetic and copies ran while one was open for 2% of the time, Pallas kernels for 12%

profile of v2, /device:TPU:32, one launch (start us, length us, event | category | flops | bytes accessed | tf_op | source)
XLA Modules:
  0.0 115.5 jit_solution(2916889258299155329)
XLA Ops:
  2.1 3.2 %collective-permute-start = (bf16[8,2048]{1,0:T(8,128)(2,1)S(1)}, bf16[8,2048]{1,0:T(8,128)(2,1)S(1)}, u32[]{:S(2)}, u32[]{:S(2)}) collective-permute-start(bf16[8,2048]{1,0:T(8,128)(2,1)S(1)} %get-tuple-element.133), channel_id=1, source_target_pairs={{0,128},{2,130},{4,132},{6,134},{8,136},{10,138},{12,140},{14,142}... | collective-permute-start | bytes 98312 | tf_op jit(solution)/shard_map/ppermute | solution.py:29
  7.5 3.3 %collective-permute-start.1 = (bf16[16,2048]{1,0:T(8,128)(2,1)S(1)}, bf16[16,2048]{1,0:T(8,128)(2,1)S(1)}, u32[]{:S(2)}, u32[]{:S(2)}) collective-permute-start(bf16[16,2048]{1,0:T(8,128)(2,1)S(1)} %pad_maximum_fusion), channel_id=1, source_target_pairs={{0,8},{2,10},{4,12},{6,14},{8,0},{10,2},{12,4},{14,6},{16,24},{18,... | collective-permute-start | bytes 196616 | tf_op jit(solution)/shard_map/ppermute | solution.py:29
  10.8 4.5 %collective-permute-start.2 = (bf16[16,2048]{1,0:T(8,128)(2,1)S(1)}, bf16[16,2048]{1,0:T(8,128)(2,1)S(1)}, u32[]{:S(2)}, u32[]{:S(2)}) collective-permute-start(bf16[16,2048]{1,0:T(8,128)(2,1)S(1)} %pad_maximum_fusion), channel_id=1, source_target_pairs={{0,16},{2,18},{4,20},{6,22},{8,24},{10,26},{12,28},{14,30},{16,0},... | collective-permute-start | bytes 196616 | tf_op jit(solution)/shard_map/ppermute | solution.py:29
  15.3 4.9 %collective-permute-done.2 = bf16[16,2048]{1,0:T(8,128)(2,1)S(1)} collective-permute-done((bf16[16,2048]{1,0:T(8,128)(2,1)S(1)}, bf16[16,2048]{1,0:T(8,128)(2,1)S(1)}, u32[]{:S(2)}, u32[]{:S(2)}) %collective-permute-start.2) | collective-permute-done | bytes 65568 | tf_op jit(solution)/shard_map/ppermute | solution.py:29
  20.3 2.1 %collective-permute-done.3 = bf16[16,2048]{1,0:T(8,128)(2,1)S(1)} collective-permute-done((bf16[16,2048]{1,0:T(8,128)(2,1)S(1)}, bf16[16,2048]{1,0:T(8,128)(2,1)S(1)}, u32[]{:S(2)}, u32[]{:S(2)}) %collective-permute-start.3) | collective-permute-done | bytes 65568 | tf_op jit(solution)/shard_map/ppermute | solution.py:29
  23.9 2.7 %collective-permute-start.5 = (bf16[64,2048]{1,0:T(8,128)(2,1)S(1)}, bf16[64,2048]{1,0:T(8,128)(2,1)S(1)}, u32[]{:S(2)}, u32[]{:S(2)}) collective-permute-start(bf16[64,2048]{1,0:T(8,128)(2,1)S(1)} %constant_dynamic-update-slice_fusion.2.p0), channel_id=1, source_target_pairs={{0,64},{2,66},{4,68},{6,70},{8,72},{10,74},{12,76},{14,78},{16,80}... | collective-permute-start | bytes 786440 | tf_op jit(solution)/shard_map/ppermute | solution.py:29
  32.1 3.8 %shard_map.94 = (bf16[1024,896]{1,0:T(8,128)(2,1)S(1)}, bf16[1024,896]{1,0:T(8,128)(2,1)S(1)}, bf16[896,1024]{1,0:T(8,128)(2,1)S(1)}) custom-call(s32[3,48]{1,0:T(4,128)S(1)} %dynamic-slice_reduce_fusion.index_ref, bf16[48,128,128]{2,1,0:T(8,128)(2,1)S(1)} %bitcast.12, bf16[48,128,128]{2,1,0:T(8,128)(2,1)S(1)} %bitcast.13, bf16[48,128,128]{2,1,0:T(8,128)(2,1)S(1)} %bitcast.14), custom_call_target="tpu_custom_call" | custom-call | tf_op jit(solution)/shard_map/pallas_call | solution.py:197
  36.4 2.6 %collective-permute-done.6.p3 = bf16[64,2048]{1,0:T(8,128)(2,1)S(1)} collective-permute-done((bf16[64,2048]{1,0:T(8,128)(2,1)S(1)}, bf16[64,2048]{1,0:T(8,128)(2,1)S(1)}, u32[]{:S(2)}, u32[]{:S(2)}) %collective-permute-start.6) | collective-permute-done | bytes 262176 | tf_op jit(solution)/shard_map/ppermute | solution.py:29
  39.0 2.4 %shard_map.95 = (f32[128,2688]{1,0:T(8,128)S(1)}, f32[128,2688]{1,0:T(8,128)S(1)}) custom-call(s32[2]{0:T(128)S(1)} %pad_add_fusion.place_ref, bf16[64,2048]{1,0:T(8,128)(2,1)S(1)} %constant_dynamic-update-slice_fusion.2.p0, bf16[64,2048]{1,0:T(8,128)(2,1)S(1)} %collective-permute-done.4.p1, bf16[64,2048]{1,0:T(8,128)(2,1)S(1)} %collective-permute-done.5.p2, ...), custom_call_target="tpu_custom_call" | custom-call | tf_op jit(solution)/shard_map/pallas_call | solution.py:213
  41.6 3.0 %collective-permute-done.8.got_ref = f32[128,2688]{1,0:T(8,128)S(1)} collective-permute-done((f32[128,2688]{1,0:T(8,128)S(1)}, f32[128,2688]{1,0:T(8,128)S(1)}, u32[]{:S(2)}, u32[]{:S(2)}) %collective-permute-start.8) | collective-permute-done | bytes 1376288 | tf_op jit(solution)/shard_map/ppermute | solution.py:29
  45.3 1.7 %collective-permute-start.9 = (f32[32,2688]{1,0:T(8,128)S(1)}, f32[32,2688]{1,0:T(8,128)S(1)}, u32[]{:S(2)}, u32[]{:S(2)}) collective-permute-start(f32[32,2688]{1,0:T(8,128)S(1)} %get-tuple-element.70), channel_id=1, source_target_pairs={{0,1},{1,0},{2,3},{3,2},{4,5},{5,4},{6,7},{7,6},{8,9},{9,8},{10,11... | collective-permute-start | bytes 1032200 | tf_op jit(solution)/shard_map/ppermute | solution.py:34
  47.0 1.9 %collective-permute-start.11 = (f32[32,2688]{1,0:T(8,128)S(1)}, f32[32,2688]{1,0:T(8,128)S(1)}, u32[]{:S(2)}, u32[]{:S(2)}) collective-permute-start(f32[32,2688]{1,0:T(8,128)S(1)} %get-tuple-element.72), channel_id=1, source_target_pairs={{0,5},{1,4},{2,7},{3,6},{4,1},{5,0},{6,3},{7,2},{8,13},{9,12},{10,... | collective-permute-start | bytes 1032200 | tf_op jit(solution)/shard_map/ppermute | solution.py:34
  51.0 7.0 %collective-permute-done.13.p2 = bf16[64,2048]{1,0:T(8,128)(2,1)S(1)} collective-permute-done((bf16[64,2048]{1,0:T(8,128)(2,1)S(1)}, bf16[64,2048]{1,0:T(8,128)(2,1)S(1)}, u32[]{:S(2)}, u32[]{:S(2)}) %collective-permute-start.13) | collective-permute-done | bytes 262176 | tf_op jit(solution)/shard_map/ppermute | solution.py:29
  58.0 5.5 %collective-permute-done.14.p3 = bf16[64,2048]{1,0:T(8,128)(2,1)S(1)} collective-permute-done((bf16[64,2048]{1,0:T(8,128)(2,1)S(1)}, bf16[64,2048]{1,0:T(8,128)(2,1)S(1)}, u32[]{:S(2)}, u32[]{:S(2)}) %collective-permute-start.14) | collective-permute-done | bytes 262176 | tf_op jit(solution)/shard_map/ppermute | solution.py:29
  64.7 1.7 %collective-permute-start.15 = (bf16[32,2688]{1,0:T(8,128)(2,1)S(1)}, bf16[32,2688]{1,0:T(8,128)(2,1)S(1)}, u32[]{:S(2)}, u32[]{:S(2)}) collective-permute-start(bf16[32,2688]{1,0:T(8,128)(2,1)S(1)} %shard_map.98), channel_id=1, source_target_pairs={{0,1},{1,0},{2,3},{3,2},{4,5},{5,4},{6,7},{7,6},{8,9},{9,8},{10,11... | collective-permute-start | bytes 516104 | tf_op jit(solution)/shard_map/ppermute | solution.py:34
  66.7 1.6 %collective-permute-start.17 = (bf16[32,2688]{1,0:T(8,128)(2,1)S(1)}, bf16[32,2688]{1,0:T(8,128)(2,1)S(1)}, u32[]{:S(2)}, u32[]{:S(2)}) collective-permute-start(bf16[32,2688]{1,0:T(8,128)(2,1)S(1)} %shard_map.98), channel_id=1, source_target_pairs={{0,5},{1,4},{2,7},{3,6},{4,1},{5,0},{6,3},{7,2},{8,13},{9,12},{10,... | collective-permute-start | bytes 516104 | tf_op jit(solution)/shard_map/ppermute | solution.py:34
  68.6 2.6 %collective-permute-done.15 = bf16[32,2688]{1,0:T(8,128)(2,1)S(1)} collective-permute-done((bf16[32,2688]{1,0:T(8,128)(2,1)S(1)}, bf16[32,2688]{1,0:T(8,128)(2,1)S(1)}, u32[]{:S(2)}, u32[]{:S(2)}) %collective-permute-start.15) | collective-permute-done | bytes 172064 | tf_op jit(solution)/shard_map/ppermute | solution.py:34
  71.2 2.5 %collective-permute-done.16 = bf16[32,2688]{1,0:T(8,128)(2,1)S(1)} collective-permute-done((bf16[32,2688]{1,0:T(8,128)(2,1)S(1)}, bf16[32,2688]{1,0:T(8,128)(2,1)S(1)}, u32[]{:S(2)}, u32[]{:S(2)}) %collective-permute-start.16) | collective-permute-done | bytes 172064 | tf_op jit(solution)/shard_map/ppermute | solution.py:34
  73.7 2.3 %collective-permute-done.17 = bf16[32,2688]{1,0:T(8,128)(2,1)S(1)} collective-permute-done((bf16[32,2688]{1,0:T(8,128)(2,1)S(1)}, bf16[32,2688]{1,0:T(8,128)(2,1)S(1)}, u32[]{:S(2)}, u32[]{:S(2)}) %collective-permute-start.17) | collective-permute-done | bytes 172064 | tf_op jit(solution)/shard_map/ppermute | solution.py:34
  76.8 1.5 %collective-permute-done.20.theirs = bf16[128,2688]{1,0:T(8,128)(2,1)S(1)} collective-permute-done((bf16[128,2688]{1,0:T(8,128)(2,1)S(1)}, bf16[128,2688]{1,0:T(8,128)(2,1)S(1)}, u32[]{:S(2)}, u32[]{:S(2)}) %collective-permute-start.20) | collective-permute-done | bytes 688160 | tf_op jit(solution)/shard_map/ppermute | solution.py:29
  78.3 2.5 %shard_map.100 = (f32[64,2048]{1,0:T(8,128)S(1)}, bf16[64,2048]{1,0:T(8,128)(2,1)S(1)}, bf16[64,2048]{1,0:T(8,128)(2,1)S(1)}, bf16[64,2048]{1,0:T(8,128)(2,1)S(1)}, bf16[256,2688]{1,0:T(8,128)(2,1)S(1)}) custom-call(s32[2]{0:T(128)S(1)} %pad_add_fusion.place_ref, bf16[128,2688]{1,0:T(8,128)(2,1)S(1)} %constant_dynamic-update-slice_fusion.8.mine, ...), custom_call_target="tpu_custom_call" | custom-call | tf_op jit(solution)/shard_map/pallas_call | solution.py:234
  80.9 1.9 %collective-permute-start.22 = (bf16[64,2048]{1,0:T(8,128)(2,1)S(1)}, bf16[64,2048]{1,0:T(8,128)(2,1)S(1)}, u32[]{:S(2)}, u32[]{:S(2)}) collective-permute-start(bf16[64,2048]{1,0:T(8,128)(2,1)S(1)} %get-tuple-element.103), channel_id=1, source_target_pairs={{0,64},{2,66},{4,68},{6,70},{8,72},{10,74},{12,76},{14,78},{16,80}... | collective-permute-start | bytes 786440 | tf_op jit(solution)/shard_map/ppermute | solution.py:29
  82.8 2.8 %collective-permute-start.23 = (bf16[64,2048]{1,0:T(8,128)(2,1)S(1)}, bf16[64,2048]{1,0:T(8,128)(2,1)S(1)}, u32[]{:S(2)}, u32[]{:S(2)}) collective-permute-start(bf16[64,2048]{1,0:T(8,128)(2,1)S(1)} %get-tuple-element.104), channel_id=1, source_target_pairs={{0,96},{2,98},{4,100},{6,102},{8,104},{10,106},{12,108},{14,110},{... | collective-permute-start | bytes 786440 | tf_op jit(solution)/shard_map/ppermute | solution.py:29
  85.5 6.2 %shard_map.101 = bf16[3,48,128,128]{3,2,1,0:T(8,128)(2,1)} custom-call(s32[3,48]{1,0:T(4,128)S(1)} %select_reduce_fusion.code_ref, bf16[256,2688]{1,0:T(8,128)(2,1)S(1)} %get-tuple-element.106.full_ref, bf16[8,128,256]{2,1,0:T(8,128)(2,1)S(1)} %get-tuple-element.85.x0, bf16[8,128,256]{2,1,0:T(8,128)(2,1)S(1)} %collective-permute-done.18.x1, ...), custom_call_target="tpu_custom_call" | custom-call | tf_op jit(solution)/shard_map/pallas_call | solution.py:243
  91.7 3.1 %collective-permute-done.22 = bf16[64,2048]{1,0:T(8,128)(2,1)S(1)} collective-permute-done((bf16[64,2048]{1,0:T(8,128)(2,1)S(1)}, bf16[64,2048]{1,0:T(8,128)(2,1)S(1)}, u32[]{:S(2)}, u32[]{:S(2)}) %collective-permute-start.22) | collective-permute-done | bytes 262176 | tf_op jit(solution)/shard_map/ppermute | solution.py:29
  94.8 2.6 %collective-permute-done.23 = bf16[64,2048]{1,0:T(8,128)(2,1)S(1)} collective-permute-done((bf16[64,2048]{1,0:T(8,128)(2,1)S(1)}, bf16[64,2048]{1,0:T(8,128)(2,1)S(1)}, u32[]{:S(2)}, u32[]{:S(2)}) %collective-permute-start.23) | collective-permute-done | bytes 262176 | tf_op jit(solution)/shard_map/ppermute | solution.py:29
  97.6 2.7 %collective-permute-start.28 = (bf16[16,2048]{1,0:T(8,128)(2,1)S(1)}, bf16[16,2048]{1,0:T(8,128)(2,1)S(1)}, u32[]{:S(2)}, u32[]{:S(2)}) collective-permute-start(bf16[16,2048]{1,0:T(8,128)(2,1)S(1)} %get-tuple-element.129), channel_id=1, source_target_pairs={{0,24},{2,26},{4,28},{6,30},{8,16},{10,18},{12,20},{14,22},{16,8},... | collective-permute-start | bytes 196616 | tf_op jit(solution)/shard_map/ppermute | solution.py:29
  100.3 2.1 %collective-permute-start.27 = (bf16[16,2048]{1,0:T(8,128)(2,1)S(1)}, bf16[16,2048]{1,0:T(8,128)(2,1)S(1)}, u32[]{:S(2)}, u32[]{:S(2)}) collective-permute-start(bf16[16,2048]{1,0:T(8,128)(2,1)S(1)} %get-tuple-element.130), channel_id=1, source_target_pairs={{0,16},{2,18},{4,20},{6,22},{8,24},{10,26},{12,28},{14,30},{16,0},... | collective-permute-start | bytes 196616 | tf_op jit(solution)/shard_map/ppermute | solution.py:29
  102.4 1.8 %collective-permute-start.26 = (bf16[16,2048]{1,0:T(8,128)(2,1)S(1)}, bf16[16,2048]{1,0:T(8,128)(2,1)S(1)}, u32[]{:S(2)}, u32[]{:S(2)}) collective-permute-start(bf16[16,2048]{1,0:T(8,128)(2,1)S(1)} %get-tuple-element.128), channel_id=1, source_target_pairs={{0,8},{2,10},{4,12},{6,14},{8,0},{10,2},{12,4},{14,6},{16,24},{18,... | collective-permute-start | bytes 196616 | tf_op jit(solution)/shard_map/ppermute | solution.py:29
  104.8 4.4 %collective-permute-done.27 = bf16[16,2048]{1,0:T(8,128)(2,1)S(1)} collective-permute-done((bf16[16,2048]{1,0:T(8,128)(2,1)S(1)}, bf16[16,2048]{1,0:T(8,128)(2,1)S(1)}, u32[]{:S(2)}, u32[]{:S(2)}) %collective-permute-start.27) | collective-permute-done | bytes 65568 | tf_op jit(solution)/shard_map/ppermute | solution.py:29
  109.3 2.2 %collective-permute-start.29 = (bf16[8,2048]{1,0:T(8,128)(2,1)S(1)}, bf16[8,2048]{1,0:T(8,128)(2,1)S(1)}, u32[]{:S(2)}, u32[]{:S(2)}) collective-permute-start(bf16[8,2048]{1,0:T(8,128)(2,1)S(1)} %slice.53), channel_id=1, source_target_pairs={{0,128},{2,130},{4,132},{6,134},{8,136},{10,138},{12,140},{14,142}... | collective-permute-start | bytes 98312 | tf_op jit(solution)/shard_map/ppermute | solution.py:29
  111.5 3.3 %collective-permute-done.29 = bf16[8,2048]{1,0:T(8,128)(2,1)S(1)} collective-permute-done((bf16[8,2048]{1,0:T(8,128)(2,1)S(1)}, bf16[8,2048]{1,0:T(8,128)(2,1)S(1)}, u32[]{:S(2)}, u32[]{:S(2)}) %collective-permute-start.29) | collective-permute-done | bytes 32800 | tf_op jit(solution)/shard_map/ppermute | solution.py:29
  (75 shorter events, 18.2 us)
Async XLA Ops:
  0.6 4.7 %copy-start = (s32[3,128,2,48]{1,3,2,0:T(8,128)S(1)}, s32[3,128,2,48]{1,3,2,0:T(8,128)}, u32[]{:S(2)}) copy-start(s32[3,128,2,48]{1,3,2,0:T(8,128)} %param.12) | copy-start | bytes 442372
  2.1 5.4 %collective-permute-start = (bf16[8,2048]{1,0:T(8,128)(2,1)S(1)}, bf16[8,2048]{1,0:T(8,128)(2,1)S(1)}, u32[]{:S(2)}, u32[]{:S(2)}) collective-permute-start(bf16[8,2048]{1,0:T(8,128)(2,1)S(1)} %get-tuple-element.133), channel_id=1, source_target_pairs={{0,128},{2,130},{4,132},{6,134},{8,136},{10,138},{12,140},{14,142}... | collective-permute-start | bytes 98312 | tf_op jit(solution)/shard_map/ppermute | solution.py:29
  7.5 7.8 %collective-permute-start.1 = (bf16[16,2048]{1,0:T(8,128)(2,1)S(1)}, bf16[16,2048]{1,0:T(8,128)(2,1)S(1)}, u32[]{:S(2)}, u32[]{:S(2)}) collective-permute-start(bf16[16,2048]{1,0:T(8,128)(2,1)S(1)} %pad_maximum_fusion), channel_id=1, source_target_pairs={{0,8},{2,10},{4,12},{6,14},{8,0},{10,2},{12,4},{14,6},{16,24},{18,... | collective-permute-start | bytes 196616 | tf_op jit(solution)/shard_map/ppermute | solution.py:29
  10.8 9.4 %collective-permute-start.2 = (bf16[16,2048]{1,0:T(8,128)(2,1)S(1)}, bf16[16,2048]{1,0:T(8,128)(2,1)S(1)}, u32[]{:S(2)}, u32[]{:S(2)}) collective-permute-start(bf16[16,2048]{1,0:T(8,128)(2,1)S(1)} %pad_maximum_fusion), channel_id=1, source_target_pairs={{0,16},{2,18},{4,20},{6,22},{8,24},{10,26},{12,28},{14,30},{16,0},... | collective-permute-start | bytes 196616 | tf_op jit(solution)/shard_map/ppermute | solution.py:29
  15.3 7.1 %collective-permute-start.3 = (bf16[16,2048]{1,0:T(8,128)(2,1)S(1)}, bf16[16,2048]{1,0:T(8,128)(2,1)S(1)}, u32[]{:S(2)}, u32[]{:S(2)}) collective-permute-start(bf16[16,2048]{1,0:T(8,128)(2,1)S(1)} %pad_maximum_fusion), channel_id=1, source_target_pairs={{0,24},{2,26},{4,28},{6,30},{8,16},{10,18},{12,20},{14,22},{16,8},... | collective-permute-start | bytes 196616 | tf_op jit(solution)/shard_map/ppermute | solution.py:29
  22.4 13.9 %collective-permute-start.4 = (bf16[64,2048]{1,0:T(8,128)(2,1)S(1)}, bf16[64,2048]{1,0:T(8,128)(2,1)S(1)}, u32[]{:S(2)}, u32[]{:S(2)}) collective-permute-start(bf16[64,2048]{1,0:T(8,128)(2,1)S(1)} %constant_dynamic-update-slice_fusion.2.p0), channel_id=1, source_target_pairs={{0,32},{2,34},{4,36},{6,38},{8,40},{10,42},{12,44},{14,46},{16,48}... | collective-permute-start | bytes 786440 | tf_op jit(solution)/shard_map/ppermute | solution.py:29
  23.9 12.5 %collective-permute-start.5 = (bf16[64,2048]{1,0:T(8,128)(2,1)S(1)}, bf16[64,2048]{1,0:T(8,128)(2,1)S(1)}, u32[]{:S(2)}, u32[]{:S(2)}) collective-permute-start(bf16[64,2048]{1,0:T(8,128)(2,1)S(1)} %constant_dynamic-update-slice_fusion.2.p0), channel_id=1, source_target_pairs={{0,64},{2,66},{4,68},{6,70},{8,72},{10,74},{12,76},{14,78},{16,80}... | collective-permute-start | bytes 786440 | tf_op jit(solution)/shard_map/ppermute | solution.py:29
  26.6 12.4 %collective-permute-start.6 = (bf16[64,2048]{1,0:T(8,128)(2,1)S(1)}, bf16[64,2048]{1,0:T(8,128)(2,1)S(1)}, u32[]{:S(2)}, u32[]{:S(2)}) collective-permute-start(bf16[64,2048]{1,0:T(8,128)(2,1)S(1)} %constant_dynamic-update-slice_fusion.2.p0), channel_id=1, source_target_pairs={{0,96},{2,98},{4,100},{6,102},{8,104},{10,106},{12,108},{14,110},{... | collective-permute-start | bytes 786440 | tf_op jit(solution)/shard_map/ppermute | solution.py:29
  27.1 11.9 %collective-permute-start.7 = (bf16[64,2048]{1,0:T(8,128)(2,1)S(1)}, bf16[64,2048]{1,0:T(8,128)(2,1)S(1)}, u32[]{:S(2)}, u32[]{:S(2)}) collective-permute-start(bf16[64,2048]{1,0:T(8,128)(2,1)S(1)} %constant_dynamic-update-slice_fusion.2.p0), channel_id=1, source_target_pairs={{0,4},{2,6},{4,0},{6,2},{8,12},{10,14},{12,8},{14,10},{16,20},{18,... | collective-permute-start | bytes 786440 | tf_op jit(solution)/shard_map/ppermute | solution.py:29
  27.9 1.4 %copy-start.1 = (bf16[1,1,48,128,128]{4,3,2,1,0:T(8,128)(2,1)S(1)}, bf16[1,1,48,128,128]{4,3,2,1,0:T(8,128)(2,1)}, u32[]{:S(2)}) copy-start(bf16[1,1,48,128,128]{4,3,2,1,0:T(8,128)(2,1)} %param.9) | copy-start | bytes 4718596
  41.4 3.2 %collective-permute-start.8 = (f32[128,2688]{1,0:T(8,128)S(1)}, f32[128,2688]{1,0:T(8,128)S(1)}, u32[]{:S(2)}, u32[]{:S(2)}) collective-permute-start(f32[128,2688]{1,0:T(8,128)S(1)} %get-tuple-element.68), channel_id=1, source_target_pairs={{0,2},{2,0},{4,6},{6,4},{8,10},{10,8},{12,14},{14,12},{16,18},{18,... | collective-permute-start | bytes 4128776 | tf_op jit(solution)/shard_map/ppermute | solution.py:29
  41.5 8.8 %collective-permute-start.12 = (bf16[64,2048]{1,0:T(8,128)(2,1)S(1)}, bf16[64,2048]{1,0:T(8,128)(2,1)S(1)}, u32[]{:S(2)}, u32[]{:S(2)}) collective-permute-start(bf16[64,2048]{1,0:T(8,128)(2,1)S(1)} %collective-permute-done.7.p0), channel_id=1, source_target_pairs={{0,32},{2,34},{4,36},{6,38},{8,40},{10,42},{12,44},{14,46},{16,48}... | collective-permute-start | bytes 786440 | tf_op jit(solution)/shard_map/ppermute | solution.py:29
  45.3 18.2 %collective-permute-start.9 = (f32[32,2688]{1,0:T(8,128)S(1)}, f32[32,2688]{1,0:T(8,128)S(1)}, u32[]{:S(2)}, u32[]{:S(2)}) collective-permute-start(f32[32,2688]{1,0:T(8,128)S(1)} %get-tuple-element.70), channel_id=1, source_target_pairs={{0,1},{1,0},{2,3},{3,2},{4,5},{5,4},{6,7},{7,6},{8,9},{9,8},{10,11... | collective-permute-start | bytes 1032200 | tf_op jit(solution)/shard_map/ppermute | solution.py:34
  47.0 16.5 %collective-permute-start.10 = (f32[32,2688]{1,0:T(8,128)S(1)}, f32[32,2688]{1,0:T(8,128)S(1)}, u32[]{:S(2)}, u32[]{:S(2)}) collective-permute-start(f32[32,2688]{1,0:T(8,128)S(1)} %get-tuple-element.71), channel_id=1, source_target_pairs={{0,4},{1,5},{2,6},{3,7},{4,0},{5,1},{6,2},{7,3},{8,12},{9,13},{10,... | collective-permute-start | bytes 1032200 | tf_op jit(solution)/shard_map/ppermute | solution.py:34
  47.0 17.1 %collective-permute-start.11 = (f32[32,2688]{1,0:T(8,128)S(1)}, f32[32,2688]{1,0:T(8,128)S(1)}, u32[]{:S(2)}, u32[]{:S(2)}) collective-permute-start(f32[32,2688]{1,0:T(8,128)S(1)} %get-tuple-element.72), channel_id=1, source_target_pairs={{0,5},{1,4},{2,7},{3,6},{4,1},{5,0},{6,3},{7,2},{8,13},{9,12},{10,... | collective-permute-start | bytes 1032200 | tf_op jit(solution)/shard_map/ppermute | solution.py:34
  48.9 9.1 %collective-permute-start.13 = (bf16[64,2048]{1,0:T(8,128)(2,1)S(1)}, bf16[64,2048]{1,0:T(8,128)(2,1)S(1)}, u32[]{:S(2)}, u32[]{:S(2)}) collective-permute-start(bf16[64,2048]{1,0:T(8,128)(2,1)S(1)} %collective-permute-done.7.p0), channel_id=1, source_target_pairs={{0,64},{2,66},{4,68},{6,70},{8,72},{10,74},{12,76},{14,78},{16,80}... | collective-permute-start | bytes 786440 | tf_op jit(solution)/shard_map/ppermute | solution.py:29
  50.3 13.2 %collective-permute-start.14 = (bf16[64,2048]{1,0:T(8,128)(2,1)S(1)}, bf16[64,2048]{1,0:T(8,128)(2,1)S(1)}, u32[]{:S(2)}, u32[]{:S(2)}) collective-permute-start(bf16[64,2048]{1,0:T(8,128)(2,1)S(1)} %collective-permute-done.7.p0), channel_id=1, source_target_pairs={{0,96},{2,98},{4,100},{6,102},{8,104},{10,106},{12,108},{14,110},{... | collective-permute-start | bytes 786440 | tf_op jit(solution)/shard_map/ppermute | solution.py:29
  64.1 11.9 %collective-permute-start.18 = (bf16[8,128,256]{2,1,0:T(8,128)(2,1)S(1)}, bf16[8,128,256]{2,1,0:T(8,128)(2,1)S(1)}, u32[]{:S(2)}, u32[]{:S(2)}) collective-permute-start(bf16[8,128,256]{2,1,0:T(8,128)(2,1)S(1)} %get-tuple-element.85.x0), channel_id=1, source_target_pairs={{0,2},{2,0},{4,6},{6,4},{8,10},{10,8},{12,14},{14,12},{16,18},{18,... | collective-permute-start | bytes 1572872 | tf_op jit(solution)/shard_map/ppermute | solution.py:29
  64.1 11.9 %collective-permute-start.19 = (bf16[8,256,128]{2,1,0:T(8,128)(2,1)S(1)}, bf16[8,256,128]{2,1,0:T(8,128)(2,1)S(1)}, u32[]{:S(2)}, u32[]{:S(2)}) collective-permute-start(bf16[8,256,128]{2,1,0:T(8,128)(2,1)S(1)} %get-tuple-element.86.y0), channel_id=1, source_target_pairs={{0,2},{2,0},{4,6},{6,4},{8,10},{10,8},{12,14},{14,12},{16,18},{18,... | collective-permute-start | bytes 1572872 | tf_op jit(solution)/shard_map/ppermute | solution.py:29
  64.7 6.5 %collective-permute-start.15 = (bf16[32,2688]{1,0:T(8,128)(2,1)S(1)}, bf16[32,2688]{1,0:T(8,128)(2,1)S(1)}, u32[]{:S(2)}, u32[]{:S(2)}) collective-permute-start(bf16[32,2688]{1,0:T(8,128)(2,1)S(1)} %shard_map.98), channel_id=1, source_target_pairs={{0,1},{1,0},{2,3},{3,2},{4,5},{5,4},{6,7},{7,6},{8,9},{9,8},{10,11... | collective-permute-start | bytes 516104 | tf_op jit(solution)/shard_map/ppermute | solution.py:34
  66.4 7.3 %collective-permute-start.16 = (bf16[32,2688]{1,0:T(8,128)(2,1)S(1)}, bf16[32,2688]{1,0:T(8,128)(2,1)S(1)}, u32[]{:S(2)}, u32[]{:S(2)}) collective-permute-start(bf16[32,2688]{1,0:T(8,128)(2,1)S(1)} %shard_map.98), channel_id=1, source_target_pairs={{0,4},{1,5},{2,6},{3,7},{4,0},{5,1},{6,2},{7,3},{8,12},{9,13},{10,... | collective-permute-start | bytes 516104 | tf_op jit(solution)/shard_map/ppermute | solution.py:34
  66.7 9.3 %collective-permute-start.17 = (bf16[32,2688]{1,0:T(8,128)(2,1)S(1)}, bf16[32,2688]{1,0:T(8,128)(2,1)S(1)}, u32[]{:S(2)}, u32[]{:S(2)}) collective-permute-start(bf16[32,2688]{1,0:T(8,128)(2,1)S(1)} %shard_map.98), channel_id=1, source_target_pairs={{0,5},{1,4},{2,7},{3,6},{4,1},{5,0},{6,3},{7,2},{8,13},{9,12},{10,... | collective-permute-start | bytes 516104 | tf_op jit(solution)/shard_map/ppermute | solution.py:34
  76.1 2.2 %collective-permute-start.20 = (bf16[128,2688]{1,0:T(8,128)(2,1)S(1)}, bf16[128,2688]{1,0:T(8,128)(2,1)S(1)}, u32[]{:S(2)}, u32[]{:S(2)}) collective-permute-start(bf16[128,2688]{1,0:T(8,128)(2,1)S(1)} %constant_dynamic-update-slice_fusion.8.mine), channel_id=1, source_target_pairs={{0,2},{2,0},{4,6},{6,4},{8,10},{10,8},{12,14},{14,12},{16,18},{18,... | collective-permute-start | bytes 2064392 | tf_op jit(solution)/shard_map/ppermute | solution.py:29
  76.2 9.4 %collective-permute-start.24 = (bf16[8,128,256]{2,1,0:T(8,128)(2,1)S(1)}, bf16[8,128,256]{2,1,0:T(8,128)(2,1)S(1)}, u32[]{:S(2)}, u32[]{:S(2)}) collective-permute-start(bf16[8,128,256]{2,1,0:T(8,128)(2,1)S(1)} %get-tuple-element.110.x2), channel_id=1, source_target_pairs={{0,2},{2,0},{4,6},{6,4},{8,10},{10,8},{12,14},{14,12},{16,18},{18,... | collective-permute-start | bytes 1572872 | tf_op jit(solution)/shard_map/ppermute | solution.py:29
  76.7 8.9 %collective-permute-start.25 = (bf16[8,256,128]{2,1,0:T(8,128)(2,1)S(1)}, bf16[8,256,128]{2,1,0:T(8,128)(2,1)S(1)}, u32[]{:S(2)}, u32[]{:S(2)}) collective-permute-start(bf16[8,256,128]{2,1,0:T(8,128)(2,1)S(1)} %get-tuple-element.112.y2), channel_id=1, source_target_pairs={{0,2},{2,0},{4,6},{6,4},{8,10},{10,8},{12,14},{14,12},{16,18},{18,... | collective-permute-start | bytes 1572872 | tf_op jit(solution)/shard_map/ppermute | solution.py:29
  80.8 11.0 %collective-permute-start.21 = (bf16[64,2048]{1,0:T(8,128)(2,1)S(1)}, bf16[64,2048]{1,0:T(8,128)(2,1)S(1)}, u32[]{:S(2)}, u32[]{:S(2)}) collective-permute-start(bf16[64,2048]{1,0:T(8,128)(2,1)S(1)} %get-tuple-element.102), channel_id=1, source_target_pairs={{0,32},{2,34},{4,36},{6,38},{8,40},{10,42},{12,44},{14,46},{16,48}... | collective-permute-start | bytes 786440 | tf_op jit(solution)/shard_map/ppermute | solution.py:29
  80.9 14.0 %collective-permute-start.22 = (bf16[64,2048]{1,0:T(8,128)(2,1)S(1)}, bf16[64,2048]{1,0:T(8,128)(2,1)S(1)}, u32[]{:S(2)}, u32[]{:S(2)}) collective-permute-start(bf16[64,2048]{1,0:T(8,128)(2,1)S(1)} %get-tuple-element.103), channel_id=1, source_target_pairs={{0,64},{2,66},{4,68},{6,70},{8,72},{10,74},{12,76},{14,78},{16,80}... | collective-permute-start | bytes 786440 | tf_op jit(solution)/shard_map/ppermute | solution.py:29
  82.8 14.6 %collective-permute-start.23 = (bf16[64,2048]{1,0:T(8,128)(2,1)S(1)}, bf16[64,2048]{1,0:T(8,128)(2,1)S(1)}, u32[]{:S(2)}, u32[]{:S(2)}) collective-permute-start(bf16[64,2048]{1,0:T(8,128)(2,1)S(1)} %get-tuple-element.104), channel_id=1, source_target_pairs={{0,96},{2,98},{4,100},{6,102},{8,104},{10,106},{12,108},{14,110},{... | collective-permute-start | bytes 786440 | tf_op jit(solution)/shard_map/ppermute | solution.py:29
  97.6 7.3 %collective-permute-start.28 = (bf16[16,2048]{1,0:T(8,128)(2,1)S(1)}, bf16[16,2048]{1,0:T(8,128)(2,1)S(1)}, u32[]{:S(2)}, u32[]{:S(2)}) collective-permute-start(bf16[16,2048]{1,0:T(8,128)(2,1)S(1)} %get-tuple-element.129), channel_id=1, source_target_pairs={{0,24},{2,26},{4,28},{6,30},{8,16},{10,18},{12,20},{14,22},{16,8},... | collective-permute-start | bytes 196616 | tf_op jit(solution)/shard_map/ppermute | solution.py:29
  100.3 9.0 %collective-permute-start.27 = (bf16[16,2048]{1,0:T(8,128)(2,1)S(1)}, bf16[16,2048]{1,0:T(8,128)(2,1)S(1)}, u32[]{:S(2)}, u32[]{:S(2)}) collective-permute-start(bf16[16,2048]{1,0:T(8,128)(2,1)S(1)} %get-tuple-element.130), channel_id=1, source_target_pairs={{0,16},{2,18},{4,20},{6,22},{8,24},{10,26},{12,28},{14,30},{16,0},... | collective-permute-start | bytes 196616 | tf_op jit(solution)/shard_map/ppermute | solution.py:29
  102.4 6.9 %collective-permute-start.26 = (bf16[16,2048]{1,0:T(8,128)(2,1)S(1)}, bf16[16,2048]{1,0:T(8,128)(2,1)S(1)}, u32[]{:S(2)}, u32[]{:S(2)}) collective-permute-start(bf16[16,2048]{1,0:T(8,128)(2,1)S(1)} %get-tuple-element.128), channel_id=1, source_target_pairs={{0,8},{2,10},{4,12},{6,14},{8,0},{10,2},{12,4},{14,6},{16,24},{18,... | collective-permute-start | bytes 196616 | tf_op jit(solution)/shard_map/ppermute | solution.py:29
  109.3 5.5 %collective-permute-start.29 = (bf16[8,2048]{1,0:T(8,128)(2,1)S(1)}, bf16[8,2048]{1,0:T(8,128)(2,1)S(1)}, u32[]{:S(2)}, u32[]{:S(2)}) collective-permute-start(bf16[8,2048]{1,0:T(8,128)(2,1)S(1)} %slice.53), channel_id=1, source_target_pairs={{0,128},{2,130},{4,132},{6,134},{8,136},{10,138},{12,140},{14,142}... | collective-permute-start | bytes 98312 | tf_op jit(solution)/shard_map/ppermute | solution.py:29
  (2 other events, 2.8 us)

commit v3 on v2

--- a/solution.py
+++ b/solution.py
@@ -85,37 +85,55 @@
     lax.fori_loop(0, CAP, one, 0)
 
 
-def partial_kernel(place_ref, p0, p1, p2, p3, wg_ref, wu_ref, wd_ref, keep_ref, send_ref, rows):
-    core = place_ref[0]
-    first = pl.multiple_of(core * 128, 128)
-    second = pl.multiple_of((1 - core) * 128, 128)
-    rows[pl.ds(first, 64), :] = p0[...]
-    rows[pl.ds(first + 64, 64), :] = p1[...]
-    rows[pl.ds(second, 64), :] = p2[...]
-    rows[pl.ds(second + 64, 64), :] = p3[...]
+def partial_kernel(place_ref, p0, p1, p2, p3, wg_ref, wu_ref, wd_ref, out_ref, rows, *, other):
+    swap = place_ref[0] != other
+
+    @pl.when(swap)
+    def _():
+        rows[:64, :] = p2[...]
+        rows[64:, :] = p3[...]
+
+    @pl.when(jnp.logical_not(swap))
+    def _():
+        rows[:64, :] = p0[...]
+        rows[64:, :] = p1[...]
+
     x = rows[:, :DQ]
     dy = rows[:, DQ:]
-    for at, value in (
-        (0, lambda: jnp.dot(x, wg_ref[...], preferred_element_type=F32)),
-        (1, lambda: jnp.dot(x, wu_ref[...], preferred_element_type=F32)),
-        (2, lambda: lax.dot_general(dy, wd_ref[...], NT, preferred_element_type=F32)),
-    ):
-        part = value()
-        keep_ref[:, at * HB : (at + 1) * HB] = part[:128]
-        send_ref[:, at * HB : (at + 1) * HB] = part[128:]
+    out_ref[:, :HB] = jnp.dot(x, wg_ref[...], preferred_element_type=F32)
+    out_ref[:, HB : 2 * HB] = jnp.dot(x, wu_ref[...], preferred_element_type=F32)
+    out_ref[:, 2 * HB :] = lax.dot_general(dy, wd_ref[...], NT, preferred_element_type=F32)
 
 
 def pair_kernel(place_ref, keep_ref, got_ref, o0, o1, o2, o3):
     me = place_ref[1]
+    lane = lax.broadcasted_iota(jnp.int32, (32, BLK), 1)
     for step, out in enumerate((o0, o1, o2, o3)):
         at = pl.ds(pl.multiple_of((me ^ step) * 32, 32), 32)
-        out[...] = keep_ref[at, :] + got_ref[at, :]
+        if step == 0:
+            out[...] = keep_ref[at, :] + got_ref[at, :]
+            continue
+        scales = jnp.zeros((32, BLK), F32)
+        for m in range(3):
+            part = slice(m * HB, (m + 1) * HB)
+            value = keep_ref[at, part] + got_ref[at, part]
+            top = jnp.max(jnp.abs(value), axis=1, keepdims=True)
+            power = jnp.clip(jnp.ceil(jnp.log2(jnp.maximum(top, 1e-35))), -110.0, 120.0)
+            whole = jnp.round(value * jnp.exp2(15.0 - power))
+            out[:, part] = jnp.clip(whole, -32767.0, 32767.0).astype(jnp.int16)
+            scales = jnp.where(lane >= m * 32, power, scales)
+        out[:, 3 * HB :] = scales.astype(jnp.int16)
 
 
 def act_kernel(a0, a1, a2, a3, out_ref):
-    def total(at):
-        part = slice(at * HB, (at + 1) * HB)
-        return (a0[:, part] + a1[:, part]) + (a2[:, part] + a3[:, part])
+    scales = [a[:, 3 * HB :].astype(F32) for a in (a1, a2, a3)]
+
+    def total(m):
+        part = slice(m * HB, (m + 1) * HB)
+        value = a0[:, part]
+        for a, scale in zip((a1, a2, a3), scales):
+            value += a[:, part].astype(F32) * jnp.exp2(scale[:, m * 32 : m * 32 + 1] - 15.0)
+        return value
 
     gate, up, dh = total(0), total(1), total(2)
     sig = jax.nn.sigmoid(gate)
@@ -145,35 +163,41 @@
         out[:, DQ:] = grad[step * 64 : (step + 1) * 64].astype(out.dtype)
 
 
-def prep_kernel(p0, p1, p2, p3, xt_ref, dy_ref, rows):
-    for step, piece in enumerate((p0, p1, p2, p3)):
-        rows[step * 64 : (step + 1) * 64, :] = piece[...]
+def prep_kernel(p0, p1, p2, p3, out_ref):
     for b in range(DB):
-        xt_ref[b] = rows[:, b * BLK : (b + 1) * BLK].T
-        dy_ref[b] = rows[:, DQ + b * BLK : DQ + (b + 1) * BLK]
-
-
-def grad_kernel(code_ref, full_ref, x0, x1, x2, x3, y0, y1, y2, y3, out_ref, xt, dy, ht, dg, du):
+        for side, pair in enumerate(((p0, p1), (p2, p3))):
+            lanes = slice(side * 128, (side + 1) * 128)
+            x = jnp.concatenate([p[:, b * BLK : (b + 1) * BLK] for p in pair], axis=0)
+            out_ref[b, :, lanes] = x.T
+            for low, p in enumerate(pair):
+                out_ref[DB + b, low * 64 : (low + 1) * 64, lanes] = p[:, DQ + b * BLK : DQ + (b + 1) * BLK]
+
+
+def grad_kernel(code_ref, full, s0, s1, s2, s3, out_ref, slab, ht, dg, du):
     turn = pl.program_id(0)
 
     @pl.when(turn == 0)
     def _():
-        for j, (x, y) in enumerate(((x0, y0), (x1, y1), (x2, y2), (x3, y3))):
-            xt[j * DB : (j + 1) * DB] = x[...]
-            dy[j * DB : (j + 1) * DB] = y[...]
+        for j, source in enumerate((s0, s1, s2, s3)):
+            slab[j * 2 * DB : (j + 1) * 2 * DB] = source[...]
         for a in range(FB):
-            ht[a] = full_ref[:, a * BLK : (a + 1) * BLK].T
-            dg[a] = full_ref[:, HB + a * BLK : HB + (a + 1) * BLK]
-            du[a] = full_ref[:, 2 * HB + a * BLK : 2 * HB + (a + 1) * BLK]
+            ht[a] = full[:, a * BLK : (a + 1) * BLK].T
+            dg[a] = full[:, HB + a * BLK : HB + (a + 1) * BLK]
+            du[a] = full[:, 2 * HB + a * BLK : 2 * HB + (a + 1) * BLK]
 
     for near in range(STEP):
         for m in range(3):
             code = code_ref[m, turn * STEP + near]
             where = jnp.maximum(code - 1, 0)
-            feat = where // 64 * DB + where % 8
+            feat = where // 64 * 2 * DB + where % 8
             hid = where % 64 // 8
-            left, right = ((xt.at[feat], dg.at[hid]), (xt.at[feat], du.at[hid]), (ht.at[hid], dy.at[feat]))[m]
-            value = jnp.dot(left[...], right[...], preferred_element_type=F32)
+            if m == 2:
+                left = ht[hid]
+                right = jnp.concatenate([slab[feat + DB, :, :128], slab[feat + DB, :, 128:]], axis=0)
+            else:
+                left = slab[feat]
+                right = (dg, du)[m][hid]
+            value = jnp.dot(left, right, preferred_element_type=F32)
             out_ref[m, near] = jnp.where(code > 0, value, 0.0).astype(BF)
 
 
@@ -210,53 +234,65 @@
     pieces, mirror, code = tie((pieces, mirror, code))
 
     half = sds((128, 3 * HB), F32)
-    keep, send = call(
-        partial_kernel, [half, half], [SMEM] + [VMEM] * 7, scratch=[pltpu.VMEM((TOKENS, 2 * DQ), BF)]
-    )(place, *pieces, wg, wu, wd)
+
+    def partial(other):
+        return call(
+            functools.partial(partial_kernel, other=other),
+            half,
+            [SMEM] + [VMEM] * 7,
+            scratch=[pltpu.VMEM((128, 2 * DQ), BF)],
+        )(place, *pieces, wg, wu, wd)
+
+    send = partial(1)
     got = row_swap(send, 1)
-    fours = call(pair_kernel, [sds((32, 3 * HB), F32)] * 4, [SMEM, VMEM, VMEM])(place, keep, got)
-    sums = [fours[0]] + [square_swap(fours[i], i) for i in range(1, 4)]
+    keep = partial(0)
+    coded = sds((32, 3 * HB + BLK), jnp.int16)
+    sums = call(pair_kernel, [sds((32, 3 * HB), F32)] + [coded] * 3, [SMEM, VMEM, VMEM])(place, keep, got)
+    sums = [sums[0]] + [square_swap(sums[i], i) for i in range(1, 4)]
 
     pieces, mirror, keep = tie((pieces, mirror, keep))
-    mirrors = [mirror] + [row_swap(mirror, x_mask(i)) for i in range(1, 4)]
-    prepped = [sds((DB, BLK, TOKENS), BF), sds((DB, TOKENS, BLK), BF)]
-    prep = call(prep_kernel, prepped, [VMEM] * 4, scratch=[pltpu.VMEM((TOKENS, 2 * DQ), BF)])
-    x0, y0 = prep(*pieces)
-    sums, mirrors, x0, y0 = tie((sums, mirrors, x0, y0))
+    mirror1, mirror3 = row_swap(mirror, x_mask(1)), row_swap(mirror, x_mask(3))
+    prep = call(prep_kernel, sds((2 * DB, BLK, TOKENS), BF), [VMEM] * 4)
+    slab0 = prep(*pieces)
+    sums, mirror1, mirror3, slab0 = tie((sums, mirror1, mirror3, slab0))
 
     share = call(act_kernel, sds((32, 3 * HB), BF), [VMEM] * 4)(*sums)
     mine = [share] + [square_swap(share, i) for i in range(1, 4)]
-    x2, y2 = prep(*tie((mirrors, share))[0])
-    x1, y1 = [row_swap(v, 1) for v in (x0, y0)]
-    mine, x1, y1, x2, y2 = tie((mine, x1, y1, x2, y2))
+    mirror, slab0, share = tie((mirror, slab0, share))
+    mirror2 = row_swap(mirror, x_mask(2))
+    slab1 = row_swap(slab0, 1)
+    mine, mirror2, slab1 = tie((mine, mirror2, slab1))
+
     mine = jnp.concatenate(mine, axis=0)
     theirs = row_swap(mine, 1)
+    slab2 = prep(mirror, mirror1, mirror2, mirror3)
+    theirs, slab2 = tie((theirs, slab2))
     outs = call(
         out_kernel,
         [sds((64, 2 * DQ), F32)] + [sds((64, 2 * DQ), BF)] * 3 + [sds((TOKENS, 3 * HB), BF)],
         [SMEM] + [VMEM] * 5,
     )(place, mine, theirs, wg, wu, wd)
     full = outs[4]
-    x3, y3 = [row_swap(v, 1) for v in tie((x2, y2, mine))[:2]]
-    far = [row_swap(outs[i], x_mask(i)) for i in range(1, 4)]
+    slab2, full = tie((slab2, full))
+    slab3 = row_swap(slab2, 1)
+    far1, far2, far3 = [row_swap(outs[i], x_mask(i)) for i in range(1, 4)]
 
     grads = call(
         grad_kernel,
         sds((3, CAP, BLK, BLK), BF),
-        [SMEM] + [VMEM] * 9,
+        [SMEM] + [VMEM] * 5,
         out_specs=pl.BlockSpec((3, STEP, BLK, BLK), lambda i: (0, i, 0, 0)),
         scratch=[
-            pltpu.VMEM((QUARTERS * DB, BLK, TOKENS), BF),
-            pltpu.VMEM((QUARTERS * DB, TOKENS, BLK), BF),
+            pltpu.VMEM((QUARTERS * 2 * DB, BLK, TOKENS), BF),
             pltpu.VMEM((FB, BLK, TOKENS), BF),
             pltpu.VMEM((FB, TOKENS, BLK), BF),
             pltpu.VMEM((FB, TOKENS, BLK), BF),
         ],
         grid=(CAP // STEP,),
         limit=24,
-    )(code, full, x0, x1, x2, x3, y0, y1, y2, y3)
-    far, grads = tie((far, grads))
-    total = outs[0] + far[0].astype(F32) + far[1].astype(F32) + far[2].astype(F32)
+    )(code, full, slab0, slab1, slab2, slab3)
+    far1, far2, far3, grads = tie((far1, far2, far3, grads))
+    total = outs[0] + far1.astype(F32) + far2.astype(F32) + far3.astype(F32)
     last = total[: 2 * TG]
     for i in range(1, 4):
         last = last + row_swap(total[i * 2 * TG : (i + 1) * 2 * TG].astype(BF), z_mask(i)).astype(F32)

time: 118 us -> 115 us (0.975); the launches traced: 115 us -> 114 us
  waiting for transfers between devices: 51.1 us -> 45 us
  starting transfers between devices: 38.6 us -> 42.1 us
  Pallas kernels: 16.3 us -> 17.6 us
    ppermute x24 -> x22, waiting for transfers between devices: 43.2 us -> 33.2 us  [row_swap(): return lax.ppermute(value, 'row', [(i, i ^ mask) for i in range(128)])]
    ppermute x6, waiting for transfers between devices: 7.91 us -> 11.8 us  [square_swap(): lax.ppermute(value, ('row', 'col'), [(i, i ^ mask) for i in range(256)])]
    ppermute x24 -> x22, starting transfers between devices: 31.4 us -> 35.1 us  [row_swap(): return lax.ppermute(value, 'row', [(i, i ^ mask) for i in range(128)])]
    pallas_call x5 -> x6, Pallas kernels: 9.85 us -> 11.3 us  [the longest x1 6.21 us: body(): call(grad_kernel, sds((3, CAP, BLK, BLK), BF), [SMEM] + [VMEM] * 5, out_s...]
  transfers between devices with their start and end apart: 30 -> 28, of which waited for: 19 -> 18; matrix products, arithmetic and copies ran while one was open for 2% -> 2% of each run, Pallas kernels for 12% -> 11%
where the time goes in v3:
time: 115 us; the launch traced here: 114 us
  waiting for transfers between devices  45 us (39%)
  starting transfers between devices  42.1 us (37%)
  Pallas kernels  17.6 us (15%)
  local copies, waits for them, and re-layouts  8.22 us (7%)
    ppermute x22, starting transfers between devices, row_swap(): return lax.ppermute(value, 'row', [(i, i ^ mask) for i in range(128)])  35.1 us
    ppermute x22, waiting for transfers between devices, row_swap(): return lax.ppermute(value, 'row', [(i, i ^ mask) for i in range(128)])  33.2 us
    ppermute x6, waiting for transfers between devices, square_swap(): lax.ppermute(value, ('row', 'col'), [(i, i ^ mask) for i in range(256)])  11.8 us
    ppermute x6, starting transfers between devices, square_swap(): lax.ppermute(value, ('row', 'col'), [(i, i ^ mask) for i in range(256)])  7.06 us
    pallas_call x1, Pallas kernels, body(): call(grad_kernel, sds((3, CAP, BLK, BLK), BF), [SMEM] + [VMEM] * 5, out_s...  6.21 us
    unnamed x15, local copies, waits for them, and re-layouts  5.06 us
    pallas_call x2, Pallas kernels, partial(): call(functools.partial(partial_kernel, other=other), half, [SMEM] + [VMEM...  3.77 us
    pallas_call x1, Pallas kernels, body(): call(dense_kernel, wide, [SMEM] + [VMEM] * 3)  3.57 us
  transfers between devices with their start and end apart: 28, of which 18 were waited for; matrix products, arithmetic and copies ran while one was open for 2% of the time, Pallas kernels for 11%

profile of v3, /device:TPU:32, one launch (start us, length us, event | category | flops | bytes accessed | tf_op | source)
XLA Modules:
  0.0 114.3 jit_solution(3170686712399305514)
XLA Ops:
  2.1 3.2 %collective-permute-start = (bf16[8,2048]{1,0:T(8,128)(2,1)S(1)}, bf16[8,2048]{1,0:T(8,128)(2,1)S(1)}, u32[]{:S(2)}, u32[]{:S(2)}) collective-permute-start(bf16[8,2048]{1,0:T(8,128)(2,1)S(1)} %get-tuple-element.111), channel_id=1, source_target_pairs={{0,128},{2,130},{4,132},{6,134},{8,136},{10,138},{12,140},{14,142}... | collective-permute-start | bytes 98312 | tf_op jit(solution)/shard_map/ppermute | solution.py:29
  7.5 5.4 %collective-permute-start.3 = (bf16[16,2048]{1,0:T(8,128)(2,1)S(1)}, bf16[16,2048]{1,0:T(8,128)(2,1)S(1)}, u32[]{:S(2)}, u32[]{:S(2)}) collective-permute-start(bf16[16,2048]{1,0:T(8,128)(2,1)S(1)} %pad_maximum_fusion), channel_id=1, source_target_pairs={{0,24},{2,26},{4,28},{6,30},{8,16},{10,18},{12,20},{14,22},{16,8},... | collective-permute-start | bytes 196616 | tf_op jit(solution)/shard_map/ppermute | solution.py:29
  12.9 1.4 %collective-permute-start.2 = (bf16[16,2048]{1,0:T(8,128)(2,1)S(1)}, bf16[16,2048]{1,0:T(8,128)(2,1)S(1)}, u32[]{:S(2)}, u32[]{:S(2)}) collective-permute-start(bf16[16,2048]{1,0:T(8,128)(2,1)S(1)} %pad_maximum_fusion), channel_id=1, source_target_pairs={{0,16},{2,18},{4,20},{6,22},{8,24},{10,26},{12,28},{14,30},{16,0},... | collective-permute-start | bytes 196616 | tf_op jit(solution)/shard_map/ppermute | solution.py:29
  15.4 4.1 %collective-permute-done.1 = bf16[16,2048]{1,0:T(8,128)(2,1)S(1)} collective-permute-done((bf16[16,2048]{1,0:T(8,128)(2,1)S(1)}, bf16[16,2048]{1,0:T(8,128)(2,1)S(1)}, u32[]{:S(2)}, u32[]{:S(2)}) %collective-permute-start.1) | collective-permute-done | bytes 65568 | tf_op jit(solution)/shard_map/ppermute | solution.py:29
  19.6 1.8 %collective-permute-done.2 = bf16[16,2048]{1,0:T(8,128)(2,1)S(1)} collective-permute-done((bf16[16,2048]{1,0:T(8,128)(2,1)S(1)}, bf16[16,2048]{1,0:T(8,128)(2,1)S(1)}, u32[]{:S(2)}, u32[]{:S(2)}) %collective-permute-start.2) | collective-permute-done | bytes 65568 | tf_op jit(solution)/shard_map/ppermute | solution.py:29
  21.4 1.4 %collective-permute-start.7 = (bf16[64,2048]{1,0:T(8,128)(2,1)S(1)}, bf16[64,2048]{1,0:T(8,128)(2,1)S(1)}, u32[]{:S(2)}, u32[]{:S(2)}) collective-permute-start(bf16[64,2048]{1,0:T(8,128)(2,1)S(1)} %constant_dynamic-update-slice_fusion.2.p0), channel_id=1, source_target_pairs={{0,4},{2,6},{4,0},{6,2},{8,12},{10,14},{12,8},{14,10},{16,20},{18,... | collective-permute-start | bytes 786440 | tf_op jit(solution)/shard_map/ppermute | solution.py:29
  22.8 2.8 %collective-permute-start.6 = (bf16[64,2048]{1,0:T(8,128)(2,1)S(1)}, bf16[64,2048]{1,0:T(8,128)(2,1)S(1)}, u32[]{:S(2)}, u32[]{:S(2)}) collective-permute-start(bf16[64,2048]{1,0:T(8,128)(2,1)S(1)} %constant_dynamic-update-slice_fusion.2.p0), channel_id=1, source_target_pairs={{0,96},{2,98},{4,100},{6,102},{8,104},{10,106},{12,108},{14,110},{... | collective-permute-start | bytes 786440 | tf_op jit(solution)/shard_map/ppermute | solution.py:29
  27.3 1.4 %copy-done.1 = bf16[1,1,48,128,128]{4,3,2,1,0:T(8,128)(2,1)S(1)} copy-done((bf16[1,1,48,128,128]{4,3,2,1,0:T(8,128)(2,1)S(1)}, bf16[1,1,48,128,128]{4,3,2,1,0:T(8,128)(2,1)}, u32[]{:S(2)}) %copy-start.1) | copy-done | bytes 1572888
  28.7 1.4 %copy-done.2 = bf16[1,1,48,128,128]{4,3,2,1,0:T(8,128)(2,1)S(1)} copy-done((bf16[1,1,48,128,128]{4,3,2,1,0:T(8,128)(2,1)S(1)}, bf16[1,1,48,128,128]{4,3,2,1,0:T(8,128)(2,1)}, u32[]{:S(2)}) %copy-start.2) | copy-done | bytes 1572888
  30.1 1.4 %copy-done.3 = bf16[1,1,48,128,128]{4,3,2,1,0:T(8,128)(2,1)S(1)} copy-done((bf16[1,1,48,128,128]{4,3,2,1,0:T(8,128)(2,1)S(1)}, bf16[1,1,48,128,128]{4,3,2,1,0:T(8,128)(2,1)}, u32[]{:S(2)}) %copy-start.3) | copy-done | bytes 1572888
  31.5 3.6 %shard_map.94 = (bf16[1024,896]{1,0:T(8,128)(2,1)S(1)}, bf16[1024,896]{1,0:T(8,128)(2,1)S(1)}, bf16[896,1024]{1,0:T(8,128)(2,1)S(1)}) custom-call(s32[3,48]{1,0:T(4,128)S(1)} %dynamic-slice_reduce_fusion.index_ref, bf16[48,128,128]{2,1,0:T(8,128)(2,1)S(1)} %bitcast.12, bf16[48,128,128]{2,1,0:T(8,128)(2,1)S(1)} %bitcast.13, bf16[48,128,128]{2,1,0:T(8,128)(2,1)S(1)} %bitcast.14), custom_call_target="tpu_custom_call" | custom-call | tf_op jit(solution)/shard_map/pallas_call | solution.py:221
  36.9 1.9 %shard_map.96 = f32[128,2688]{1,0:T(8,128)S(1)} custom-call(s32[2]{0:T(128)S(1)} %pad_add_fusion.place_ref, bf16[64,2048]{1,0:T(8,128)(2,1)S(1)} %constant_dynamic-update-slice_fusion.2.p0, bf16[64,2048]{1,0:T(8,128)(2,1)S(1)} %collective-permute-done.4.p1, bf16[64,2048]{1,0:T(8,128)(2,1)S(1)} %collective-permute-done.5.p2, ...), custom_call_target="tpu_custom_call" | custom-call | tf_op jit(solution)/shard_map/pallas_call | solution.py:239
  38.9 1.9 %shard_map.95.keep_ref = f32[128,2688]{1,0:T(8,128)S(1)} custom-call(s32[2]{0:T(128)S(1)} %pad_add_fusion.place_ref, bf16[64,2048]{1,0:T(8,128)(2,1)S(1)} %constant_dynamic-update-slice_fusion.2.p0, bf16[64,2048]{1,0:T(8,128)(2,1)S(1)} %collective-permute-done.4.p1, bf16[64,2048]{1,0:T(8,128)(2,1)S(1)} %collective-permute-done.5.p2, ...), custom_call_target="tpu_custom_call" | custom-call | tf_op jit(solution)/shard_map/pallas_call | solution.py:239
  40.8 2.8 %collective-permute-start.13 = (bf16[64,2048]{1,0:T(8,128)(2,1)S(1)}, bf16[64,2048]{1,0:T(8,128)(2,1)S(1)}, u32[]{:S(2)}, u32[]{:S(2)}) collective-permute-start(bf16[64,2048]{1,0:T(8,128)(2,1)S(1)} %collective-permute-done.7.p0), channel_id=1, source_target_pairs={{0,96},{2,98},{4,100},{6,102},{8,104},{10,106},{12,108},{14,110},{... | collective-permute-start | bytes 786440 | tf_op jit(solution)/shard_map/ppermute | solution.py:29
  45.8 2.5 %collective-permute-start.11 = (s16[32,2816]{1,0:T(8,128)(2,1)S(1)}, s16[32,2816]{1,0:T(8,128)(2,1)S(1)}, u32[]{:S(2)}, u32[]{:S(2)}) collective-permute-start(s16[32,2816]{1,0:T(8,128)(2,1)S(1)} %get-tuple-element.59), channel_id=1, source_target_pairs={{0,5},{1,4},{2,7},{3,6},{4,1},{5,0},{6,3},{7,2},{8,13},{9,12},{10,... | collective-permute-start | bytes 540680 | tf_op jit(solution)/shard_map/ppermute | solution.py:34
  48.5 2.3 %collective-permute-done.13.p3 = bf16[64,2048]{1,0:T(8,128)(2,1)S(1)} collective-permute-done((bf16[64,2048]{1,0:T(8,128)(2,1)S(1)}, bf16[64,2048]{1,0:T(8,128)(2,1)S(1)}, u32[]{:S(2)}, u32[]{:S(2)}) %collective-permute-start.13) | collective-permute-done | bytes 262176 | tf_op jit(solution)/shard_map/ppermute | solution.py:29
  52.4 3.8 %collective-permute-done.11.a3 = s16[32,2816]{1,0:T(8,128)(2,1)S(1)} collective-permute-done((s16[32,2816]{1,0:T(8,128)(2,1)S(1)}, s16[32,2816]{1,0:T(8,128)(2,1)S(1)}, u32[]{:S(2)}, u32[]{:S(2)}) %collective-permute-start.11) | collective-permute-done | bytes 180256 | tf_op jit(solution)/shard_map/ppermute | solution.py:34
  56.8 1.7 %collective-permute-start.17 = (bf16[64,2048]{1,0:T(8,128)(2,1)S(1)}, bf16[64,2048]{1,0:T(8,128)(2,1)S(1)}, u32[]{:S(2)}, u32[]{:S(2)}) collective-permute-start(bf16[64,2048]{1,0:T(8,128)(2,1)S(1)} %collective-permute-done.7.p0), channel_id=1, source_target_pairs={{0,64},{2,66},{4,68},{6,70},{8,72},{10,74},{12,76},{14,78},{16,80}... | collective-permute-start | bytes 786440 | tf_op jit(solution)/shard_map/ppermute | solution.py:29
  59.0 1.4 %collective-permute-start.15 = (bf16[32,2688]{1,0:T(8,128)(2,1)S(1)}, bf16[32,2688]{1,0:T(8,128)(2,1)S(1)}, u32[]{:S(2)}, u32[]{:S(2)}) collective-permute-start(bf16[32,2688]{1,0:T(8,128)(2,1)S(1)} %shard_map.99), channel_id=1, source_target_pairs={{0,4},{1,5},{2,6},{3,7},{4,0},{5,1},{6,2},{7,3},{8,12},{9,13},{10,... | collective-permute-start | bytes 516104 | tf_op jit(solution)/shard_map/ppermute | solution.py:34
  60.4 1.6 %collective-permute-start.14 = (bf16[32,2688]{1,0:T(8,128)(2,1)S(1)}, bf16[32,2688]{1,0:T(8,128)(2,1)S(1)}, u32[]{:S(2)}, u32[]{:S(2)}) collective-permute-start(bf16[32,2688]{1,0:T(8,128)(2,1)S(1)} %shard_map.99), channel_id=1, source_target_pairs={{0,1},{1,0},{2,3},{3,2},{4,5},{5,4},{6,7},{7,6},{8,9},{9,8},{10,11... | collective-permute-start | bytes 516104 | tf_op jit(solution)/shard_map/ppermute | solution.py:34
  62.0 4.7 %collective-permute-done.16 = bf16[32,2688]{1,0:T(8,128)(2,1)S(1)} collective-permute-done((bf16[32,2688]{1,0:T(8,128)(2,1)S(1)}, bf16[32,2688]{1,0:T(8,128)(2,1)S(1)}, u32[]{:S(2)}, u32[]{:S(2)}) %collective-permute-start.16) | collective-permute-done | bytes 172064 | tf_op jit(solution)/shard_map/ppermute | solution.py:34
  66.7 1.8 %collective-permute-done.15 = bf16[32,2688]{1,0:T(8,128)(2,1)S(1)} collective-permute-done((bf16[32,2688]{1,0:T(8,128)(2,1)S(1)}, bf16[32,2688]{1,0:T(8,128)(2,1)S(1)}, u32[]{:S(2)}, u32[]{:S(2)}) %collective-permute-start.15) | collective-permute-done | bytes 172064 | tf_op jit(solution)/shard_map/ppermute | solution.py:34
  70.0 1.9 %collective-permute-done.19.theirs = bf16[128,2688]{1,0:T(8,128)(2,1)S(1)} collective-permute-done((bf16[128,2688]{1,0:T(8,128)(2,1)S(1)}, bf16[128,2688]{1,0:T(8,128)(2,1)S(1)}, u32[]{:S(2)}, u32[]{:S(2)}) %collective-permute-start.19) | collective-permute-done | bytes 688160 | tf_op jit(solution)/shard_map/ppermute | solution.py:29
  71.9 2.5 %shard_map.101 = (f32[64,2048]{1,0:T(8,128)S(1)}, bf16[64,2048]{1,0:T(8,128)(2,1)S(1)}, bf16[64,2048]{1,0:T(8,128)(2,1)S(1)}, bf16[64,2048]{1,0:T(8,128)(2,1)S(1)}, bf16[256,2688]{1,0:T(8,128)(2,1)S(1)}) custom-call(s32[2]{0:T(128)S(1)} %pad_add_fusion.place_ref, bf16[128,2688]{1,0:T(8,128)(2,1)S(1)} %constant_dynamic-update-slice_fusion.8.mine, ...), custom_call_target="tpu_custom_call" | custom-call | tf_op jit(solution)/shard_map/pallas_call | solution.py:270
  74.9 3.9 %collective-permute-start.21 = (bf16[64,2048]{1,0:T(8,128)(2,1)S(1)}, bf16[64,2048]{1,0:T(8,128)(2,1)S(1)}, u32[]{:S(2)}, u32[]{:S(2)}) collective-permute-start(bf16[64,2048]{1,0:T(8,128)(2,1)S(1)} %get-tuple-element.83), channel_id=1, source_target_pairs={{0,64},{2,66},{4,68},{6,70},{8,72},{10,74},{12,76},{14,78},{16,80}... | collective-permute-start | bytes 786440 | tf_op jit(solution)/shard_map/ppermute | solution.py:29
  79.3 6.2 %shard_map.102 = bf16[3,48,128,128]{3,2,1,0:T(8,128)(2,1)} custom-call(s32[3,48]{1,0:T(4,128)S(1)} %select_reduce_fusion.code_ref, bf16[256,2688]{1,0:T(8,128)(2,1)S(1)} %get-tuple-element.88.full, bf16[16,128,256]{2,1,0:T(8,128)(2,1)S(1)} %shard_map.98.s0, bf16[16,128,256]{2,1,0:T(8,128)(2,1)S(1)} %collective-permute-done.18.s1, ...), custom_call_target="tpu_custom_call" | custom-call | tf_op jit(solution)/shard_map/pallas_call | solution.py:280
  85.5 5.6 %collective-permute-done.21 = bf16[64,2048]{1,0:T(8,128)(2,1)S(1)} collective-permute-done((bf16[64,2048]{1,0:T(8,128)(2,1)S(1)}, bf16[64,2048]{1,0:T(8,128)(2,1)S(1)}, u32[]{:S(2)}, u32[]{:S(2)}) %collective-permute-start.21) | collective-permute-done | bytes 262176 | tf_op jit(solution)/shard_map/ppermute | solution.py:29
  91.1 2.6 %collective-permute-done.22 = bf16[64,2048]{1,0:T(8,128)(2,1)S(1)} collective-permute-done((bf16[64,2048]{1,0:T(8,128)(2,1)S(1)}, bf16[64,2048]{1,0:T(8,128)(2,1)S(1)}, u32[]{:S(2)}, u32[]{:S(2)}) %collective-permute-start.22) | collective-permute-done | bytes 262176 | tf_op jit(solution)/shard_map/ppermute | solution.py:29
  94.5 5.0 %collective-permute-start.26 = (bf16[16,2048]{1,0:T(8,128)(2,1)S(1)}, bf16[16,2048]{1,0:T(8,128)(2,1)S(1)}, u32[]{:S(2)}, u32[]{:S(2)}) collective-permute-start(bf16[16,2048]{1,0:T(8,128)(2,1)S(1)} %get-tuple-element.107), channel_id=1, source_target_pairs={{0,24},{2,26},{4,28},{6,30},{8,16},{10,18},{12,20},{14,22},{16,8},... | collective-permute-start | bytes 196616 | tf_op jit(solution)/shard_map/ppermute | solution.py:29
  101.8 6.3 %collective-permute-done.25 = bf16[16,2048]{1,0:T(8,128)(2,1)S(1)} collective-permute-done((bf16[16,2048]{1,0:T(8,128)(2,1)S(1)}, bf16[16,2048]{1,0:T(8,128)(2,1)S(1)}, u32[]{:S(2)}, u32[]{:S(2)}) %collective-permute-start.25) | collective-permute-done | bytes 65568 | tf_op jit(solution)/shard_map/ppermute | solution.py:29
  108.1 1.7 %collective-permute-start.27 = (bf16[8,2048]{1,0:T(8,128)(2,1)S(1)}, bf16[8,2048]{1,0:T(8,128)(2,1)S(1)}, u32[]{:S(2)}, u32[]{:S(2)}) collective-permute-start(bf16[8,2048]{1,0:T(8,128)(2,1)S(1)} %slice.53), channel_id=1, source_target_pairs={{0,128},{2,130},{4,132},{6,134},{8,136},{10,138},{12,140},{14,142}... | collective-permute-start | bytes 98312 | tf_op jit(solution)/shard_map/ppermute | solution.py:29
  109.9 3.8 %collective-permute-done.27 = bf16[8,2048]{1,0:T(8,128)(2,1)S(1)} collective-permute-done((bf16[8,2048]{1,0:T(8,128)(2,1)S(1)}, bf16[8,2048]{1,0:T(8,128)(2,1)S(1)}, u32[]{:S(2)}, u32[]{:S(2)}) %collective-permute-start.27) | collective-permute-done | bytes 32800 | tf_op jit(solution)/shard_map/ppermute | solution.py:29
  (72 shorter events, 19.7 us)
Async XLA Ops:
  0.6 4.9 %copy-start = (s32[3,128,2,48]{1,3,2,0:T(8,128)S(1)}, s32[3,128,2,48]{1,3,2,0:T(8,128)}, u32[]{:S(2)}) copy-start(s32[3,128,2,48]{1,3,2,0:T(8,128)} %param.12) | copy-start | bytes 442372
  2.1 5.4 %collective-permute-start = (bf16[8,2048]{1,0:T(8,128)(2,1)S(1)}, bf16[8,2048]{1,0:T(8,128)(2,1)S(1)}, u32[]{:S(2)}, u32[]{:S(2)}) collective-permute-start(bf16[8,2048]{1,0:T(8,128)(2,1)S(1)} %get-tuple-element.111), channel_id=1, source_target_pairs={{0,128},{2,130},{4,132},{6,134},{8,136},{10,138},{12,140},{14,142}... | collective-permute-start | bytes 98312 | tf_op jit(solution)/shard_map/ppermute | solution.py:29
  7.5 13.8 %collective-permute-start.3 = (bf16[16,2048]{1,0:T(8,128)(2,1)S(1)}, bf16[16,2048]{1,0:T(8,128)(2,1)S(1)}, u32[]{:S(2)}, u32[]{:S(2)}) collective-permute-start(bf16[16,2048]{1,0:T(8,128)(2,1)S(1)} %pad_maximum_fusion), channel_id=1, source_target_pairs={{0,24},{2,26},{4,28},{6,30},{8,16},{10,18},{12,20},{14,22},{16,8},... | collective-permute-start | bytes 196616 | tf_op jit(solution)/shard_map/ppermute | solution.py:29
  12.9 8.4 %collective-permute-start.2 = (bf16[16,2048]{1,0:T(8,128)(2,1)S(1)}, bf16[16,2048]{1,0:T(8,128)(2,1)S(1)}, u32[]{:S(2)}, u32[]{:S(2)}) collective-permute-start(bf16[16,2048]{1,0:T(8,128)(2,1)S(1)} %pad_maximum_fusion), channel_id=1, source_target_pairs={{0,16},{2,18},{4,20},{6,22},{8,24},{10,26},{12,28},{14,30},{16,0},... | collective-permute-start | bytes 196616 | tf_op jit(solution)/shard_map/ppermute | solution.py:29
  14.4 5.2 %collective-permute-start.1 = (bf16[16,2048]{1,0:T(8,128)(2,1)S(1)}, bf16[16,2048]{1,0:T(8,128)(2,1)S(1)}, u32[]{:S(2)}, u32[]{:S(2)}) collective-permute-start(bf16[16,2048]{1,0:T(8,128)(2,1)S(1)} %pad_maximum_fusion), channel_id=1, source_target_pairs={{0,8},{2,10},{4,12},{6,14},{8,0},{10,2},{12,4},{14,6},{16,24},{18,... | collective-permute-start | bytes 196616 | tf_op jit(solution)/shard_map/ppermute | solution.py:29
  21.4 14.0 %collective-permute-start.7 = (bf16[64,2048]{1,0:T(8,128)(2,1)S(1)}, bf16[64,2048]{1,0:T(8,128)(2,1)S(1)}, u32[]{:S(2)}, u32[]{:S(2)}) collective-permute-start(bf16[64,2048]{1,0:T(8,128)(2,1)S(1)} %constant_dynamic-update-slice_fusion.2.p0), channel_id=1, source_target_pairs={{0,4},{2,6},{4,0},{6,2},{8,12},{10,14},{12,8},{14,10},{16,20},{18,... | collective-permute-start | bytes 786440 | tf_op jit(solution)/shard_map/ppermute | solution.py:29
  22.8 13.4 %collective-permute-start.6 = (bf16[64,2048]{1,0:T(8,128)(2,1)S(1)}, bf16[64,2048]{1,0:T(8,128)(2,1)S(1)}, u32[]{:S(2)}, u32[]{:S(2)}) collective-permute-start(bf16[64,2048]{1,0:T(8,128)(2,1)S(1)} %constant_dynamic-update-slice_fusion.2.p0), channel_id=1, source_target_pairs={{0,96},{2,98},{4,100},{6,102},{8,104},{10,106},{12,108},{14,110},{... | collective-permute-start | bytes 786440 | tf_op jit(solution)/shard_map/ppermute | solution.py:29
  25.5 10.7 %collective-permute-start.5 = (bf16[64,2048]{1,0:T(8,128)(2,1)S(1)}, bf16[64,2048]{1,0:T(8,128)(2,1)S(1)}, u32[]{:S(2)}, u32[]{:S(2)}) collective-permute-start(bf16[64,2048]{1,0:T(8,128)(2,1)S(1)} %constant_dynamic-update-slice_fusion.2.p0), channel_id=1, source_target_pairs={{0,64},{2,66},{4,68},{6,70},{8,72},{10,74},{12,76},{14,78},{16,80}... | collective-permute-start | bytes 786440 | tf_op jit(solution)/shard_map/ppermute | solution.py:29
  26.3 10.5 %collective-permute-start.4 = (bf16[64,2048]{1,0:T(8,128)(2,1)S(1)}, bf16[64,2048]{1,0:T(8,128)(2,1)S(1)}, u32[]{:S(2)}, u32[]{:S(2)}) collective-permute-start(bf16[64,2048]{1,0:T(8,128)(2,1)S(1)} %constant_dynamic-update-slice_fusion.2.p0), channel_id=1, source_target_pairs={{0,32},{2,34},{4,36},{6,38},{8,40},{10,42},{12,44},{14,46},{16,48}... | collective-permute-start | bytes 786440 | tf_op jit(solution)/shard_map/ppermute | solution.py:29
  27.3 1.4 %copy-start.1 = (bf16[1,1,48,128,128]{4,3,2,1,0:T(8,128)(2,1)S(1)}, bf16[1,1,48,128,128]{4,3,2,1,0:T(8,128)(2,1)}, u32[]{:S(2)}) copy-start(bf16[1,1,48,128,128]{4,3,2,1,0:T(8,128)(2,1)} %param.9) | copy-start | bytes 4718596
  28.7 1.4 %copy-start.2 = (bf16[1,1,48,128,128]{4,3,2,1,0:T(8,128)(2,1)S(1)}, bf16[1,1,48,128,128]{4,3,2,1,0:T(8,128)(2,1)}, u32[]{:S(2)}) copy-start(bf16[1,1,48,128,128]{4,3,2,1,0:T(8,128)(2,1)} %param.10) | copy-start | bytes 4718596
  30.1 1.4 %copy-start.3 = (bf16[1,1,48,128,128]{4,3,2,1,0:T(8,128)(2,1)S(1)}, bf16[1,1,48,128,128]{4,3,2,1,0:T(8,128)(2,1)}, u32[]{:S(2)}) copy-start(bf16[1,1,48,128,128]{4,3,2,1,0:T(8,128)(2,1)} %param.11) | copy-start | bytes 4718596
  38.8 5.1 %collective-permute-start.8 = (f32[128,2688]{1,0:T(8,128)S(1)}, f32[128,2688]{1,0:T(8,128)S(1)}, u32[]{:S(2)}, u32[]{:S(2)}) collective-permute-start(f32[128,2688]{1,0:T(8,128)S(1)} %shard_map.96), channel_id=1, source_target_pairs={{0,2},{2,0},{4,6},{6,4},{8,10},{10,8},{12,14},{14,12},{16,18},{18,... | collective-permute-start | bytes 4128776 | tf_op jit(solution)/shard_map/ppermute | solution.py:29
  40.8 10.0 %collective-permute-start.13 = (bf16[64,2048]{1,0:T(8,128)(2,1)S(1)}, bf16[64,2048]{1,0:T(8,128)(2,1)S(1)}, u32[]{:S(2)}, u32[]{:S(2)}) collective-permute-start(bf16[64,2048]{1,0:T(8,128)(2,1)S(1)} %collective-permute-done.7.p0), channel_id=1, source_target_pairs={{0,96},{2,98},{4,100},{6,102},{8,104},{10,106},{12,108},{14,110},{... | collective-permute-start | bytes 786440 | tf_op jit(solution)/shard_map/ppermute | solution.py:29
  43.6 8.4 %collective-permute-start.12 = (bf16[64,2048]{1,0:T(8,128)(2,1)S(1)}, bf16[64,2048]{1,0:T(8,128)(2,1)S(1)}, u32[]{:S(2)}, u32[]{:S(2)}) collective-permute-start(bf16[64,2048]{1,0:T(8,128)(2,1)S(1)} %collective-permute-done.7.p0), channel_id=1, source_target_pairs={{0,32},{2,34},{4,36},{6,38},{8,40},{10,42},{12,44},{14,46},{16,48}... | collective-permute-start | bytes 786440 | tf_op jit(solution)/shard_map/ppermute | solution.py:29
  44.7 7.3 %collective-permute-start.9 = (s16[32,2816]{1,0:T(8,128)(2,1)S(1)}, s16[32,2816]{1,0:T(8,128)(2,1)S(1)}, u32[]{:S(2)}, u32[]{:S(2)}) collective-permute-start(s16[32,2816]{1,0:T(8,128)(2,1)S(1)} %get-tuple-element.57), channel_id=1, source_target_pairs={{0,1},{1,0},{2,3},{3,2},{4,5},{5,4},{6,7},{7,6},{8,9},{9,8},{10,11... | collective-permute-start | bytes 540680 | tf_op jit(solution)/shard_map/ppermute | solution.py:34
  45.0 7.4 %collective-permute-start.10 = (s16[32,2816]{1,0:T(8,128)(2,1)S(1)}, s16[32,2816]{1,0:T(8,128)(2,1)S(1)}, u32[]{:S(2)}, u32[]{:S(2)}) collective-permute-start(s16[32,2816]{1,0:T(8,128)(2,1)S(1)} %get-tuple-element.58), channel_id=1, source_target_pairs={{0,4},{1,5},{2,6},{3,7},{4,0},{5,1},{6,2},{7,3},{8,12},{9,13},{10,... | collective-permute-start | bytes 540680 | tf_op jit(solution)/shard_map/ppermute | solution.py:34
  45.8 10.5 %collective-permute-start.11 = (s16[32,2816]{1,0:T(8,128)(2,1)S(1)}, s16[32,2816]{1,0:T(8,128)(2,1)S(1)}, u32[]{:S(2)}, u32[]{:S(2)}) collective-permute-start(s16[32,2816]{1,0:T(8,128)(2,1)S(1)} %get-tuple-element.59), channel_id=1, source_target_pairs={{0,5},{1,4},{2,7},{3,6},{4,1},{5,0},{6,3},{7,2},{8,13},{9,12},{10,... | collective-permute-start | bytes 540680 | tf_op jit(solution)/shard_map/ppermute | solution.py:34
  56.5 13.0 %collective-permute-start.18 = (bf16[16,128,256]{2,1,0:T(8,128)(2,1)S(1)}, bf16[16,128,256]{2,1,0:T(8,128)(2,1)S(1)}, u32[]{:S(2)}, u32[]{:S(2)}) collective-permute-start(bf16[16,128,256]{2,1,0:T(8,128)(2,1)S(1)} %shard_map.98.s0), channel_id=1, source_target_pairs={{0,2},{2,0},{4,6},{6,4},{8,10},{10,8},{12,14},{14,12},{16,18},{18,... | collective-permute-start | bytes 3145736 | tf_op jit(solution)/shard_map/ppermute | solution.py:29
  56.8 12.8 %collective-permute-start.17 = (bf16[64,2048]{1,0:T(8,128)(2,1)S(1)}, bf16[64,2048]{1,0:T(8,128)(2,1)S(1)}, u32[]{:S(2)}, u32[]{:S(2)}) collective-permute-start(bf16[64,2048]{1,0:T(8,128)(2,1)S(1)} %collective-permute-done.7.p0), channel_id=1, source_target_pairs={{0,64},{2,66},{4,68},{6,70},{8,72},{10,74},{12,76},{14,78},{16,80}... | collective-permute-start | bytes 786440 | tf_op jit(solution)/shard_map/ppermute | solution.py:29
  58.5 8.2 %collective-permute-start.16 = (bf16[32,2688]{1,0:T(8,128)(2,1)S(1)}, bf16[32,2688]{1,0:T(8,128)(2,1)S(1)}, u32[]{:S(2)}, u32[]{:S(2)}) collective-permute-start(bf16[32,2688]{1,0:T(8,128)(2,1)S(1)} %shard_map.99), channel_id=1, source_target_pairs={{0,5},{1,4},{2,7},{3,6},{4,1},{5,0},{6,3},{7,2},{8,13},{9,12},{10,... | collective-permute-start | bytes 516104 | tf_op jit(solution)/shard_map/ppermute | solution.py:34
  59.0 9.5 %collective-permute-start.15 = (bf16[32,2688]{1,0:T(8,128)(2,1)S(1)}, bf16[32,2688]{1,0:T(8,128)(2,1)S(1)}, u32[]{:S(2)}, u32[]{:S(2)}) collective-permute-start(bf16[32,2688]{1,0:T(8,128)(2,1)S(1)} %shard_map.99), channel_id=1, source_target_pairs={{0,4},{1,5},{2,6},{3,7},{4,0},{5,1},{6,2},{7,3},{8,12},{9,13},{10,... | collective-permute-start | bytes 516104 | tf_op jit(solution)/shard_map/ppermute | solution.py:34
  60.4 9.2 %collective-permute-start.14 = (bf16[32,2688]{1,0:T(8,128)(2,1)S(1)}, bf16[32,2688]{1,0:T(8,128)(2,1)S(1)}, u32[]{:S(2)}, u32[]{:S(2)}) collective-permute-start(bf16[32,2688]{1,0:T(8,128)(2,1)S(1)} %shard_map.99), channel_id=1, source_target_pairs={{0,1},{1,0},{2,3},{3,2},{4,5},{5,4},{6,7},{7,6},{8,9},{9,8},{10,11... | collective-permute-start | bytes 516104 | tf_op jit(solution)/shard_map/ppermute | solution.py:34
  69.7 2.2 %collective-permute-start.19 = (bf16[128,2688]{1,0:T(8,128)(2,1)S(1)}, bf16[128,2688]{1,0:T(8,128)(2,1)S(1)}, u32[]{:S(2)}, u32[]{:S(2)}) collective-permute-start(bf16[128,2688]{1,0:T(8,128)(2,1)S(1)} %constant_dynamic-update-slice_fusion.8.mine), channel_id=1, source_target_pairs={{0,2},{2,0},{4,6},{6,4},{8,10},{10,8},{12,14},{14,12},{16,18},{18,... | collective-permute-start | bytes 2064392 | tf_op jit(solution)/shard_map/ppermute | solution.py:29
  74.4 4.9 %collective-permute-start.23 = (bf16[16,128,256]{2,1,0:T(8,128)(2,1)S(1)}, bf16[16,128,256]{2,1,0:T(8,128)(2,1)S(1)}, u32[]{:S(2)}, u32[]{:S(2)}) collective-permute-start(bf16[16,128,256]{2,1,0:T(8,128)(2,1)S(1)} %shard_map.100.s2), channel_id=1, source_target_pairs={{0,2},{2,0},{4,6},{6,4},{8,10},{10,8},{12,14},{14,12},{16,18},{18,... | collective-permute-start | bytes 3145736 | tf_op jit(solution)/shard_map/ppermute | solution.py:29
  74.6 11.0 %collective-permute-start.20 = (bf16[64,2048]{1,0:T(8,128)(2,1)S(1)}, bf16[64,2048]{1,0:T(8,128)(2,1)S(1)}, u32[]{:S(2)}, u32[]{:S(2)}) collective-permute-start(bf16[64,2048]{1,0:T(8,128)(2,1)S(1)} %get-tuple-element.82), channel_id=1, source_target_pairs={{0,32},{2,34},{4,36},{6,38},{8,40},{10,42},{12,44},{14,46},{16,48}... | collective-permute-start | bytes 786440 | tf_op jit(solution)/shard_map/ppermute | solution.py:29
  74.9 16.1 %collective-permute-start.21 = (bf16[64,2048]{1,0:T(8,128)(2,1)S(1)}, bf16[64,2048]{1,0:T(8,128)(2,1)S(1)}, u32[]{:S(2)}, u32[]{:S(2)}) collective-permute-start(bf16[64,2048]{1,0:T(8,128)(2,1)S(1)} %get-tuple-element.83), channel_id=1, source_target_pairs={{0,64},{2,66},{4,68},{6,70},{8,72},{10,74},{12,76},{14,78},{16,80}... | collective-permute-start | bytes 786440 | tf_op jit(solution)/shard_map/ppermute | solution.py:29
  78.8 14.8 %collective-permute-start.22 = (bf16[64,2048]{1,0:T(8,128)(2,1)S(1)}, bf16[64,2048]{1,0:T(8,128)(2,1)S(1)}, u32[]{:S(2)}, u32[]{:S(2)}) collective-permute-start(bf16[64,2048]{1,0:T(8,128)(2,1)S(1)} %get-tuple-element.84), channel_id=1, source_target_pairs={{0,96},{2,98},{4,100},{6,102},{8,104},{10,106},{12,108},{14,110},{... | collective-permute-start | bytes 786440 | tf_op jit(solution)/shard_map/ppermute | solution.py:29
  93.8 6.6 %collective-permute-start.24 = (bf16[16,2048]{1,0:T(8,128)(2,1)S(1)}, bf16[16,2048]{1,0:T(8,128)(2,1)S(1)}, u32[]{:S(2)}, u32[]{:S(2)}) collective-permute-start(bf16[16,2048]{1,0:T(8,128)(2,1)S(1)} %get-tuple-element.106), channel_id=1, source_target_pairs={{0,8},{2,10},{4,12},{6,14},{8,0},{10,2},{12,4},{14,6},{16,24},{18,... | collective-permute-start | bytes 196616 | tf_op jit(solution)/shard_map/ppermute | solution.py:29
  94.5 7.3 %collective-permute-start.26 = (bf16[16,2048]{1,0:T(8,128)(2,1)S(1)}, bf16[16,2048]{1,0:T(8,128)(2,1)S(1)}, u32[]{:S(2)}, u32[]{:S(2)}) collective-permute-start(bf16[16,2048]{1,0:T(8,128)(2,1)S(1)} %get-tuple-element.107), channel_id=1, source_target_pairs={{0,24},{2,26},{4,28},{6,30},{8,16},{10,18},{12,20},{14,22},{16,8},... | collective-permute-start | bytes 196616 | tf_op jit(solution)/shard_map/ppermute | solution.py:29
  99.4 8.7 %collective-permute-start.25 = (bf16[16,2048]{1,0:T(8,128)(2,1)S(1)}, bf16[16,2048]{1,0:T(8,128)(2,1)S(1)}, u32[]{:S(2)}, u32[]{:S(2)}) collective-permute-start(bf16[16,2048]{1,0:T(8,128)(2,1)S(1)} %get-tuple-element.108), channel_id=1, source_target_pairs={{0,16},{2,18},{4,20},{6,22},{8,24},{10,26},{12,28},{14,30},{16,0},... | collective-permute-start | bytes 196616 | tf_op jit(solution)/shard_map/ppermute | solution.py:29
  108.1 5.5 %collective-permute-start.27 = (bf16[8,2048]{1,0:T(8,128)(2,1)S(1)}, bf16[8,2048]{1,0:T(8,128)(2,1)S(1)}, u32[]{:S(2)}, u32[]{:S(2)}) collective-permute-start(bf16[8,2048]{1,0:T(8,128)(2,1)S(1)} %slice.53), channel_id=1, source_target_pairs={{0,128},{2,130},{4,132},{6,134},{8,136},{10,138},{12,140},{14,142}... | collective-permute-start | bytes 98312 | tf_op jit(solution)/shard_map/ppermute | solution.py:29

commit v4 on v3

--- a/solution.py
+++ b/solution.py
@@ -211,8 +211,10 @@
     own_index = lax.dynamic_index_in_dim(all_index, row, axis=1, keepdims=False)
 
     tie = lax.optimization_barrier
-    shard = jnp.concatenate([activations, out_grad], axis=1)
-    pair = jnp.concatenate([shard, row_swap(shard, Y_MASK)], axis=0)
+    other = [row_swap(activations, Y_MASK), row_swap(out_grad, Y_MASK)]
+    pair = jnp.concatenate(
+        [jnp.concatenate([activations, out_grad], axis=1), jnp.concatenate(other, axis=1)], axis=0
+    )
     near = jnp.concatenate([pair] + [row_swap(pair, z_mask(i)) for i in range(1, 4)], axis=0)
     pieces = [near] + [row_swap(near, x_mask(i)) for i in range(1, 4)]
     mirror = row_swap(near, 2)
@@ -250,23 +252,19 @@
     sums = call(pair_kernel, [sds((32, 3 * HB), F32)] + [coded] * 3, [SMEM, VMEM, VMEM])(place, keep, got)
     sums = [sums[0]] + [square_swap(sums[i], i) for i in range(1, 4)]
 
-    pieces, mirror, keep = tie((pieces, mirror, keep))
-    mirror1, mirror3 = row_swap(mirror, x_mask(1)), row_swap(mirror, x_mask(3))
     prep = call(prep_kernel, sds((2 * DB, BLK, TOKENS), BF), [VMEM] * 4)
-    slab0 = prep(*pieces)
-    sums, mirror1, mirror3, slab0 = tie((sums, mirror1, mirror3, slab0))
-
+    mirror, keep = tie((mirror, keep))
+    mirror1, mirror2, mirror3 = [row_swap(mirror, x_mask(i)) for i in (1, 2, 3)]
+    slab0 = prep(*tie((pieces, sums[0]))[0])
+    sums, mirror1, slab0 = tie((sums, mirror1, slab0))
     share = call(act_kernel, sds((32, 3 * HB), BF), [VMEM] * 4)(*sums)
     mine = [share] + [square_swap(share, i) for i in range(1, 4)]
-    mirror, slab0, share = tie((mirror, slab0, share))
-    mirror2 = row_swap(mirror, x_mask(2))
     slab1 = row_swap(slab0, 1)
-    mine, mirror2, slab1 = tie((mine, mirror2, slab1))
-
+    mine, mirror2, mirror3 = tie((mine, mirror2, mirror3))
     mine = jnp.concatenate(mine, axis=0)
     theirs = row_swap(mine, 1)
     slab2 = prep(mirror, mirror1, mirror2, mirror3)
-    theirs, slab2 = tie((theirs, slab2))
+    theirs, slab2, slab1 = tie((theirs, slab2, slab1))
     outs = call(
         out_kernel,
         [sds((64, 2 * DQ), F32)] + [sds((64, 2 * DQ), BF)] * 3 + [sds((TOKENS, 3 * HB), BF)],
@@ -296,8 +294,9 @@
     last = total[: 2 * TG]
     for i in range(1, 4):
         last = last + row_swap(total[i * 2 * TG : (i + 1) * 2 * TG].astype(BF), z_mask(i)).astype(F32)
-    last = (last[:TG] + row_swap(last[TG:].astype(BF), Y_MASK).astype(F32)).astype(BF)
-    return last[:, :DQ], last[:, DQ:], grads.reshape(3, 1, 1, CAP, BLK, BLK)
+    got = row_swap(last[TG:].astype(BF), Y_MASK).astype(F32)
+    mixed_rows, input_grad = [(last[:TG, c] + got[:, c]).astype(BF) for c in (slice(0, DQ), slice(DQ, 2 * DQ))]
+    return mixed_rows, input_grad, grads.reshape(3, 1, 1, CAP, BLK, BLK)
 
 
 def solution(mesh):

time: 115 us -> 111 us (0.965)
  waiting for transfers between devices: 45 us -> 35.4 us
  starting transfers between devices: 42.1 us -> 46.9 us
  other arithmetic: 0.47 us -> 1.82 us
    ppermute x6, waiting for transfers between devices: 11.8 us -> 6.19 us  [square_swap(): lax.ppermute(value, ('row', 'col'), [(i, i ^ mask) for i in range(256)])]
    ppermute x22 -> x23, starting transfers between devices: 35.1 us -> 39.8 us  [row_swap(): return lax.ppermute(value, 'row', [(i, i ^ mask) for i in range(128)])]
    ppermute x22 -> x23, waiting for transfers between devices: 33.2 us -> 29.2 us  [row_swap(): return lax.ppermute(value, 'row', [(i, i ^ mask) for i in range(128)])]
    unnamed x15 -> x17, local copies, waits for them, and re-layouts: 5.06 us -> 5.74 us
  transfers between devices with their start and end apart: 28 -> 29, of which waited for: 18 -> 15; matrix products, arithmetic and copies ran while one was open for 2% -> 3% of each run, Pallas kernels for 11% -> 12%
where the time goes in v4:
time: 111 us; the launch traced here: 110 us
  starting transfers between devices  46.9 us (42%)
  waiting for transfers between devices  35.4 us (32%)
  Pallas kernels  17.4 us (16%)
  local copies, waits for them, and re-layouts  7.58 us (7%)
  other arithmetic  1.82 us (2%)
    ppermute x23, starting transfers between devices, row_swap(): return lax.ppermute(value, 'row', [(i, i ^ mask) for i in range(128)])  39.8 us
    ppermute x23, waiting for transfers between devices, row_swap(): return lax.ppermute(value, 'row', [(i, i ^ mask) for i in range(128)])  29.2 us
    ppermute x6, starting transfers between devices, square_swap(): lax.ppermute(value, ('row', 'col'), [(i, i ^ mask) for i in range(256)])  7.15 us
    pallas_call x1, Pallas kernels, body(): call(grad_kernel, sds((3, CAP, BLK, BLK), BF), [SMEM] + [VMEM] * 5, out_s...  6.21 us
    ppermute x6, waiting for transfers between devices, square_swap(): lax.ppermute(value, ('row', 'col'), [(i, i ^ mask) for i in range(256)])  6.19 us
    unnamed x17, local copies, waits for them, and re-layouts  5.74 us
    pallas_call x2, Pallas kernels, partial(): call(functools.partial(partial_kernel, other=other), half, [SMEM] + [VMEM...  3.77 us
    pallas_call x1, Pallas kernels, body(): call(dense_kernel, wide, [SMEM] + [VMEM] * 3)  3.45 us
  transfers between devices with their start and end apart: 29, of which 15 were waited for; matrix products, arithmetic and copies ran while one was open for 3% of the time, Pallas kernels for 12%

profile of v4, /device:TPU:32, one launch (start us, length us, event | category | flops | bytes accessed | tf_op | source)
XLA Modules:
  0.0 110.1 jit_solution(12589126819214686523)
XLA Ops:
  0.6 3.3 %collective-permute-start = (bf16[8,1024]{1,0:T(8,128)(2,1)}, bf16[8,1024]{1,0:T(8,128)(2,1)S(1)}, u32[]{:S(2)}, u32[]{:S(2)}) collective-permute-start(bf16[8,1024]{1,0:T(8,128)(2,1)} %param.7), channel_id=1, source_target_pairs={{0,128},{2,130},{4,132},{6,134},{8,136},{10,138},{12,140},{14,142}... | collective-permute-start | bytes 49160 | tf_op jit(solution)/shard_map/ppermute | solution.py:29
  7.1 2.2 %collective-permute-done.1 = bf16[8,1024]{1,0:T(8,128)(2,1)S(1)} collective-permute-done((bf16[8,1024]{1,0:T(8,128)(2,1)}, bf16[8,1024]{1,0:T(8,128)(2,1)S(1)}, u32[]{:S(2)}, u32[]{:S(2)}) %collective-permute-start.1) | collective-permute-done | bytes 16416 | tf_op jit(solution)/shard_map/ppermute | solution.py:29
  10.1 5.4 %collective-permute-start.4 = (bf16[16,2048]{1,0:T(8,128)(2,1)S(1)}, bf16[16,2048]{1,0:T(8,128)(2,1)S(1)}, u32[]{:S(2)}, u32[]{:S(2)}) collective-permute-start(bf16[16,2048]{1,0:T(8,128)(2,1)S(1)} %maximum_maximum_fusion), channel_id=1, source_target_pairs={{0,24},{2,26},{4,28},{6,30},{8,16},{10,18},{12,20},{14,22},{16,8},... | collective-permute-start | bytes 196616 | tf_op jit(solution)/shard_map/ppermute | solution.py:29
  15.5 1.4 %collective-permute-start.3 = (bf16[16,2048]{1,0:T(8,128)(2,1)S(1)}, bf16[16,2048]{1,0:T(8,128)(2,1)S(1)}, u32[]{:S(2)}, u32[]{:S(2)}) collective-permute-start(bf16[16,2048]{1,0:T(8,128)(2,1)S(1)} %maximum_maximum_fusion), channel_id=1, source_target_pairs={{0,16},{2,18},{4,20},{6,22},{8,24},{10,26},{12,28},{14,30},{16,0},... | collective-permute-start | bytes 196616 | tf_op jit(solution)/shard_map/ppermute | solution.py:29
  18.0 4.3 %collective-permute-done.2 = bf16[16,2048]{1,0:T(8,128)(2,1)S(1)} collective-permute-done((bf16[16,2048]{1,0:T(8,128)(2,1)S(1)}, bf16[16,2048]{1,0:T(8,128)(2,1)S(1)}, u32[]{:S(2)}, u32[]{:S(2)}) %collective-permute-start.2) | collective-permute-done | bytes 65568 | tf_op jit(solution)/shard_map/ppermute | solution.py:29
  22.2 1.7 %collective-permute-done.3 = bf16[16,2048]{1,0:T(8,128)(2,1)S(1)} collective-permute-done((bf16[16,2048]{1,0:T(8,128)(2,1)S(1)}, bf16[16,2048]{1,0:T(8,128)(2,1)S(1)}, u32[]{:S(2)}, u32[]{:S(2)}) %collective-permute-start.3) | collective-permute-done | bytes 65568 | tf_op jit(solution)/shard_map/ppermute | solution.py:29
  25.2 2.8 %collective-permute-start.7 = (bf16[64,2048]{1,0:T(8,128)(2,1)S(1)}, bf16[64,2048]{1,0:T(8,128)(2,1)S(1)}, u32[]{:S(2)}, u32[]{:S(2)}) collective-permute-start(bf16[64,2048]{1,0:T(8,128)(2,1)S(1)} %constant_dynamic-update-slice_fusion.p0), channel_id=1, source_target_pairs={{0,96},{2,98},{4,100},{6,102},{8,104},{10,106},{12,108},{14,110},{... | collective-permute-start | bytes 786440 | tf_op jit(solution)/shard_map/ppermute | solution.py:29
  29.7 1.4 %copy-done.1 = bf16[1,1,48,128,128]{4,3,2,1,0:T(8,128)(2,1)S(1)} copy-done((bf16[1,1,48,128,128]{4,3,2,1,0:T(8,128)(2,1)S(1)}, bf16[1,1,48,128,128]{4,3,2,1,0:T(8,128)(2,1)}, u32[]{:S(2)}) %copy-start.1) | copy-done | bytes 1572888
  31.2 1.4 %copy-done.2 = bf16[1,1,48,128,128]{4,3,2,1,0:T(8,128)(2,1)S(1)} copy-done((bf16[1,1,48,128,128]{4,3,2,1,0:T(8,128)(2,1)S(1)}, bf16[1,1,48,128,128]{4,3,2,1,0:T(8,128)(2,1)}, u32[]{:S(2)}) %copy-start.2) | copy-done | bytes 1572888
  32.6 1.4 %copy-done.3 = bf16[1,1,48,128,128]{4,3,2,1,0:T(8,128)(2,1)S(1)} copy-done((bf16[1,1,48,128,128]{4,3,2,1,0:T(8,128)(2,1)S(1)}, bf16[1,1,48,128,128]{4,3,2,1,0:T(8,128)(2,1)}, u32[]{:S(2)}) %copy-start.3) | copy-done | bytes 1572888
  34.0 3.4 %shard_map.94 = (bf16[1024,896]{1,0:T(8,128)(2,1)S(1)}, bf16[1024,896]{1,0:T(8,128)(2,1)S(1)}, bf16[896,1024]{1,0:T(8,128)(2,1)S(1)}) custom-call(s32[3,48]{1,0:T(4,128)S(1)} %dynamic-slice_reduce_fusion.index_ref, bf16[48,128,128]{2,1,0:T(8,128)(2,1)S(1)} %bitcast.12, bf16[48,128,128]{2,1,0:T(8,128)(2,1)S(1)} %bitcast.13, bf16[48,128,128]{2,1,0:T(8,128)(2,1)S(1)} %bitcast.14), custom_call_target="tpu_custom_call" | custom-call | tf_op jit(solution)/shard_map/pallas_call | solution.py:223
  37.8 1.9 %shard_map.96 = f32[128,2688]{1,0:T(8,128)S(1)} custom-call(s32[2]{0:T(128)S(1)} %pad_add_fusion.place_ref, bf16[64,2048]{1,0:T(8,128)(2,1)S(1)} %constant_dynamic-update-slice_fusion.p0, bf16[64,2048]{1,0:T(8,128)(2,1)S(1)} %collective-permute-done.5.p1, bf16[64,2048]{1,0:T(8,128)(2,1)S(1)} %collective-permute-done.6.p2, ...), custom_call_target="tpu_custom_call" | custom-call | tf_op jit(solution)/shard_map/pallas_call | solution.py:241
  39.8 1.9 %shard_map.95.keep_ref = f32[128,2688]{1,0:T(8,128)S(1)} custom-call(s32[2]{0:T(128)S(1)} %pad_add_fusion.place_ref, bf16[64,2048]{1,0:T(8,128)(2,1)S(1)} %constant_dynamic-update-slice_fusion.p0, bf16[64,2048]{1,0:T(8,128)(2,1)S(1)} %collective-permute-done.5.p1, bf16[64,2048]{1,0:T(8,128)(2,1)S(1)} %collective-permute-done.6.p2, ...), custom_call_target="tpu_custom_call" | custom-call | tf_op jit(solution)/shard_map/pallas_call | solution.py:241
  41.7 1.6 %collective-permute-start.13 = (bf16[64,2048]{1,0:T(8,128)(2,1)S(1)}, bf16[64,2048]{1,0:T(8,128)(2,1)S(1)}, u32[]{:S(2)}, u32[]{:S(2)}) collective-permute-start(bf16[64,2048]{1,0:T(8,128)(2,1)S(1)} %collective-permute-done.8.p0), channel_id=1, source_target_pairs={{0,32},{2,34},{4,36},{6,38},{8,40},{10,42},{12,44},{14,46},{16,48}... | collective-permute-start | bytes 786440 | tf_op jit(solution)/shard_map/ppermute | solution.py:29
  45.6 2.1 %collective-permute-start.12 = (s16[32,2816]{1,0:T(8,128)(2,1)S(1)}, s16[32,2816]{1,0:T(8,128)(2,1)S(1)}, u32[]{:S(2)}, u32[]{:S(2)}) collective-permute-start(s16[32,2816]{1,0:T(8,128)(2,1)S(1)} %get-tuple-element.57), channel_id=1, source_target_pairs={{0,5},{1,4},{2,7},{3,6},{4,1},{5,0},{6,3},{7,2},{8,13},{9,12},{10,... | collective-permute-start | bytes 540680 | tf_op jit(solution)/shard_map/ppermute | solution.py:34
  47.7 2.4 %collective-permute-start.18 = (bf16[64,2048]{1,0:T(8,128)(2,1)S(1)}, bf16[64,2048]{1,0:T(8,128)(2,1)S(1)}, u32[]{:S(2)}, u32[]{:S(2)}) collective-permute-start(bf16[64,2048]{1,0:T(8,128)(2,1)S(1)} %collective-permute-done.8.p0), channel_id=1, source_target_pairs={{0,96},{2,98},{4,100},{6,102},{8,104},{10,106},{12,108},{14,110},{... | collective-permute-start | bytes 786440 | tf_op jit(solution)/shard_map/ppermute | solution.py:29
  50.5 3.1 %collective-permute-start.17 = (bf16[64,2048]{1,0:T(8,128)(2,1)S(1)}, bf16[64,2048]{1,0:T(8,128)(2,1)S(1)}, u32[]{:S(2)}, u32[]{:S(2)}) collective-permute-start(bf16[64,2048]{1,0:T(8,128)(2,1)S(1)} %collective-permute-done.8.p0), channel_id=1, source_target_pairs={{0,64},{2,66},{4,68},{6,70},{8,72},{10,74},{12,76},{14,78},{16,80}... | collective-permute-start | bytes 786440 | tf_op jit(solution)/shard_map/ppermute | solution.py:29
  53.8 2.1 %collective-permute-done.12.a3 = s16[32,2816]{1,0:T(8,128)(2,1)S(1)} collective-permute-done((s16[32,2816]{1,0:T(8,128)(2,1)S(1)}, s16[32,2816]{1,0:T(8,128)(2,1)S(1)}, u32[]{:S(2)}, u32[]{:S(2)}) %collective-permute-start.12) | collective-permute-done | bytes 180256 | tf_op jit(solution)/shard_map/ppermute | solution.py:34
  58.4 1.3 %collective-permute-start.14 = (bf16[32,2688]{1,0:T(8,128)(2,1)S(1)}, bf16[32,2688]{1,0:T(8,128)(2,1)S(1)}, u32[]{:S(2)}, u32[]{:S(2)}) collective-permute-start(bf16[32,2688]{1,0:T(8,128)(2,1)S(1)} %shard_map.99), channel_id=1, source_target_pairs={{0,1},{1,0},{2,3},{3,2},{4,5},{5,4},{6,7},{7,6},{8,9},{9,8},{10,11... | collective-permute-start | bytes 516104 | tf_op jit(solution)/shard_map/ppermute | solution.py:34
  59.7 2.4 %collective-permute-done.18.p3 = bf16[64,2048]{1,0:T(8,128)(2,1)S(1)} collective-permute-done((bf16[64,2048]{1,0:T(8,128)(2,1)S(1)}, bf16[64,2048]{1,0:T(8,128)(2,1)S(1)}, u32[]{:S(2)}, u32[]{:S(2)}) %collective-permute-start.18) | collective-permute-done | bytes 262176 | tf_op jit(solution)/shard_map/ppermute | solution.py:29
  62.1 2.2 %collective-permute-done.16 = bf16[32,2688]{1,0:T(8,128)(2,1)S(1)} collective-permute-done((bf16[32,2688]{1,0:T(8,128)(2,1)S(1)}, bf16[32,2688]{1,0:T(8,128)(2,1)S(1)}, u32[]{:S(2)}, u32[]{:S(2)}) %collective-permute-start.16) | collective-permute-done | bytes 172064 | tf_op jit(solution)/shard_map/ppermute | solution.py:34
  66.6 1.9 %collective-permute-done.19.theirs = bf16[128,2688]{1,0:T(8,128)(2,1)S(1)} collective-permute-done((bf16[128,2688]{1,0:T(8,128)(2,1)S(1)}, bf16[128,2688]{1,0:T(8,128)(2,1)S(1)}, u32[]{:S(2)}, u32[]{:S(2)}) %collective-permute-start.19) | collective-permute-done | bytes 688160 | tf_op jit(solution)/shard_map/ppermute | solution.py:29
  68.5 2.5 %shard_map.101 = (f32[64,2048]{1,0:T(8,128)S(1)}, bf16[64,2048]{1,0:T(8,128)(2,1)S(1)}, bf16[64,2048]{1,0:T(8,128)(2,1)S(1)}, bf16[64,2048]{1,0:T(8,128)(2,1)S(1)}, bf16[256,2688]{1,0:T(8,128)(2,1)S(1)}) custom-call(s32[2]{0:T(128)S(1)} %pad_add_fusion.place_ref, bf16[128,2688]{1,0:T(8,128)(2,1)S(1)} %constant_dynamic-update-slice_fusion.6.mine, ...), custom_call_target="tpu_custom_call" | custom-call | tf_op jit(solution)/shard_map/pallas_call | solution.py:268
  72.2 2.7 %collective-permute-start.22 = (bf16[64,2048]{1,0:T(8,128)(2,1)S(1)}, bf16[64,2048]{1,0:T(8,128)(2,1)S(1)}, u32[]{:S(2)}, u32[]{:S(2)}) collective-permute-start(bf16[64,2048]{1,0:T(8,128)(2,1)S(1)} %get-tuple-element.79), channel_id=1, source_target_pairs={{0,64},{2,66},{4,68},{6,70},{8,72},{10,74},{12,76},{14,78},{16,80}... | collective-permute-start | bytes 786440 | tf_op jit(solution)/shard_map/ppermute | solution.py:29
  75.9 6.2 %shard_map.102 = bf16[3,48,128,128]{3,2,1,0:T(8,128)(2,1)} custom-call(s32[3,48]{1,0:T(4,128)S(1)} %select_reduce_fusion.code_ref, bf16[256,2688]{1,0:T(8,128)(2,1)S(1)} %get-tuple-element.84.full, bf16[16,128,256]{2,1,0:T(8,128)(2,1)S(1)} %shard_map.98.s0, bf16[16,128,256]{2,1,0:T(8,128)(2,1)S(1)} %collective-permute-done.20.s1, ...), custom_call_target="tpu_custom_call" | custom-call | tf_op jit(solution)/shard_map/pallas_call | solution.py:278
  82.1 5.0 %collective-permute-done.22 = bf16[64,2048]{1,0:T(8,128)(2,1)S(1)} collective-permute-done((bf16[64,2048]{1,0:T(8,128)(2,1)S(1)}, bf16[64,2048]{1,0:T(8,128)(2,1)S(1)}, u32[]{:S(2)}, u32[]{:S(2)}) %collective-permute-start.22) | collective-permute-done | bytes 262176 | tf_op jit(solution)/shard_map/ppermute | solution.py:29
  87.1 2.6 %collective-permute-done.23 = bf16[64,2048]{1,0:T(8,128)(2,1)S(1)} collective-permute-done((bf16[64,2048]{1,0:T(8,128)(2,1)S(1)}, bf16[64,2048]{1,0:T(8,128)(2,1)S(1)}, u32[]{:S(2)}, u32[]{:S(2)}) %collective-permute-start.23) | collective-permute-done | bytes 262176 | tf_op jit(solution)/shard_map/ppermute | solution.py:29
  91.1 3.2 %collective-permute-start.27 = (bf16[16,2048]{1,0:T(8,128)(2,1)S(1)}, bf16[16,2048]{1,0:T(8,128)(2,1)S(1)}, u32[]{:S(2)}, u32[]{:S(2)}) collective-permute-start(bf16[16,2048]{1,0:T(8,128)(2,1)S(1)} %get-tuple-element.103), channel_id=1, source_target_pairs={{0,24},{2,26},{4,28},{6,30},{8,16},{10,18},{12,20},{14,22},{16,8},... | collective-permute-start | bytes 196616 | tf_op jit(solution)/shard_map/ppermute | solution.py:29
  94.3 2.1 %collective-permute-start.26 = (bf16[16,2048]{1,0:T(8,128)(2,1)S(1)}, bf16[16,2048]{1,0:T(8,128)(2,1)S(1)}, u32[]{:S(2)}, u32[]{:S(2)}) collective-permute-start(bf16[16,2048]{1,0:T(8,128)(2,1)S(1)} %get-tuple-element.104), channel_id=1, source_target_pairs={{0,16},{2,18},{4,20},{6,22},{8,24},{10,26},{12,28},{14,30},{16,0},... | collective-permute-start | bytes 196616 | tf_op jit(solution)/shard_map/ppermute | solution.py:29
  97.6 5.6 %collective-permute-done.26 = bf16[16,2048]{1,0:T(8,128)(2,1)S(1)} collective-permute-done((bf16[16,2048]{1,0:T(8,128)(2,1)S(1)}, bf16[16,2048]{1,0:T(8,128)(2,1)S(1)}, u32[]{:S(2)}, u32[]{:S(2)}) %collective-permute-start.26) | collective-permute-done | bytes 65568 | tf_op jit(solution)/shard_map/ppermute | solution.py:29
  103.3 4.3 %collective-permute-start.28 = (bf16[8,2048]{1,0:T(8,128)(2,1)S(1)}, bf16[8,2048]{1,0:T(8,128)(2,1)S(1)}, u32[]{:S(2)}, u32[]{:S(2)}) collective-permute-start(bf16[8,2048]{1,0:T(8,128)(2,1)S(1)} %slice.63), channel_id=1, source_target_pairs={{0,128},{2,130},{4,132},{6,134},{8,136},{10,138},{12,140},{14,142}... | collective-permute-start | bytes 98312 | tf_op jit(solution)/shard_map/ppermute | solution.py:29
  107.5 1.9 %collective-permute-done.28 = bf16[8,2048]{1,0:T(8,128)(2,1)S(1)} collective-permute-done((bf16[8,2048]{1,0:T(8,128)(2,1)S(1)}, bf16[8,2048]{1,0:T(8,128)(2,1)S(1)}, u32[]{:S(2)}, u32[]{:S(2)}) %collective-permute-start.28) | collective-permute-done | bytes 32800 | tf_op jit(solution)/shard_map/ppermute | solution.py:29
  (75 shorter events, 21.5 us)
Async XLA Ops:
  0.6 4.5 %copy-start = (s32[3,128,2,48]{1,3,2,0:T(8,128)S(1)}, s32[3,128,2,48]{1,3,2,0:T(8,128)}, u32[]{:S(2)}) copy-start(s32[3,128,2,48]{1,3,2,0:T(8,128)} %param.12) | copy-start | bytes 442372
  0.6 6.5 %collective-permute-start = (bf16[8,1024]{1,0:T(8,128)(2,1)}, bf16[8,1024]{1,0:T(8,128)(2,1)S(1)}, u32[]{:S(2)}, u32[]{:S(2)}) collective-permute-start(bf16[8,1024]{1,0:T(8,128)(2,1)} %param.7), channel_id=1, source_target_pairs={{0,128},{2,130},{4,132},{6,134},{8,136},{10,138},{12,140},{14,142}... | collective-permute-start | bytes 49160 | tf_op jit(solution)/shard_map/ppermute | solution.py:29
  3.9 5.5 %collective-permute-start.1 = (bf16[8,1024]{1,0:T(8,128)(2,1)}, bf16[8,1024]{1,0:T(8,128)(2,1)S(1)}, u32[]{:S(2)}, u32[]{:S(2)}) collective-permute-start(bf16[8,1024]{1,0:T(8,128)(2,1)} %param.8), channel_id=1, source_target_pairs={{0,128},{2,130},{4,132},{6,134},{8,136},{10,138},{12,140},{14,142}... | collective-permute-start | bytes 49160 | tf_op jit(solution)/shard_map/ppermute | solution.py:29
  10.1 13.8 %collective-permute-start.4 = (bf16[16,2048]{1,0:T(8,128)(2,1)S(1)}, bf16[16,2048]{1,0:T(8,128)(2,1)S(1)}, u32[]{:S(2)}, u32[]{:S(2)}) collective-permute-start(bf16[16,2048]{1,0:T(8,128)(2,1)S(1)} %maximum_maximum_fusion), channel_id=1, source_target_pairs={{0,24},{2,26},{4,28},{6,30},{8,16},{10,18},{12,20},{14,22},{16,8},... | collective-permute-start | bytes 196616 | tf_op jit(solution)/shard_map/ppermute | solution.py:29
  15.5 8.4 %collective-permute-start.3 = (bf16[16,2048]{1,0:T(8,128)(2,1)S(1)}, bf16[16,2048]{1,0:T(8,128)(2,1)S(1)}, u32[]{:S(2)}, u32[]{:S(2)}) collective-permute-start(bf16[16,2048]{1,0:T(8,128)(2,1)S(1)} %maximum_maximum_fusion), channel_id=1, source_target_pairs={{0,16},{2,18},{4,20},{6,22},{8,24},{10,26},{12,28},{14,30},{16,0},... | collective-permute-start | bytes 196616 | tf_op jit(solution)/shard_map/ppermute | solution.py:29
  17.0 5.3 %collective-permute-start.2 = (bf16[16,2048]{1,0:T(8,128)(2,1)S(1)}, bf16[16,2048]{1,0:T(8,128)(2,1)S(1)}, u32[]{:S(2)}, u32[]{:S(2)}) collective-permute-start(bf16[16,2048]{1,0:T(8,128)(2,1)S(1)} %maximum_maximum_fusion), channel_id=1, source_target_pairs={{0,8},{2,10},{4,12},{6,14},{8,0},{10,2},{12,4},{14,6},{16,24},{18,... | collective-permute-start | bytes 196616 | tf_op jit(solution)/shard_map/ppermute | solution.py:29
  24.0 13.7 %collective-permute-start.8 = (bf16[64,2048]{1,0:T(8,128)(2,1)S(1)}, bf16[64,2048]{1,0:T(8,128)(2,1)S(1)}, u32[]{:S(2)}, u32[]{:S(2)}) collective-permute-start(bf16[64,2048]{1,0:T(8,128)(2,1)S(1)} %constant_dynamic-update-slice_fusion.p0), channel_id=1, source_target_pairs={{0,4},{2,6},{4,0},{6,2},{8,12},{10,14},{12,8},{14,10},{16,20},{18,... | collective-permute-start | bytes 786440 | tf_op jit(solution)/shard_map/ppermute | solution.py:29
  25.2 12.5 %collective-permute-start.7 = (bf16[64,2048]{1,0:T(8,128)(2,1)S(1)}, bf16[64,2048]{1,0:T(8,128)(2,1)S(1)}, u32[]{:S(2)}, u32[]{:S(2)}) collective-permute-start(bf16[64,2048]{1,0:T(8,128)(2,1)S(1)} %constant_dynamic-update-slice_fusion.p0), channel_id=1, source_target_pairs={{0,96},{2,98},{4,100},{6,102},{8,104},{10,106},{12,108},{14,110},{... | collective-permute-start | bytes 786440 | tf_op jit(solution)/shard_map/ppermute | solution.py:29
  28.0 9.7 %collective-permute-start.6 = (bf16[64,2048]{1,0:T(8,128)(2,1)S(1)}, bf16[64,2048]{1,0:T(8,128)(2,1)S(1)}, u32[]{:S(2)}, u32[]{:S(2)}) collective-permute-start(bf16[64,2048]{1,0:T(8,128)(2,1)S(1)} %constant_dynamic-update-slice_fusion.p0), channel_id=1, source_target_pairs={{0,64},{2,66},{4,68},{6,70},{8,72},{10,74},{12,76},{14,78},{16,80}... | collective-permute-start | bytes 786440 | tf_op jit(solution)/shard_map/ppermute | solution.py:29
  28.8 9.0 %collective-permute-start.5 = (bf16[64,2048]{1,0:T(8,128)(2,1)S(1)}, bf16[64,2048]{1,0:T(8,128)(2,1)S(1)}, u32[]{:S(2)}, u32[]{:S(2)}) collective-permute-start(bf16[64,2048]{1,0:T(8,128)(2,1)S(1)} %constant_dynamic-update-slice_fusion.p0), channel_id=1, source_target_pairs={{0,32},{2,34},{4,36},{6,38},{8,40},{10,42},{12,44},{14,46},{16,48}... | collective-permute-start | bytes 786440 | tf_op jit(solution)/shard_map/ppermute | solution.py:29
  29.7 1.4 %copy-start.1 = (bf16[1,1,48,128,128]{4,3,2,1,0:T(8,128)(2,1)S(1)}, bf16[1,1,48,128,128]{4,3,2,1,0:T(8,128)(2,1)}, u32[]{:S(2)}) copy-start(bf16[1,1,48,128,128]{4,3,2,1,0:T(8,128)(2,1)} %param.9) | copy-start | bytes 4718596
  32.6 1.4 %copy-start.3 = (bf16[1,1,48,128,128]{4,3,2,1,0:T(8,128)(2,1)S(1)}, bf16[1,1,48,128,128]{4,3,2,1,0:T(8,128)(2,1)}, u32[]{:S(2)}) copy-start(bf16[1,1,48,128,128]{4,3,2,1,0:T(8,128)(2,1)} %param.11) | copy-start | bytes 4718596
  39.7 3.6 %collective-permute-start.9 = (f32[128,2688]{1,0:T(8,128)S(1)}, f32[128,2688]{1,0:T(8,128)S(1)}, u32[]{:S(2)}, u32[]{:S(2)}) collective-permute-start(f32[128,2688]{1,0:T(8,128)S(1)} %shard_map.96), channel_id=1, source_target_pairs={{0,2},{2,0},{4,6},{6,4},{8,10},{10,8},{12,14},{14,12},{16,18},{18,... | collective-permute-start | bytes 4128776 | tf_op jit(solution)/shard_map/ppermute | solution.py:29
  41.7 8.8 %collective-permute-start.13 = (bf16[64,2048]{1,0:T(8,128)(2,1)S(1)}, bf16[64,2048]{1,0:T(8,128)(2,1)S(1)}, u32[]{:S(2)}, u32[]{:S(2)}) collective-permute-start(bf16[64,2048]{1,0:T(8,128)(2,1)S(1)} %collective-permute-done.8.p0), channel_id=1, source_target_pairs={{0,32},{2,34},{4,36},{6,38},{8,40},{10,42},{12,44},{14,46},{16,48}... | collective-permute-start | bytes 786440 | tf_op jit(solution)/shard_map/ppermute | solution.py:29
  44.1 9.7 %collective-permute-start.10 = (s16[32,2816]{1,0:T(8,128)(2,1)S(1)}, s16[32,2816]{1,0:T(8,128)(2,1)S(1)}, u32[]{:S(2)}, u32[]{:S(2)}) collective-permute-start(s16[32,2816]{1,0:T(8,128)(2,1)S(1)} %get-tuple-element.55), channel_id=1, source_target_pairs={{0,1},{1,0},{2,3},{3,2},{4,5},{5,4},{6,7},{7,6},{8,9},{9,8},{10,11... | collective-permute-start | bytes 540680 | tf_op jit(solution)/shard_map/ppermute | solution.py:34
  44.9 8.9 %collective-permute-start.11 = (s16[32,2816]{1,0:T(8,128)(2,1)S(1)}, s16[32,2816]{1,0:T(8,128)(2,1)S(1)}, u32[]{:S(2)}, u32[]{:S(2)}) collective-permute-start(s16[32,2816]{1,0:T(8,128)(2,1)S(1)} %get-tuple-element.56), channel_id=1, source_target_pairs={{0,4},{1,5},{2,6},{3,7},{4,0},{5,1},{6,2},{7,3},{8,12},{9,13},{10,... | collective-permute-start | bytes 540680 | tf_op jit(solution)/shard_map/ppermute | solution.py:34
  45.6 10.3 %collective-permute-start.12 = (s16[32,2816]{1,0:T(8,128)(2,1)S(1)}, s16[32,2816]{1,0:T(8,128)(2,1)S(1)}, u32[]{:S(2)}, u32[]{:S(2)}) collective-permute-start(s16[32,2816]{1,0:T(8,128)(2,1)S(1)} %get-tuple-element.57), channel_id=1, source_target_pairs={{0,5},{1,4},{2,7},{3,6},{4,1},{5,0},{6,3},{7,2},{8,13},{9,12},{10,... | collective-permute-start | bytes 540680 | tf_op jit(solution)/shard_map/ppermute | solution.py:34
  47.7 14.4 %collective-permute-start.18 = (bf16[64,2048]{1,0:T(8,128)(2,1)S(1)}, bf16[64,2048]{1,0:T(8,128)(2,1)S(1)}, u32[]{:S(2)}, u32[]{:S(2)}) collective-permute-start(bf16[64,2048]{1,0:T(8,128)(2,1)S(1)} %collective-permute-done.8.p0), channel_id=1, source_target_pairs={{0,96},{2,98},{4,100},{6,102},{8,104},{10,106},{12,108},{14,110},{... | collective-permute-start | bytes 786440 | tf_op jit(solution)/shard_map/ppermute | solution.py:29
  50.5 11.7 %collective-permute-start.17 = (bf16[64,2048]{1,0:T(8,128)(2,1)S(1)}, bf16[64,2048]{1,0:T(8,128)(2,1)S(1)}, u32[]{:S(2)}, u32[]{:S(2)}) collective-permute-start(bf16[64,2048]{1,0:T(8,128)(2,1)S(1)} %collective-permute-done.8.p0), channel_id=1, source_target_pairs={{0,64},{2,66},{4,68},{6,70},{8,72},{10,74},{12,76},{14,78},{16,80}... | collective-permute-start | bytes 786440 | tf_op jit(solution)/shard_map/ppermute | solution.py:29
  56.1 8.2 %collective-permute-start.16 = (bf16[32,2688]{1,0:T(8,128)(2,1)S(1)}, bf16[32,2688]{1,0:T(8,128)(2,1)S(1)}, u32[]{:S(2)}, u32[]{:S(2)}) collective-permute-start(bf16[32,2688]{1,0:T(8,128)(2,1)S(1)} %shard_map.99), channel_id=1, source_target_pairs={{0,5},{1,4},{2,7},{3,6},{4,1},{5,0},{6,3},{7,2},{8,13},{9,12},{10,... | collective-permute-start | bytes 516104 | tf_op jit(solution)/shard_map/ppermute | solution.py:34
  57.0 8.4 %collective-permute-start.15 = (bf16[32,2688]{1,0:T(8,128)(2,1)S(1)}, bf16[32,2688]{1,0:T(8,128)(2,1)S(1)}, u32[]{:S(2)}, u32[]{:S(2)}) collective-permute-start(bf16[32,2688]{1,0:T(8,128)(2,1)S(1)} %shard_map.99), channel_id=1, source_target_pairs={{0,4},{1,5},{2,6},{3,7},{4,0},{5,1},{6,2},{7,3},{8,12},{9,13},{10,... | collective-permute-start | bytes 516104 | tf_op jit(solution)/shard_map/ppermute | solution.py:34
  58.4 7.8 %collective-permute-start.14 = (bf16[32,2688]{1,0:T(8,128)(2,1)S(1)}, bf16[32,2688]{1,0:T(8,128)(2,1)S(1)}, u32[]{:S(2)}, u32[]{:S(2)}) collective-permute-start(bf16[32,2688]{1,0:T(8,128)(2,1)S(1)} %shard_map.99), channel_id=1, source_target_pairs={{0,1},{1,0},{2,3},{3,2},{4,5},{5,4},{6,7},{7,6},{8,9},{9,8},{10,11... | collective-permute-start | bytes 516104 | tf_op jit(solution)/shard_map/ppermute | solution.py:34
  62.1 6.4 %collective-permute-start.20 = (bf16[16,128,256]{2,1,0:T(8,128)(2,1)S(1)}, bf16[16,128,256]{2,1,0:T(8,128)(2,1)S(1)}, u32[]{:S(2)}, u32[]{:S(2)}) collective-permute-start(bf16[16,128,256]{2,1,0:T(8,128)(2,1)S(1)} %shard_map.98.s0), channel_id=1, source_target_pairs={{0,2},{2,0},{4,6},{6,4},{8,10},{10,8},{12,14},{14,12},{16,18},{18,... | collective-permute-start | bytes 3145736 | tf_op jit(solution)/shard_map/ppermute | solution.py:29
  66.3 2.2 %collective-permute-start.19 = (bf16[128,2688]{1,0:T(8,128)(2,1)S(1)}, bf16[128,2688]{1,0:T(8,128)(2,1)S(1)}, u32[]{:S(2)}, u32[]{:S(2)}) collective-permute-start(bf16[128,2688]{1,0:T(8,128)(2,1)S(1)} %constant_dynamic-update-slice_fusion.6.mine), channel_id=1, source_target_pairs={{0,2},{2,0},{4,6},{6,4},{8,10},{10,8},{12,14},{14,12},{16,18},{18,... | collective-permute-start | bytes 2064392 | tf_op jit(solution)/shard_map/ppermute | solution.py:29
  71.0 4.9 %collective-permute-start.24 = (bf16[16,128,256]{2,1,0:T(8,128)(2,1)S(1)}, bf16[16,128,256]{2,1,0:T(8,128)(2,1)S(1)}, u32[]{:S(2)}, u32[]{:S(2)}) collective-permute-start(bf16[16,128,256]{2,1,0:T(8,128)(2,1)S(1)} %shard_map.100.s2), channel_id=1, source_target_pairs={{0,2},{2,0},{4,6},{6,4},{8,10},{10,8},{12,14},{14,12},{16,18},{18,... | collective-permute-start | bytes 3145736 | tf_op jit(solution)/shard_map/ppermute | solution.py:29
  71.2 10.9 %collective-permute-start.21 = (bf16[64,2048]{1,0:T(8,128)(2,1)S(1)}, bf16[64,2048]{1,0:T(8,128)(2,1)S(1)}, u32[]{:S(2)}, u32[]{:S(2)}) collective-permute-start(bf16[64,2048]{1,0:T(8,128)(2,1)S(1)} %get-tuple-element.78), channel_id=1, source_target_pairs={{0,32},{2,34},{4,36},{6,38},{8,40},{10,42},{12,44},{14,46},{16,48}... | collective-permute-start | bytes 786440 | tf_op jit(solution)/shard_map/ppermute | solution.py:29
  72.2 15.0 %collective-permute-start.22 = (bf16[64,2048]{1,0:T(8,128)(2,1)S(1)}, bf16[64,2048]{1,0:T(8,128)(2,1)S(1)}, u32[]{:S(2)}, u32[]{:S(2)}) collective-permute-start(bf16[64,2048]{1,0:T(8,128)(2,1)S(1)} %get-tuple-element.79), channel_id=1, source_target_pairs={{0,64},{2,66},{4,68},{6,70},{8,72},{10,74},{12,76},{14,78},{16,80}... | collective-permute-start | bytes 786440 | tf_op jit(solution)/shard_map/ppermute | solution.py:29
  74.8 14.8 %collective-permute-start.23 = (bf16[64,2048]{1,0:T(8,128)(2,1)S(1)}, bf16[64,2048]{1,0:T(8,128)(2,1)S(1)}, u32[]{:S(2)}, u32[]{:S(2)}) collective-permute-start(bf16[64,2048]{1,0:T(8,128)(2,1)S(1)} %get-tuple-element.80), channel_id=1, source_target_pairs={{0,96},{2,98},{4,100},{6,102},{8,104},{10,106},{12,108},{14,110},{... | collective-permute-start | bytes 786440 | tf_op jit(solution)/shard_map/ppermute | solution.py:29
  89.8 6.6 %collective-permute-start.25 = (bf16[16,2048]{1,0:T(8,128)(2,1)S(1)}, bf16[16,2048]{1,0:T(8,128)(2,1)S(1)}, u32[]{:S(2)}, u32[]{:S(2)}) collective-permute-start(bf16[16,2048]{1,0:T(8,128)(2,1)S(1)} %get-tuple-element.102), channel_id=1, source_target_pairs={{0,8},{2,10},{4,12},{6,14},{8,0},{10,2},{12,4},{14,6},{16,24},{18,... | collective-permute-start | bytes 196616 | tf_op jit(solution)/shard_map/ppermute | solution.py:29
  91.1 6.5 %collective-permute-start.27 = (bf16[16,2048]{1,0:T(8,128)(2,1)S(1)}, bf16[16,2048]{1,0:T(8,128)(2,1)S(1)}, u32[]{:S(2)}, u32[]{:S(2)}) collective-permute-start(bf16[16,2048]{1,0:T(8,128)(2,1)S(1)} %get-tuple-element.103), channel_id=1, source_target_pairs={{0,24},{2,26},{4,28},{6,30},{8,16},{10,18},{12,20},{14,22},{16,8},... | collective-permute-start | bytes 196616 | tf_op jit(solution)/shard_map/ppermute | solution.py:29
  94.3 8.9 %collective-permute-start.26 = (bf16[16,2048]{1,0:T(8,128)(2,1)S(1)}, bf16[16,2048]{1,0:T(8,128)(2,1)S(1)}, u32[]{:S(2)}, u32[]{:S(2)}) collective-permute-start(bf16[16,2048]{1,0:T(8,128)(2,1)S(1)} %get-tuple-element.104), channel_id=1, source_target_pairs={{0,16},{2,18},{4,20},{6,22},{8,24},{10,26},{12,28},{14,30},{16,0},... | collective-permute-start | bytes 196616 | tf_op jit(solution)/shard_map/ppermute | solution.py:29
  103.3 6.2 %collective-permute-start.28 = (bf16[8,2048]{1,0:T(8,128)(2,1)S(1)}, bf16[8,2048]{1,0:T(8,128)(2,1)S(1)}, u32[]{:S(2)}, u32[]{:S(2)}) collective-permute-start(bf16[8,2048]{1,0:T(8,128)(2,1)S(1)} %slice.63), channel_id=1, source_target_pairs={{0,128},{2,130},{4,132},{6,134},{8,136},{10,138},{12,140},{14,142}... | collective-permute-start | bytes 98312 | tf_op jit(solution)/shard_map/ppermute | solution.py:29
  (1 other events, 1.4 us)

commit v5 on v4

--- a/solution.py
+++ b/solution.py
@@ -18,6 +18,7 @@
 TG = 8
 STEP = 8
 TOKENS = 256
+ORDER = (1, 3, 2)
 BF = jnp.bfloat16
 F32 = jnp.float32
 NT = (((1,), (1,)), ((), ()))
@@ -62,6 +63,17 @@
         scratch_shapes=list(scratch),
         compiler_params=pltpu.CompilerParams(vmem_limit_bytes=limit * 2**20),
     )
+
+
+def stack_kernel(p0, p1, p2, p3, out_ref):
+    height = p0.shape[0]
+    for at, piece in enumerate((p0, p1, p2, p3)):
+        out_ref[at * height : (at + 1) * height, :] = piece[...]
+
+
+def stack(parts):
+    shape = (4 * parts[0].shape[0],) + parts[0].shape[1:]
+    return call(stack_kernel, sds(shape, parts[0].dtype), [VMEM] * 4)(*parts)
 
 
 def dense_kernel(index_ref, gate_ref, up_ref, down_ref, wg_ref, wu_ref, wd_ref):
@@ -215,8 +227,8 @@
     pair = jnp.concatenate(
         [jnp.concatenate([activations, out_grad], axis=1), jnp.concatenate(other, axis=1)], axis=0
     )
-    near = jnp.concatenate([pair] + [row_swap(pair, z_mask(i)) for i in range(1, 4)], axis=0)
-    pieces = [near] + [row_swap(near, x_mask(i)) for i in range(1, 4)]
+    near = stack([pair] + [row_swap(pair, z_mask(i)) for i in ORDER])
+    pieces = [near] + [row_swap(near, x_mask(i)) for i in ORDER]
     mirror = row_swap(near, 2)
 
     wide = [sds((DQ, HB), BF), sds((DQ, HB), BF), sds((HB, DQ), BF)]
@@ -250,11 +262,11 @@
     keep = partial(0)
     coded = sds((32, 3 * HB + BLK), jnp.int16)
     sums = call(pair_kernel, [sds((32, 3 * HB), F32)] + [coded] * 3, [SMEM, VMEM, VMEM])(place, keep, got)
-    sums = [sums[0]] + [square_swap(sums[i], i) for i in range(1, 4)]
+    sums = [sums[0]] + [square_swap(sums[i], i) for i in (3, 1, 2)]
 
     prep = call(prep_kernel, sds((2 * DB, BLK, TOKENS), BF), [VMEM] * 4)
     mirror, keep = tie((mirror, keep))
-    mirror1, mirror2, mirror3 = [row_swap(mirror, x_mask(i)) for i in (1, 2, 3)]
+    mirror1, mirror2, mirror3 = [row_swap(mirror, x_mask(i)) for i in ORDER]
     slab0 = prep(*tie((pieces, sums[0]))[0])
     sums, mirror1, slab0 = tie((sums, mirror1, slab0))
     share = call(act_kernel, sds((32, 3 * HB), BF), [VMEM] * 4)(*sums)
@@ -273,7 +285,7 @@
     full = outs[4]
     slab2, full = tie((slab2, full))
     slab3 = row_swap(slab2, 1)
-    far1, far2, far3 = [row_swap(outs[i], x_mask(i)) for i in range(1, 4)]
+    far3, far1, far2 = [row_swap(outs[at], x_mask(ORDER[at - 1])) for at in (3, 1, 2)]
 
     grads = call(
         grad_kernel,
@@ -289,11 +301,12 @@
         grid=(CAP // STEP,),
         limit=24,
     )(code, full, slab0, slab1, slab2, slab3)
-    far1, far2, far3, grads = tie((far1, far2, far3, grads))
-    total = outs[0] + far1.astype(F32) + far2.astype(F32) + far3.astype(F32)
+    far3, far1, far2, grads = tie((far3, far1, far2, grads))
+    total = outs[0] + far3.astype(F32) + far1.astype(F32) + far2.astype(F32)
     last = total[: 2 * TG]
-    for i in range(1, 4):
-        last = last + row_swap(total[i * 2 * TG : (i + 1) * 2 * TG].astype(BF), z_mask(i)).astype(F32)
+    for at in (3, 1, 2):
+        part = total[at * 2 * TG : (at + 1) * 2 * TG].astype(BF)
+        last = last + row_swap(part, z_mask(ORDER[at - 1])).astype(F32)
     got = row_swap(last[TG:].astype(BF), Y_MASK).astype(F32)
     mixed_rows, input_grad = [(last[:TG, c] + got[:, c]).astype(BF) for c in (slice(0, DQ), slice(DQ, 2 * DQ))]
     return mixed_rows, input_grad, grads.reshape(3, 1, 1, CAP, BLK, BLK)

time: 111 us -> 106 us (0.955)
  starting transfers between devices: 46.9 us -> 42.7 us
  local copies, waits for them, and re-layouts: 7.58 us -> 6.1 us
    ppermute x23, starting transfers between devices: 39.8 us -> 35.6 us  [row_swap(): return lax.ppermute(value, 'row', [(i, i ^ mask) for i in range(128)])]
    unnamed x17 -> x11, local copies, waits for them, and re-layouts: 5.74 us -> 4.29 us
  transfers between devices with their start and end apart: 29 -> 29, of which waited for: 15 -> 17; matrix products, arithmetic and copies ran while one was open for 3% -> 2% of each run, Pallas kernels for 12% -> 13%
where the time goes in v5:
time: 106 us; the launch traced here: 104 us
  starting transfers between devices  42.7 us (40%)
  waiting for transfers between devices  35.5 us (33%)
  Pallas kernels  17.5 us (17%)
  local copies, waits for them, and re-layouts  6.1 us (6%)
  other arithmetic  1.82 us (2%)
    ppermute x23, starting transfers between devices, row_swap(): return lax.ppermute(value, 'row', [(i, i ^ mask) for i in range(128)])  35.6 us
    ppermute x23, waiting for transfers between devices, row_swap(): return lax.ppermute(value, 'row', [(i, i ^ mask) for i in range(128)])  28.7 us
    ppermute x6, starting transfers between devices, square_swap(): lax.ppermute(value, ('row', 'col'), [(i, i ^ mask) for i in range(256)])  7.15 us
    ppermute x6, waiting for transfers between devices, square_swap(): lax.ppermute(value, ('row', 'col'), [(i, i ^ mask) for i in range(256)])  6.82 us
    pallas_call x1, Pallas kernels, body(): call(grad_kernel, sds((3, CAP, BLK, BLK), BF), [SMEM] + [VMEM] * 5, out_s...  6.21 us
    unnamed x11, local copies, waits for them, and re-layouts  4.29 us
    pallas_call x2, Pallas kernels, partial(): call(functools.partial(partial_kernel, other=other), half, [SMEM] + [VMEM...  3.77 us
    pallas_call x1, Pallas kernels, body(): call(dense_kernel, wide, [SMEM] + [VMEM] * 3)  3.48 us
  transfers between devices with their start and end apart: 29, of which 17 were waited for; matrix products, arithmetic and copies ran while one was open for 2% of the time, Pallas kernels for 13%

profile of v5, /device:TPU:32, one launch (start us, length us, event | category | flops | bytes accessed | tf_op | source)
XLA Modules:
  0.0 104.5 jit_solution(8798173350201941100)
XLA Ops:
  0.6 3.3 %collective-permute-start = (bf16[8,1024]{1,0:T(8,128)(2,1)}, bf16[8,1024]{1,0:T(8,128)(2,1)S(1)}, u32[]{:S(2)}, u32[]{:S(2)}) collective-permute-start(bf16[8,1024]{1,0:T(8,128)(2,1)} %param.7), channel_id=1, source_target_pairs={{0,128},{2,130},{4,132},{6,134},{8,136},{10,138},{12,140},{14,142}... | collective-permute-start | bytes 49160 | tf_op jit(solution)/shard_map/ppermute | solution.py:30
  4.7 1.5 %collective-permute-done = bf16[8,1024]{1,0:T(8,128)(2,1)S(1)} collective-permute-done((bf16[8,1024]{1,0:T(8,128)(2,1)}, bf16[8,1024]{1,0:T(8,128)(2,1)S(1)}, u32[]{:S(2)}, u32[]{:S(2)}) %collective-permute-start) | collective-permute-done | bytes 16416 | tf_op jit(solution)/shard_map/ppermute | solution.py:30
  6.2 3.2 %collective-permute-done.1 = bf16[8,1024]{1,0:T(8,128)(2,1)S(1)} collective-permute-done((bf16[8,1024]{1,0:T(8,128)(2,1)}, bf16[8,1024]{1,0:T(8,128)(2,1)S(1)}, u32[]{:S(2)}, u32[]{:S(2)}) %collective-permute-start.1) | collective-permute-done | bytes 16416 | tf_op jit(solution)/shard_map/ppermute | solution.py:30
  10.1 6.3 %collective-permute-start.4 = (bf16[16,2048]{1,0:T(8,128)(2,1)S(1)}, bf16[16,2048]{1,0:T(8,128)(2,1)S(1)}, u32[]{:S(2)}, u32[]{:S(2)}) collective-permute-start(bf16[16,2048]{1,0:T(8,128)(2,1)S(1)} %maximum_maximum_fusion.p0), channel_id=1, source_target_pairs={{0,16},{2,18},{4,20},{6,22},{8,24},{10,26},{12,28},{14,30},{16,0},... | collective-permute-start | bytes 196616 | tf_op jit(solution)/shard_map/ppermute | solution.py:30
  19.3 4.2 %collective-permute-done.3.p2 = bf16[16,2048]{1,0:T(8,128)(2,1)S(1)} collective-permute-done((bf16[16,2048]{1,0:T(8,128)(2,1)S(1)}, bf16[16,2048]{1,0:T(8,128)(2,1)S(1)}, u32[]{:S(2)}, u32[]{:S(2)}) %collective-permute-start.3) | collective-permute-done | bytes 65568 | tf_op jit(solution)/shard_map/ppermute | solution.py:30
  24.0 3.0 %collective-permute-start.7 = (bf16[64,2048]{1,0:T(8,128)(2,1)S(1)}, bf16[64,2048]{1,0:T(8,128)(2,1)S(1)}, u32[]{:S(2)}, u32[]{:S(2)}) collective-permute-start(bf16[64,2048]{1,0:T(8,128)(2,1)S(1)} %shard_map.94.p0), channel_id=1, source_target_pairs={{0,64},{2,66},{4,68},{6,70},{8,72},{10,74},{12,76},{14,78},{16,80}... | collective-permute-start | bytes 786440 | tf_op jit(solution)/shard_map/ppermute | solution.py:30
  28.6 1.4 %copy-done.1 = bf16[1,1,48,128,128]{4,3,2,1,0:T(8,128)(2,1)S(1)} copy-done((bf16[1,1,48,128,128]{4,3,2,1,0:T(8,128)(2,1)S(1)}, bf16[1,1,48,128,128]{4,3,2,1,0:T(8,128)(2,1)}, u32[]{:S(2)}) %copy-start.1) | copy-done | bytes 1572888
  30.0 1.4 %copy-done.2 = bf16[1,1,48,128,128]{4,3,2,1,0:T(8,128)(2,1)S(1)} copy-done((bf16[1,1,48,128,128]{4,3,2,1,0:T(8,128)(2,1)S(1)}, bf16[1,1,48,128,128]{4,3,2,1,0:T(8,128)(2,1)}, u32[]{:S(2)}) %copy-start.2) | copy-done | bytes 1572888
  31.4 1.4 %copy-done.3 = bf16[1,1,48,128,128]{4,3,2,1,0:T(8,128)(2,1)S(1)} copy-done((bf16[1,1,48,128,128]{4,3,2,1,0:T(8,128)(2,1)S(1)}, bf16[1,1,48,128,128]{4,3,2,1,0:T(8,128)(2,1)}, u32[]{:S(2)}) %copy-start.3) | copy-done | bytes 1572888
  32.8 3.5 %shard_map.95 = (bf16[1024,896]{1,0:T(8,128)(2,1)S(1)}, bf16[1024,896]{1,0:T(8,128)(2,1)S(1)}, bf16[896,1024]{1,0:T(8,128)(2,1)S(1)}) custom-call(s32[3,48]{1,0:T(4,128)S(1)} %dynamic-slice_reduce_fusion.index_ref, bf16[48,128,128]{2,1,0:T(8,128)(2,1)S(1)} %bitcast.12, bf16[48,128,128]{2,1,0:T(8,128)(2,1)S(1)} %bitcast.13, bf16[48,128,128]{2,1,0:T(8,128)(2,1)S(1)} %bitcast.14), custom_call_target="tpu_custom_call" | custom-call | tf_op jit(solution)/shard_map/pallas_call | solution.py:235
  36.6 1.9 %shard_map.97 = f32[128,2688]{1,0:T(8,128)S(1)} custom-call(s32[2]{0:T(128)S(1)} %pad_add_fusion.place_ref, bf16[64,2048]{1,0:T(8,128)(2,1)S(1)} %shard_map.94.p0, bf16[64,2048]{1,0:T(8,128)(2,1)S(1)} %collective-permute-done.5.p1, bf16[64,2048]{1,0:T(8,128)(2,1)S(1)} %collective-permute-done.6.p2, bf16[64,2048]{1,0:T(8,128)(2,1)S(1)} %collective-permute-done.7.p3, ...), custom_call_target="tpu_custom_call" | custom-call | tf_op jit(solution)/shard_map/pallas_call | solution.py:253
  38.6 1.9 %shard_map.96.keep_ref = f32[128,2688]{1,0:T(8,128)S(1)} custom-call(s32[2]{0:T(128)S(1)} %pad_add_fusion.place_ref, bf16[64,2048]{1,0:T(8,128)(2,1)S(1)} %shard_map.94.p0, bf16[64,2048]{1,0:T(8,128)(2,1)S(1)} %collective-permute-done.5.p1, bf16[64,2048]{1,0:T(8,128)(2,1)S(1)} %collective-permute-done.6.p2, bf16[64,2048]{1,0:T(8,128)(2,1)S(1)} %collective-permute-done.7.p3, ...), custom_call_target="tpu_custom_call" | custom-call | tf_op jit(solution)/shard_map/pallas_call | solution.py:253
  40.5 2.3 %collective-permute-start.13 = (bf16[64,2048]{1,0:T(8,128)(2,1)S(1)}, bf16[64,2048]{1,0:T(8,128)(2,1)S(1)}, u32[]{:S(2)}, u32[]{:S(2)}) collective-permute-start(bf16[64,2048]{1,0:T(8,128)(2,1)S(1)} %collective-permute-done.8.p0), channel_id=1, source_target_pairs={{0,32},{2,34},{4,36},{6,38},{8,40},{10,42},{12,44},{14,46},{16,48}... | collective-permute-start | bytes 786440 | tf_op jit(solution)/shard_map/ppermute | solution.py:30
  44.9 1.6 %collective-permute-start.11 = (s16[32,2816]{1,0:T(8,128)(2,1)S(1)}, s16[32,2816]{1,0:T(8,128)(2,1)S(1)}, u32[]{:S(2)}, u32[]{:S(2)}) collective-permute-start(s16[32,2816]{1,0:T(8,128)(2,1)S(1)} %get-tuple-element.56), channel_id=1, source_target_pairs={{0,1},{1,0},{2,3},{3,2},{4,5},{5,4},{6,7},{7,6},{8,9},{9,8},{10,11... | collective-permute-start | bytes 540680 | tf_op jit(solution)/shard_map/ppermute | solution.py:35
  47.3 2.1 %collective-permute-start.18 = (bf16[64,2048]{1,0:T(8,128)(2,1)S(1)}, bf16[64,2048]{1,0:T(8,128)(2,1)S(1)}, u32[]{:S(2)}, u32[]{:S(2)}) collective-permute-start(bf16[64,2048]{1,0:T(8,128)(2,1)S(1)} %collective-permute-done.8.p0), channel_id=1, source_target_pairs={{0,64},{2,66},{4,68},{6,70},{8,72},{10,74},{12,76},{14,78},{16,80}... | collective-permute-start | bytes 786440 | tf_op jit(solution)/shard_map/ppermute | solution.py:30
  49.8 2.2 %collective-permute-start.17 = (bf16[64,2048]{1,0:T(8,128)(2,1)S(1)}, bf16[64,2048]{1,0:T(8,128)(2,1)S(1)}, u32[]{:S(2)}, u32[]{:S(2)}) collective-permute-start(bf16[64,2048]{1,0:T(8,128)(2,1)S(1)} %collective-permute-done.8.p0), channel_id=1, source_target_pairs={{0,96},{2,98},{4,100},{6,102},{8,104},{10,106},{12,108},{14,110},{... | collective-permute-start | bytes 786440 | tf_op jit(solution)/shard_map/ppermute | solution.py:30
  52.3 2.9 %collective-permute-done.11.a2 = s16[32,2816]{1,0:T(8,128)(2,1)S(1)} collective-permute-done((s16[32,2816]{1,0:T(8,128)(2,1)S(1)}, s16[32,2816]{1,0:T(8,128)(2,1)S(1)}, u32[]{:S(2)}, u32[]{:S(2)}) %collective-permute-start.11) | collective-permute-done | bytes 180256 | tf_op jit(solution)/shard_map/ppermute | solution.py:35
  55.4 1.4 %collective-permute-start.16 = (bf16[32,2688]{1,0:T(8,128)(2,1)S(1)}, bf16[32,2688]{1,0:T(8,128)(2,1)S(1)}, u32[]{:S(2)}, u32[]{:S(2)}) collective-permute-start(bf16[32,2688]{1,0:T(8,128)(2,1)S(1)} %shard_map.100), channel_id=1, source_target_pairs={{0,5},{1,4},{2,7},{3,6},{4,1},{5,0},{6,3},{7,2},{8,13},{9,12},{10,... | collective-permute-start | bytes 516104 | tf_op jit(solution)/shard_map/ppermute | solution.py:35
  59.0 3.4 %collective-permute-done.17.p2 = bf16[64,2048]{1,0:T(8,128)(2,1)S(1)} collective-permute-done((bf16[64,2048]{1,0:T(8,128)(2,1)S(1)}, bf16[64,2048]{1,0:T(8,128)(2,1)S(1)}, u32[]{:S(2)}, u32[]{:S(2)}) %collective-permute-start.17) | collective-permute-done | bytes 262176 | tf_op jit(solution)/shard_map/ppermute | solution.py:30
  63.7 1.5 %collective-permute-done.15 = bf16[32,2688]{1,0:T(8,128)(2,1)S(1)} collective-permute-done((bf16[32,2688]{1,0:T(8,128)(2,1)S(1)}, bf16[32,2688]{1,0:T(8,128)(2,1)S(1)}, u32[]{:S(2)}, u32[]{:S(2)}) %collective-permute-start.15) | collective-permute-done | bytes 172064 | tf_op jit(solution)/shard_map/ppermute | solution.py:35
  66.7 1.9 %collective-permute-done.19.theirs = bf16[128,2688]{1,0:T(8,128)(2,1)S(1)} collective-permute-done((bf16[128,2688]{1,0:T(8,128)(2,1)S(1)}, bf16[128,2688]{1,0:T(8,128)(2,1)S(1)}, u32[]{:S(2)}, u32[]{:S(2)}) %collective-permute-start.19) | collective-permute-done | bytes 688160 | tf_op jit(solution)/shard_map/ppermute | solution.py:30
  68.6 2.5 %shard_map.102 = (f32[64,2048]{1,0:T(8,128)S(1)}, bf16[64,2048]{1,0:T(8,128)(2,1)S(1)}, bf16[64,2048]{1,0:T(8,128)(2,1)S(1)}, bf16[64,2048]{1,0:T(8,128)(2,1)S(1)}, bf16[256,2688]{1,0:T(8,128)(2,1)S(1)}) custom-call(s32[2]{0:T(128)S(1)} %pad_add_fusion.place_ref, bf16[128,2688]{1,0:T(8,128)(2,1)S(1)} %constant_dynamic-update-slice_fusion.mine, ...), custom_call_target="tpu_custom_call" | custom-call | tf_op jit(solution)/shard_map/pallas_call | solution.py:280
  71.3 2.0 %collective-permute-start.21 = (bf16[64,2048]{1,0:T(8,128)(2,1)S(1)}, bf16[64,2048]{1,0:T(8,128)(2,1)S(1)}, u32[]{:S(2)}, u32[]{:S(2)}) collective-permute-start(bf16[64,2048]{1,0:T(8,128)(2,1)S(1)} %get-tuple-element.78), channel_id=1, source_target_pairs={{0,64},{2,66},{4,68},{6,70},{8,72},{10,74},{12,76},{14,78},{16,80}... | collective-permute-start | bytes 786440 | tf_op jit(solution)/shard_map/ppermute | solution.py:30
  73.7 1.7 %collective-permute-start.23 = (bf16[64,2048]{1,0:T(8,128)(2,1)S(1)}, bf16[64,2048]{1,0:T(8,128)(2,1)S(1)}, u32[]{:S(2)}, u32[]{:S(2)}) collective-permute-start(bf16[64,2048]{1,0:T(8,128)(2,1)S(1)} %get-tuple-element.80), channel_id=1, source_target_pairs={{0,96},{2,98},{4,100},{6,102},{8,104},{10,106},{12,108},{14,110},{... | collective-permute-start | bytes 786440 | tf_op jit(solution)/shard_map/ppermute | solution.py:30
  75.4 6.2 %shard_map.103 = bf16[3,48,128,128]{3,2,1,0:T(8,128)(2,1)} custom-call(s32[3,48]{1,0:T(4,128)S(1)} %select_reduce_fusion.code_ref, bf16[256,2688]{1,0:T(8,128)(2,1)S(1)} %get-tuple-element.84.full, bf16[16,128,256]{2,1,0:T(8,128)(2,1)S(1)} %shard_map.99.s0, bf16[16,128,256]{2,1,0:T(8,128)(2,1)S(1)} %collective-permute-done.20.s1, ...), custom_call_target="tpu_custom_call" | custom-call | tf_op jit(solution)/shard_map/pallas_call | solution.py:290
  82.0 3.9 %collective-permute-done.22 = bf16[64,2048]{1,0:T(8,128)(2,1)S(1)} collective-permute-done((bf16[64,2048]{1,0:T(8,128)(2,1)S(1)}, bf16[64,2048]{1,0:T(8,128)(2,1)S(1)}, u32[]{:S(2)}, u32[]{:S(2)}) %collective-permute-start.22) | collective-permute-done | bytes 262176 | tf_op jit(solution)/shard_map/ppermute | solution.py:30
  87.2 3.8 %collective-permute-start.25 = (bf16[16,2048]{1,0:T(8,128)(2,1)S(1)}, bf16[16,2048]{1,0:T(8,128)(2,1)S(1)}, u32[]{:S(2)}, u32[]{:S(2)}) collective-permute-start(bf16[16,2048]{1,0:T(8,128)(2,1)S(1)} %get-tuple-element.102), channel_id=1, source_target_pairs={{0,16},{2,18},{4,20},{6,22},{8,24},{10,26},{12,28},{14,30},{16,0},... | collective-permute-start | bytes 196616 | tf_op jit(solution)/shard_map/ppermute | solution.py:30
  92.0 1.8 %collective-permute-start.26 = (bf16[16,2048]{1,0:T(8,128)(2,1)S(1)}, bf16[16,2048]{1,0:T(8,128)(2,1)S(1)}, u32[]{:S(2)}, u32[]{:S(2)}) collective-permute-start(bf16[16,2048]{1,0:T(8,128)(2,1)S(1)} %get-tuple-element.104), channel_id=1, source_target_pairs={{0,8},{2,10},{4,12},{6,14},{8,0},{10,2},{12,4},{14,6},{16,24},{18,... | collective-permute-start | bytes 196616 | tf_op jit(solution)/shard_map/ppermute | solution.py:30
  93.8 3.0 %collective-permute-done.25 = bf16[16,2048]{1,0:T(8,128)(2,1)S(1)} collective-permute-done((bf16[16,2048]{1,0:T(8,128)(2,1)S(1)}, bf16[16,2048]{1,0:T(8,128)(2,1)S(1)}, u32[]{:S(2)}, u32[]{:S(2)}) %collective-permute-start.25) | collective-permute-done | bytes 65568 | tf_op jit(solution)/shard_map/ppermute | solution.py:30
  96.8 1.5 %collective-permute-done.27 = bf16[16,2048]{1,0:T(8,128)(2,1)S(1)} collective-permute-done((bf16[16,2048]{1,0:T(8,128)(2,1)S(1)}, bf16[16,2048]{1,0:T(8,128)(2,1)S(1)}, u32[]{:S(2)}, u32[]{:S(2)}) %collective-permute-start.27) | collective-permute-done | bytes 65568 | tf_op jit(solution)/shard_map/ppermute | solution.py:30
  98.3 1.7 %collective-permute-start.28 = (bf16[8,2048]{1,0:T(8,128)(2,1)S(1)}, bf16[8,2048]{1,0:T(8,128)(2,1)S(1)}, u32[]{:S(2)}, u32[]{:S(2)}) collective-permute-start(bf16[8,2048]{1,0:T(8,128)(2,1)S(1)} %slice.63), channel_id=1, source_target_pairs={{0,128},{2,130},{4,132},{6,134},{8,136},{10,138},{12,140},{14,142}... | collective-permute-start | bytes 98312 | tf_op jit(solution)/shard_map/ppermute | solution.py:30
  100.1 3.8 %collective-permute-done.28 = bf16[8,2048]{1,0:T(8,128)(2,1)S(1)} collective-permute-done((bf16[8,2048]{1,0:T(8,128)(2,1)S(1)}, bf16[8,2048]{1,0:T(8,128)(2,1)S(1)}, u32[]{:S(2)}, u32[]{:S(2)}) %collective-permute-start.28) | collective-permute-done | bytes 32800 | tf_op jit(solution)/shard_map/ppermute | solution.py:30
  (69 shorter events, 19.3 us)
Async XLA Ops:
  0.6 3.8 %copy-start = (s32[3,128,2,48]{1,3,2,0:T(8,128)S(1)}, s32[3,128,2,48]{1,3,2,0:T(8,128)}, u32[]{:S(2)}) copy-start(s32[3,128,2,48]{1,3,2,0:T(8,128)} %param.12) | copy-start | bytes 442372
  0.6 5.5 %collective-permute-start = (bf16[8,1024]{1,0:T(8,128)(2,1)}, bf16[8,1024]{1,0:T(8,128)(2,1)S(1)}, u32[]{:S(2)}, u32[]{:S(2)}) collective-permute-start(bf16[8,1024]{1,0:T(8,128)(2,1)} %param.7), channel_id=1, source_target_pairs={{0,128},{2,130},{4,132},{6,134},{8,136},{10,138},{12,140},{14,142}... | collective-permute-start | bytes 49160 | tf_op jit(solution)/shard_map/ppermute | solution.py:30
  3.9 5.5 %collective-permute-start.1 = (bf16[8,1024]{1,0:T(8,128)(2,1)}, bf16[8,1024]{1,0:T(8,128)(2,1)S(1)}, u32[]{:S(2)}, u32[]{:S(2)}) collective-permute-start(bf16[8,1024]{1,0:T(8,128)(2,1)} %param.8), channel_id=1, source_target_pairs={{0,128},{2,130},{4,132},{6,134},{8,136},{10,138},{12,140},{14,142}... | collective-permute-start | bytes 49160 | tf_op jit(solution)/shard_map/ppermute | solution.py:30
  10.1 9.2 %collective-permute-start.4 = (bf16[16,2048]{1,0:T(8,128)(2,1)S(1)}, bf16[16,2048]{1,0:T(8,128)(2,1)S(1)}, u32[]{:S(2)}, u32[]{:S(2)}) collective-permute-start(bf16[16,2048]{1,0:T(8,128)(2,1)S(1)} %maximum_maximum_fusion.p0), channel_id=1, source_target_pairs={{0,16},{2,18},{4,20},{6,22},{8,24},{10,26},{12,28},{14,30},{16,0},... | collective-permute-start | bytes 196616 | tf_op jit(solution)/shard_map/ppermute | solution.py:30
  16.4 7.1 %collective-permute-start.3 = (bf16[16,2048]{1,0:T(8,128)(2,1)S(1)}, bf16[16,2048]{1,0:T(8,128)(2,1)S(1)}, u32[]{:S(2)}, u32[]{:S(2)}) collective-permute-start(bf16[16,2048]{1,0:T(8,128)(2,1)S(1)} %maximum_maximum_fusion.p0), channel_id=1, source_target_pairs={{0,24},{2,26},{4,28},{6,30},{8,16},{10,18},{12,20},{14,22},{16,8},... | collective-permute-start | bytes 196616 | tf_op jit(solution)/shard_map/ppermute | solution.py:30
  17.0 6.5 %collective-permute-start.2 = (bf16[16,2048]{1,0:T(8,128)(2,1)S(1)}, bf16[16,2048]{1,0:T(8,128)(2,1)S(1)}, u32[]{:S(2)}, u32[]{:S(2)}) collective-permute-start(bf16[16,2048]{1,0:T(8,128)(2,1)S(1)} %maximum_maximum_fusion.p0), channel_id=1, source_target_pairs={{0,8},{2,10},{4,12},{6,14},{8,0},{10,2},{12,4},{14,6},{16,24},{18,... | collective-permute-start | bytes 196616 | tf_op jit(solution)/shard_map/ppermute | solution.py:30
  23.5 13.1 %collective-permute-start.8 = (bf16[64,2048]{1,0:T(8,128)(2,1)S(1)}, bf16[64,2048]{1,0:T(8,128)(2,1)S(1)}, u32[]{:S(2)}, u32[]{:S(2)}) collective-permute-start(bf16[64,2048]{1,0:T(8,128)(2,1)S(1)} %shard_map.94.p0), channel_id=1, source_target_pairs={{0,4},{2,6},{4,0},{6,2},{8,12},{10,14},{12,8},{14,10},{16,20},{18,... | collective-permute-start | bytes 786440 | tf_op jit(solution)/shard_map/ppermute | solution.py:30
  24.0 12.6 %collective-permute-start.7 = (bf16[64,2048]{1,0:T(8,128)(2,1)S(1)}, bf16[64,2048]{1,0:T(8,128)(2,1)S(1)}, u32[]{:S(2)}, u32[]{:S(2)}) collective-permute-start(bf16[64,2048]{1,0:T(8,128)(2,1)S(1)} %shard_map.94.p0), channel_id=1, source_target_pairs={{0,64},{2,66},{4,68},{6,70},{8,72},{10,74},{12,76},{14,78},{16,80}... | collective-permute-start | bytes 786440 | tf_op jit(solution)/shard_map/ppermute | solution.py:30
  27.0 9.6 %collective-permute-start.6 = (bf16[64,2048]{1,0:T(8,128)(2,1)S(1)}, bf16[64,2048]{1,0:T(8,128)(2,1)S(1)}, u32[]{:S(2)}, u32[]{:S(2)}) collective-permute-start(bf16[64,2048]{1,0:T(8,128)(2,1)S(1)} %shard_map.94.p0), channel_id=1, source_target_pairs={{0,96},{2,98},{4,100},{6,102},{8,104},{10,106},{12,108},{14,110},{... | collective-permute-start | bytes 786440 | tf_op jit(solution)/shard_map/ppermute | solution.py:30
  28.2 8.4 %collective-permute-start.5 = (bf16[64,2048]{1,0:T(8,128)(2,1)S(1)}, bf16[64,2048]{1,0:T(8,128)(2,1)S(1)}, u32[]{:S(2)}, u32[]{:S(2)}) collective-permute-start(bf16[64,2048]{1,0:T(8,128)(2,1)S(1)} %shard_map.94.p0), channel_id=1, source_target_pairs={{0,32},{2,34},{4,36},{6,38},{8,40},{10,42},{12,44},{14,46},{16,48}... | collective-permute-start | bytes 786440 | tf_op jit(solution)/shard_map/ppermute | solution.py:30
  28.6 1.4 %copy-start.1 = (bf16[1,1,48,128,128]{4,3,2,1,0:T(8,128)(2,1)S(1)}, bf16[1,1,48,128,128]{4,3,2,1,0:T(8,128)(2,1)}, u32[]{:S(2)}) copy-start(bf16[1,1,48,128,128]{4,3,2,1,0:T(8,128)(2,1)} %param.9) | copy-start | bytes 4718596
  30.0 1.4 %copy-start.2 = (bf16[1,1,48,128,128]{4,3,2,1,0:T(8,128)(2,1)S(1)}, bf16[1,1,48,128,128]{4,3,2,1,0:T(8,128)(2,1)}, u32[]{:S(2)}) copy-start(bf16[1,1,48,128,128]{4,3,2,1,0:T(8,128)(2,1)} %param.10) | copy-start | bytes 4718596
  38.5 4.3 %collective-permute-start.9 = (f32[128,2688]{1,0:T(8,128)S(1)}, f32[128,2688]{1,0:T(8,128)S(1)}, u32[]{:S(2)}, u32[]{:S(2)}) collective-permute-start(f32[128,2688]{1,0:T(8,128)S(1)} %shard_map.97), channel_id=1, source_target_pairs={{0,2},{2,0},{4,6},{6,4},{8,10},{10,8},{12,14},{14,12},{16,18},{18,... | collective-permute-start | bytes 4128776 | tf_op jit(solution)/shard_map/ppermute | solution.py:30
  40.5 9.3 %collective-permute-start.13 = (bf16[64,2048]{1,0:T(8,128)(2,1)S(1)}, bf16[64,2048]{1,0:T(8,128)(2,1)S(1)}, u32[]{:S(2)}, u32[]{:S(2)}) collective-permute-start(bf16[64,2048]{1,0:T(8,128)(2,1)S(1)} %collective-permute-done.8.p0), channel_id=1, source_target_pairs={{0,32},{2,34},{4,36},{6,38},{8,40},{10,42},{12,44},{14,46},{16,48}... | collective-permute-start | bytes 786440 | tf_op jit(solution)/shard_map/ppermute | solution.py:30
  43.7 8.6 %collective-permute-start.10 = (s16[32,2816]{1,0:T(8,128)(2,1)S(1)}, s16[32,2816]{1,0:T(8,128)(2,1)S(1)}, u32[]{:S(2)}, u32[]{:S(2)}) collective-permute-start(s16[32,2816]{1,0:T(8,128)(2,1)S(1)} %get-tuple-element.55), channel_id=1, source_target_pairs={{0,5},{1,4},{2,7},{3,6},{4,1},{5,0},{6,3},{7,2},{8,13},{9,12},{10,... | collective-permute-start | bytes 540680 | tf_op jit(solution)/shard_map/ppermute | solution.py:35
  44.9 10.3 %collective-permute-start.11 = (s16[32,2816]{1,0:T(8,128)(2,1)S(1)}, s16[32,2816]{1,0:T(8,128)(2,1)S(1)}, u32[]{:S(2)}, u32[]{:S(2)}) collective-permute-start(s16[32,2816]{1,0:T(8,128)(2,1)S(1)} %get-tuple-element.56), channel_id=1, source_target_pairs={{0,1},{1,0},{2,3},{3,2},{4,5},{5,4},{6,7},{7,6},{8,9},{9,8},{10,11... | collective-permute-start | bytes 540680 | tf_op jit(solution)/shard_map/ppermute | solution.py:35
  46.5 8.7 %collective-permute-start.12 = (s16[32,2816]{1,0:T(8,128)(2,1)S(1)}, s16[32,2816]{1,0:T(8,128)(2,1)S(1)}, u32[]{:S(2)}, u32[]{:S(2)}) collective-permute-start(s16[32,2816]{1,0:T(8,128)(2,1)S(1)} %get-tuple-element.57), channel_id=1, source_target_pairs={{0,4},{1,5},{2,6},{3,7},{4,0},{5,1},{6,2},{7,3},{8,12},{9,13},{10,... | collective-permute-start | bytes 540680 | tf_op jit(solution)/shard_map/ppermute | solution.py:35
  47.3 11.7 %collective-permute-start.18 = (bf16[64,2048]{1,0:T(8,128)(2,1)S(1)}, bf16[64,2048]{1,0:T(8,128)(2,1)S(1)}, u32[]{:S(2)}, u32[]{:S(2)}) collective-permute-start(bf16[64,2048]{1,0:T(8,128)(2,1)S(1)} %collective-permute-done.8.p0), channel_id=1, source_target_pairs={{0,64},{2,66},{4,68},{6,70},{8,72},{10,74},{12,76},{14,78},{16,80}... | collective-permute-start | bytes 786440 | tf_op jit(solution)/shard_map/ppermute | solution.py:30
  49.8 12.6 %collective-permute-start.17 = (bf16[64,2048]{1,0:T(8,128)(2,1)S(1)}, bf16[64,2048]{1,0:T(8,128)(2,1)S(1)}, u32[]{:S(2)}, u32[]{:S(2)}) collective-permute-start(bf16[64,2048]{1,0:T(8,128)(2,1)S(1)} %collective-permute-done.8.p0), channel_id=1, source_target_pairs={{0,96},{2,98},{4,100},{6,102},{8,104},{10,106},{12,108},{14,110},{... | collective-permute-start | bytes 786440 | tf_op jit(solution)/shard_map/ppermute | solution.py:30
  55.4 8.3 %collective-permute-start.16 = (bf16[32,2688]{1,0:T(8,128)(2,1)S(1)}, bf16[32,2688]{1,0:T(8,128)(2,1)S(1)}, u32[]{:S(2)}, u32[]{:S(2)}) collective-permute-start(bf16[32,2688]{1,0:T(8,128)(2,1)S(1)} %shard_map.100), channel_id=1, source_target_pairs={{0,5},{1,4},{2,7},{3,6},{4,1},{5,0},{6,3},{7,2},{8,13},{9,12},{10,... | collective-permute-start | bytes 516104 | tf_op jit(solution)/shard_map/ppermute | solution.py:35
  56.8 8.4 %collective-permute-start.15 = (bf16[32,2688]{1,0:T(8,128)(2,1)S(1)}, bf16[32,2688]{1,0:T(8,128)(2,1)S(1)}, u32[]{:S(2)}, u32[]{:S(2)}) collective-permute-start(bf16[32,2688]{1,0:T(8,128)(2,1)S(1)} %shard_map.100), channel_id=1, source_target_pairs={{0,4},{1,5},{2,6},{3,7},{4,0},{5,1},{6,2},{7,3},{8,12},{9,13},{10,... | collective-permute-start | bytes 516104 | tf_op jit(solution)/shard_map/ppermute | solution.py:35
  57.6 8.7 %collective-permute-start.14 = (bf16[32,2688]{1,0:T(8,128)(2,1)S(1)}, bf16[32,2688]{1,0:T(8,128)(2,1)S(1)}, u32[]{:S(2)}, u32[]{:S(2)}) collective-permute-start(bf16[32,2688]{1,0:T(8,128)(2,1)S(1)} %shard_map.100), channel_id=1, source_target_pairs={{0,1},{1,0},{2,3},{3,2},{4,5},{5,4},{6,7},{7,6},{8,9},{9,8},{10,11... | collective-permute-start | bytes 516104 | tf_op jit(solution)/shard_map/ppermute | solution.py:35
  59.0 9.6 %collective-permute-start.20 = (bf16[16,128,256]{2,1,0:T(8,128)(2,1)S(1)}, bf16[16,128,256]{2,1,0:T(8,128)(2,1)S(1)}, u32[]{:S(2)}, u32[]{:S(2)}) collective-permute-start(bf16[16,128,256]{2,1,0:T(8,128)(2,1)S(1)} %shard_map.99.s0), channel_id=1, source_target_pairs={{0,2},{2,0},{4,6},{6,4},{8,10},{10,8},{12,14},{14,12},{16,18},{18,... | collective-permute-start | bytes 3145736 | tf_op jit(solution)/shard_map/ppermute | solution.py:30
  66.4 2.2 %collective-permute-start.19 = (bf16[128,2688]{1,0:T(8,128)(2,1)S(1)}, bf16[128,2688]{1,0:T(8,128)(2,1)S(1)}, u32[]{:S(2)}, u32[]{:S(2)}) collective-permute-start(bf16[128,2688]{1,0:T(8,128)(2,1)S(1)} %constant_dynamic-update-slice_fusion.mine), channel_id=1, source_target_pairs={{0,2},{2,0},{4,6},{6,4},{8,10},{10,8},{12,14},{14,12},{16,18},{18,... | collective-permute-start | bytes 2064392 | tf_op jit(solution)/shard_map/ppermute | solution.py:30
  71.1 4.3 %collective-permute-start.24 = (bf16[16,128,256]{2,1,0:T(8,128)(2,1)S(1)}, bf16[16,128,256]{2,1,0:T(8,128)(2,1)S(1)}, u32[]{:S(2)}, u32[]{:S(2)}) collective-permute-start(bf16[16,128,256]{2,1,0:T(8,128)(2,1)S(1)} %shard_map.101.s2), channel_id=1, source_target_pairs={{0,2},{2,0},{4,6},{6,4},{8,10},{10,8},{12,14},{14,12},{16,18},{18,... | collective-permute-start | bytes 3145736 | tf_op jit(solution)/shard_map/ppermute | solution.py:30
  71.3 10.7 %collective-permute-start.21 = (bf16[64,2048]{1,0:T(8,128)(2,1)S(1)}, bf16[64,2048]{1,0:T(8,128)(2,1)S(1)}, u32[]{:S(2)}, u32[]{:S(2)}) collective-permute-start(bf16[64,2048]{1,0:T(8,128)(2,1)S(1)} %get-tuple-element.78), channel_id=1, source_target_pairs={{0,64},{2,66},{4,68},{6,70},{8,72},{10,74},{12,76},{14,78},{16,80}... | collective-permute-start | bytes 786440 | tf_op jit(solution)/shard_map/ppermute | solution.py:30
  73.3 12.6 %collective-permute-start.22 = (bf16[64,2048]{1,0:T(8,128)(2,1)S(1)}, bf16[64,2048]{1,0:T(8,128)(2,1)S(1)}, u32[]{:S(2)}, u32[]{:S(2)}) collective-permute-start(bf16[64,2048]{1,0:T(8,128)(2,1)S(1)} %get-tuple-element.79), channel_id=1, source_target_pairs={{0,32},{2,34},{4,36},{6,38},{8,40},{10,42},{12,44},{14,46},{16,48}... | collective-permute-start | bytes 786440 | tf_op jit(solution)/shard_map/ppermute | solution.py:30
  73.7 13.3 %collective-permute-start.23 = (bf16[64,2048]{1,0:T(8,128)(2,1)S(1)}, bf16[64,2048]{1,0:T(8,128)(2,1)S(1)}, u32[]{:S(2)}, u32[]{:S(2)}) collective-permute-start(bf16[64,2048]{1,0:T(8,128)(2,1)S(1)} %get-tuple-element.80), channel_id=1, source_target_pairs={{0,96},{2,98},{4,100},{6,102},{8,104},{10,106},{12,108},{14,110},{... | collective-permute-start | bytes 786440 | tf_op jit(solution)/shard_map/ppermute | solution.py:30
  87.2 9.6 %collective-permute-start.25 = (bf16[16,2048]{1,0:T(8,128)(2,1)S(1)}, bf16[16,2048]{1,0:T(8,128)(2,1)S(1)}, u32[]{:S(2)}, u32[]{:S(2)}) collective-permute-start(bf16[16,2048]{1,0:T(8,128)(2,1)S(1)} %get-tuple-element.102), channel_id=1, source_target_pairs={{0,16},{2,18},{4,20},{6,22},{8,24},{10,26},{12,28},{14,30},{16,0},... | collective-permute-start | bytes 196616 | tf_op jit(solution)/shard_map/ppermute | solution.py:30
  91.0 7.3 %collective-permute-start.27 = (bf16[16,2048]{1,0:T(8,128)(2,1)S(1)}, bf16[16,2048]{1,0:T(8,128)(2,1)S(1)}, u32[]{:S(2)}, u32[]{:S(2)}) collective-permute-start(bf16[16,2048]{1,0:T(8,128)(2,1)S(1)} %get-tuple-element.103), channel_id=1, source_target_pairs={{0,24},{2,26},{4,28},{6,30},{8,16},{10,18},{12,20},{14,22},{16,8},... | collective-permute-start | bytes 196616 | tf_op jit(solution)/shard_map/ppermute | solution.py:30
  92.0 6.3 %collective-permute-start.26 = (bf16[16,2048]{1,0:T(8,128)(2,1)S(1)}, bf16[16,2048]{1,0:T(8,128)(2,1)S(1)}, u32[]{:S(2)}, u32[]{:S(2)}) collective-permute-start(bf16[16,2048]{1,0:T(8,128)(2,1)S(1)} %get-tuple-element.104), channel_id=1, source_target_pairs={{0,8},{2,10},{4,12},{6,14},{8,0},{10,2},{12,4},{14,6},{16,24},{18,... | collective-permute-start | bytes 196616 | tf_op jit(solution)/shard_map/ppermute | solution.py:30
  98.3 5.5 %collective-permute-start.28 = (bf16[8,2048]{1,0:T(8,128)(2,1)S(1)}, bf16[8,2048]{1,0:T(8,128)(2,1)S(1)}, u32[]{:S(2)}, u32[]{:S(2)}) collective-permute-start(bf16[8,2048]{1,0:T(8,128)(2,1)S(1)} %slice.63), channel_id=1, source_target_pairs={{0,128},{2,130},{4,132},{6,134},{8,136},{10,138},{12,140},{14,142}... | collective-permute-start | bytes 98312 | tf_op jit(solution)/shard_map/ppermute | solution.py:30
  (1 other events, 1.4 us)

commit v6 on v5

--- a/solution.py
+++ b/solution.py
@@ -223,13 +223,11 @@
     own_index = lax.dynamic_index_in_dim(all_index, row, axis=1, keepdims=False)
 
     tie = lax.optimization_barrier
-    other = [row_swap(activations, Y_MASK), row_swap(out_grad, Y_MASK)]
-    pair = jnp.concatenate(
-        [jnp.concatenate([activations, out_grad], axis=1), jnp.concatenate(other, axis=1)], axis=0
-    )
+    shard = jnp.concatenate([activations, out_grad], axis=1)
+    pair = jnp.concatenate([shard, row_swap(shard, Y_MASK)], axis=0)
     near = stack([pair] + [row_swap(pair, z_mask(i)) for i in ORDER])
     pieces = [near] + [row_swap(near, x_mask(i)) for i in ORDER]
-    mirror = row_swap(near, 2)
+    halves = [row_swap(near[at * 32 : (at + 1) * 32], 2) for at in range(2)]
 
     wide = [sds((DQ, HB), BF), sds((DQ, HB), BF), sds((HB, DQ), BF)]
     wg, wu, wd = call(dense_kernel, wide, [SMEM] + [VMEM] * 3)(
@@ -245,7 +243,8 @@
     targets = quarter * CAP + jnp.arange(CAP, dtype=jnp.int32)
     hits = dest.reshape(3, 1, QUARTERS * CAP) == targets[None, :, None]
     code = jnp.sum(jnp.where(hits, value, 0), axis=2, dtype=jnp.int32)
-    pieces, mirror, code = tie((pieces, mirror, code))
+    pieces, halves, code = tie((pieces, halves, code))
+    mirror = jnp.concatenate(halves, axis=0)
 
     half = sds((128, 3 * HB), F32)
 

time: 106 us -> 104 us (0.981)
  waiting for transfers between devices: 35.5 us -> 31.6 us
  starting transfers between devices: 42.7 us -> 45.5 us
    ppermute x23, waiting for transfers between devices: 28.7 us -> 25.3 us  [row_swap(): return lax.ppermute(value, 'row', [(i, i ^ mask) for i in range(128)])]
    ppermute x23, starting transfers between devices: 35.6 us -> 38.3 us  [row_swap(): return lax.ppermute(value, 'row', [(i, i ^ mask) for i in range(128)])]
    unnamed x11 -> x12, local copies, waits for them, and re-layouts: 4.29 us -> 3.72 us
  transfers between devices with their start and end apart: 29 -> 29, of which waited for: 17 -> 16; matrix products, arithmetic and copies ran while one was open for 2% -> 2% of each run, Pallas kernels for 13% -> 13%
where the time goes in v6:
time: 104 us; the launch traced here: 103 us
  starting transfers between devices  45.5 us (44%)
  waiting for transfers between devices  31.6 us (30%)
  Pallas kernels  17.5 us (17%)
  local copies, waits for them, and re-layouts  6.28 us (6%)
  other arithmetic  1.11 us (1%)
    ppermute x23, starting transfers between devices, row_swap(): return lax.ppermute(value, 'row', [(i, i ^ mask) for i in range(128)])  38.3 us
    ppermute x23, waiting for transfers between devices, row_swap(): return lax.ppermute(value, 'row', [(i, i ^ mask) for i in range(128)])  25.3 us
    ppermute x6, starting transfers between devices, square_swap(): lax.ppermute(value, ('row', 'col'), [(i, i ^ mask) for i in range(256)])  7.15 us
    ppermute x6, waiting for transfers between devices, square_swap(): lax.ppermute(value, ('row', 'col'), [(i, i ^ mask) for i in range(256)])  6.37 us
    pallas_call x1, Pallas kernels, body(): call(grad_kernel, sds((3, CAP, BLK, BLK), BF), [SMEM] + [VMEM] * 5, out_s...  6.21 us
    pallas_call x2, Pallas kernels, partial(): call(functools.partial(partial_kernel, other=other), half, [SMEM] + [VMEM...  3.77 us
    unnamed x12, local copies, waits for them, and re-layouts  3.72 us
    pallas_call x1, Pallas kernels, body(): call(dense_kernel, wide, [SMEM] + [VMEM] * 3)  3.52 us
  transfers between devices with their start and end apart: 29, of which 16 were waited for; matrix products, arithmetic and copies ran while one was open for 2% of the time, Pallas kernels for 13%

profile of v6, /device:TPU:32, one launch (start us, length us, event | category | flops | bytes accessed | tf_op | source)
XLA Modules:
  0.0 103.0 jit_solution(8509798056752743528)
XLA Ops:
  2.2 3.2 %collective-permute-start = (bf16[8,2048]{1,0:T(8,128)(2,1)S(1)}, bf16[8,2048]{1,0:T(8,128)(2,1)S(1)}, u32[]{:S(2)}, u32[]{:S(2)}) collective-permute-start(bf16[8,2048]{1,0:T(8,128)(2,1)S(1)} %constant_dynamic-update-slice_fusion), channel_id=1, source_target_pairs={{0,128},{2,130},{4,132},{6,134},{8,136},{10,138},{12,140},{14,142}... | collective-permute-start | bytes 98312 | tf_op jit(solution)/shard_map/ppermute | solution.py:30
  7.6 6.3 %collective-permute-start.3 = (bf16[16,2048]{1,0:T(8,128)(2,1)S(1)}, bf16[16,2048]{1,0:T(8,128)(2,1)S(1)}, u32[]{:S(2)}, u32[]{:S(2)}) collective-permute-start(bf16[16,2048]{1,0:T(8,128)(2,1)S(1)} %pad_maximum_fusion.1.p0), channel_id=1, source_target_pairs={{0,16},{2,18},{4,20},{6,22},{8,24},{10,26},{12,28},{14,30},{16,0},... | collective-permute-start | bytes 196616 | tf_op jit(solution)/shard_map/ppermute | solution.py:30
  15.4 1.6 %collective-permute-done.3.p3 = bf16[16,2048]{1,0:T(8,128)(2,1)S(1)} collective-permute-done((bf16[16,2048]{1,0:T(8,128)(2,1)S(1)}, bf16[16,2048]{1,0:T(8,128)(2,1)S(1)}, u32[]{:S(2)}, u32[]{:S(2)}) %collective-permute-start.3) | collective-permute-done | bytes 65568 | tf_op jit(solution)/shard_map/ppermute | solution.py:30
  17.0 4.0 %collective-permute-done.2.p2 = bf16[16,2048]{1,0:T(8,128)(2,1)S(1)} collective-permute-done((bf16[16,2048]{1,0:T(8,128)(2,1)S(1)}, bf16[16,2048]{1,0:T(8,128)(2,1)S(1)}, u32[]{:S(2)}, u32[]{:S(2)}) %collective-permute-start.2) | collective-permute-done | bytes 65568 | tf_op jit(solution)/shard_map/ppermute | solution.py:30
  21.0 3.1 %collective-permute-start.6 = (bf16[64,2048]{1,0:T(8,128)(2,1)S(1)}, bf16[64,2048]{1,0:T(8,128)(2,1)S(1)}, u32[]{:S(2)}, u32[]{:S(2)}) collective-permute-start(bf16[64,2048]{1,0:T(8,128)(2,1)S(1)} %shard_map.94.p0), channel_id=1, source_target_pairs={{0,64},{2,66},{4,68},{6,70},{8,72},{10,74},{12,76},{14,78},{16,80}... | collective-permute-start | bytes 786440 | tf_op jit(solution)/shard_map/ppermute | solution.py:30
  25.9 1.6 %collective-permute-start.7 = (bf16[32,2048]{1,0:T(8,128)(2,1)S(1)}, bf16[32,2048]{1,0:T(8,128)(2,1)S(1)}, u32[]{:S(2)}, u32[]{:S(2)}) collective-permute-start(bf16[32,2048]{1,0:T(8,128)(2,1)S(1)} %get-tuple-element.108), channel_id=1, source_target_pairs={{0,4},{2,6},{4,0},{6,2},{8,12},{10,14},{12,8},{14,10},{16,20},{18,... | collective-permute-start | bytes 393224 | tf_op jit(solution)/shard_map/ppermute | solution.py:30
  27.9 1.4 %copy-done.2 = bf16[1,1,48,128,128]{4,3,2,1,0:T(8,128)(2,1)S(1)} copy-done((bf16[1,1,48,128,128]{4,3,2,1,0:T(8,128)(2,1)S(1)}, bf16[1,1,48,128,128]{4,3,2,1,0:T(8,128)(2,1)}, u32[]{:S(2)}) %copy-start.2) | copy-done | bytes 1572888
  29.3 1.4 %copy-done.3 = bf16[1,1,48,128,128]{4,3,2,1,0:T(8,128)(2,1)S(1)} copy-done((bf16[1,1,48,128,128]{4,3,2,1,0:T(8,128)(2,1)S(1)}, bf16[1,1,48,128,128]{4,3,2,1,0:T(8,128)(2,1)}, u32[]{:S(2)}) %copy-start.3) | copy-done | bytes 1572888
  30.7 3.5 %shard_map.95 = (bf16[1024,896]{1,0:T(8,128)(2,1)S(1)}, bf16[1024,896]{1,0:T(8,128)(2,1)S(1)}, bf16[896,1024]{1,0:T(8,128)(2,1)S(1)}) custom-call(s32[3,48]{1,0:T(4,128)S(1)} %dynamic-slice_reduce_fusion.index_ref, bf16[48,128,128]{2,1,0:T(8,128)(2,1)S(1)} %bitcast.12, bf16[48,128,128]{2,1,0:T(8,128)(2,1)S(1)} %bitcast.13, bf16[48,128,128]{2,1,0:T(8,128)(2,1)S(1)} %bitcast.14), custom_call_target="tpu_custom_call" | custom-call | tf_op jit(solution)/shard_map/pallas_call | solution.py:233
  34.5 1.9 %shard_map.97 = f32[128,2688]{1,0:T(8,128)S(1)} custom-call(s32[2]{0:T(128)S(1)} %pad_add_fusion.place_ref, bf16[64,2048]{1,0:T(8,128)(2,1)S(1)} %shard_map.94.p0, bf16[64,2048]{1,0:T(8,128)(2,1)S(1)} %collective-permute-done.4.p1, bf16[64,2048]{1,0:T(8,128)(2,1)S(1)} %collective-permute-done.5.p2, bf16[64,2048]{1,0:T(8,128)(2,1)S(1)} %collective-permute-done.6.p3, ...), custom_call_target="tpu_custom_call" | custom-call | tf_op jit(solution)/shard_map/pallas_call | solution.py:252
  36.5 1.9 %shard_map.96.keep_ref = f32[128,2688]{1,0:T(8,128)S(1)} custom-call(s32[2]{0:T(128)S(1)} %pad_add_fusion.place_ref, bf16[64,2048]{1,0:T(8,128)(2,1)S(1)} %shard_map.94.p0, bf16[64,2048]{1,0:T(8,128)(2,1)S(1)} %collective-permute-done.4.p1, bf16[64,2048]{1,0:T(8,128)(2,1)S(1)} %collective-permute-done.5.p2, bf16[64,2048]{1,0:T(8,128)(2,1)S(1)} %collective-permute-done.6.p3, ...), custom_call_target="tpu_custom_call" | custom-call | tf_op jit(solution)/shard_map/pallas_call | solution.py:252
  38.4 1.9 %collective-permute-start.13 = (bf16[64,2048]{1,0:T(8,128)(2,1)S(1)}, bf16[64,2048]{1,0:T(8,128)(2,1)S(1)}, u32[]{:S(2)}, u32[]{:S(2)}) collective-permute-start(bf16[64,2048]{1,0:T(8,128)(2,1)S(1)} %pad_maximum_fusion.p0), channel_id=1, source_target_pairs={{0,32},{2,34},{4,36},{6,38},{8,40},{10,42},{12,44},{14,46},{16,48}... | collective-permute-start | bytes 786440 | tf_op jit(solution)/shard_map/ppermute | solution.py:30
  41.2 1.7 %collective-permute-start.10 = (s16[32,2816]{1,0:T(8,128)(2,1)S(1)}, s16[32,2816]{1,0:T(8,128)(2,1)S(1)}, u32[]{:S(2)}, u32[]{:S(2)}) collective-permute-start(s16[32,2816]{1,0:T(8,128)(2,1)S(1)} %get-tuple-element.56), channel_id=1, source_target_pairs={{0,5},{1,4},{2,7},{3,6},{4,1},{5,0},{6,3},{7,2},{8,13},{9,12},{10,... | collective-permute-start | bytes 540680 | tf_op jit(solution)/shard_map/ppermute | solution.py:35
  43.5 1.2 %collective-permute-start.12 = (s16[32,2816]{1,0:T(8,128)(2,1)S(1)}, s16[32,2816]{1,0:T(8,128)(2,1)S(1)}, u32[]{:S(2)}, u32[]{:S(2)}) collective-permute-start(s16[32,2816]{1,0:T(8,128)(2,1)S(1)} %get-tuple-element.58), channel_id=1, source_target_pairs={{0,4},{1,5},{2,6},{3,7},{4,0},{5,1},{6,2},{7,3},{8,12},{9,13},{10,... | collective-permute-start | bytes 540680 | tf_op jit(solution)/shard_map/ppermute | solution.py:35
  44.8 2.8 %collective-permute-start.18 = (bf16[64,2048]{1,0:T(8,128)(2,1)S(1)}, bf16[64,2048]{1,0:T(8,128)(2,1)S(1)}, u32[]{:S(2)}, u32[]{:S(2)}) collective-permute-start(bf16[64,2048]{1,0:T(8,128)(2,1)S(1)} %pad_maximum_fusion.p0), channel_id=1, source_target_pairs={{0,64},{2,66},{4,68},{6,70},{8,72},{10,74},{12,76},{14,78},{16,80}... | collective-permute-start | bytes 786440 | tf_op jit(solution)/shard_map/ppermute | solution.py:30
  47.6 2.3 %collective-permute-start.17 = (bf16[64,2048]{1,0:T(8,128)(2,1)S(1)}, bf16[64,2048]{1,0:T(8,128)(2,1)S(1)}, u32[]{:S(2)}, u32[]{:S(2)}) collective-permute-start(bf16[64,2048]{1,0:T(8,128)(2,1)S(1)} %pad_maximum_fusion.p0), channel_id=1, source_target_pairs={{0,96},{2,98},{4,100},{6,102},{8,104},{10,106},{12,108},{14,110},{... | collective-permute-start | bytes 786440 | tf_op jit(solution)/shard_map/ppermute | solution.py:30
  50.1 2.6 %collective-permute-done.11.a2 = s16[32,2816]{1,0:T(8,128)(2,1)S(1)} collective-permute-done((s16[32,2816]{1,0:T(8,128)(2,1)S(1)}, s16[32,2816]{1,0:T(8,128)(2,1)S(1)}, u32[]{:S(2)}, u32[]{:S(2)}) %collective-permute-start.11) | collective-permute-done | bytes 180256 | tf_op jit(solution)/shard_map/ppermute | solution.py:35
  53.1 1.6 %collective-permute-start.16 = (bf16[32,2688]{1,0:T(8,128)(2,1)S(1)}, bf16[32,2688]{1,0:T(8,128)(2,1)S(1)}, u32[]{:S(2)}, u32[]{:S(2)}) collective-permute-start(bf16[32,2688]{1,0:T(8,128)(2,1)S(1)} %shard_map.100), channel_id=1, source_target_pairs={{0,5},{1,4},{2,7},{3,6},{4,1},{5,0},{6,3},{7,2},{8,13},{9,12},{10,... | collective-permute-start | bytes 516104 | tf_op jit(solution)/shard_map/ppermute | solution.py:35
  56.6 3.6 %collective-permute-done.17.p2 = bf16[64,2048]{1,0:T(8,128)(2,1)S(1)} collective-permute-done((bf16[64,2048]{1,0:T(8,128)(2,1)S(1)}, bf16[64,2048]{1,0:T(8,128)(2,1)S(1)}, u32[]{:S(2)}, u32[]{:S(2)}) %collective-permute-start.17) | collective-permute-done | bytes 262176 | tf_op jit(solution)/shard_map/ppermute | solution.py:30
  61.4 1.7 %collective-permute-done.15 = bf16[32,2688]{1,0:T(8,128)(2,1)S(1)} collective-permute-done((bf16[32,2688]{1,0:T(8,128)(2,1)S(1)}, bf16[32,2688]{1,0:T(8,128)(2,1)S(1)}, u32[]{:S(2)}, u32[]{:S(2)}) %collective-permute-start.15) | collective-permute-done | bytes 172064 | tf_op jit(solution)/shard_map/ppermute | solution.py:35
  64.3 1.9 %collective-permute-done.19.theirs = bf16[128,2688]{1,0:T(8,128)(2,1)S(1)} collective-permute-done((bf16[128,2688]{1,0:T(8,128)(2,1)S(1)}, bf16[128,2688]{1,0:T(8,128)(2,1)S(1)}, u32[]{:S(2)}, u32[]{:S(2)}) %collective-permute-start.19) | collective-permute-done | bytes 688160 | tf_op jit(solution)/shard_map/ppermute | solution.py:30
  66.2 2.5 %shard_map.102 = (f32[64,2048]{1,0:T(8,128)S(1)}, bf16[64,2048]{1,0:T(8,128)(2,1)S(1)}, bf16[64,2048]{1,0:T(8,128)(2,1)S(1)}, bf16[64,2048]{1,0:T(8,128)(2,1)S(1)}, bf16[256,2688]{1,0:T(8,128)(2,1)S(1)}) custom-call(s32[2]{0:T(128)S(1)} %pad_add_fusion.place_ref, bf16[128,2688]{1,0:T(8,128)(2,1)S(1)} %constant_dynamic-update-slice_fusion.2.mine, ...), custom_call_target="tpu_custom_call" | custom-call | tf_op jit(solution)/shard_map/pallas_call | solution.py:279
  68.9 2.8 %collective-permute-start.21 = (bf16[64,2048]{1,0:T(8,128)(2,1)S(1)}, bf16[64,2048]{1,0:T(8,128)(2,1)S(1)}, u32[]{:S(2)}, u32[]{:S(2)}) collective-permute-start(bf16[64,2048]{1,0:T(8,128)(2,1)S(1)} %get-tuple-element.80), channel_id=1, source_target_pairs={{0,64},{2,66},{4,68},{6,70},{8,72},{10,74},{12,76},{14,78},{16,80}... | collective-permute-start | bytes 786440 | tf_op jit(solution)/shard_map/ppermute | solution.py:30
  73.0 6.2 %shard_map.103 = bf16[3,48,128,128]{3,2,1,0:T(8,128)(2,1)} custom-call(s32[3,48]{1,0:T(4,128)S(1)} %select_reduce_fusion.code_ref, bf16[256,2688]{1,0:T(8,128)(2,1)S(1)} %get-tuple-element.86.full, bf16[16,128,256]{2,1,0:T(8,128)(2,1)S(1)} %shard_map.99.s0, bf16[16,128,256]{2,1,0:T(8,128)(2,1)S(1)} %collective-permute-done.20.s1, ...), custom_call_target="tpu_custom_call" | custom-call | tf_op jit(solution)/shard_map/pallas_call | solution.py:289
  79.6 4.7 %collective-permute-done.22 = bf16[64,2048]{1,0:T(8,128)(2,1)S(1)} collective-permute-done((bf16[64,2048]{1,0:T(8,128)(2,1)S(1)}, bf16[64,2048]{1,0:T(8,128)(2,1)S(1)}, u32[]{:S(2)}, u32[]{:S(2)}) %collective-permute-start.22) | collective-permute-done | bytes 262176 | tf_op jit(solution)/shard_map/ppermute | solution.py:30
  84.8 3.8 %collective-permute-start.25 = (bf16[16,2048]{1,0:T(8,128)(2,1)S(1)}, bf16[16,2048]{1,0:T(8,128)(2,1)S(1)}, u32[]{:S(2)}, u32[]{:S(2)}) collective-permute-start(bf16[16,2048]{1,0:T(8,128)(2,1)S(1)} %get-tuple-element.104), channel_id=1, source_target_pairs={{0,16},{2,18},{4,20},{6,22},{8,24},{10,26},{12,28},{14,30},{16,0},... | collective-permute-start | bytes 196616 | tf_op jit(solution)/shard_map/ppermute | solution.py:30
  88.6 1.2 %collective-permute-start.27 = (bf16[16,2048]{1,0:T(8,128)(2,1)S(1)}, bf16[16,2048]{1,0:T(8,128)(2,1)S(1)}, u32[]{:S(2)}, u32[]{:S(2)}) collective-permute-start(bf16[16,2048]{1,0:T(8,128)(2,1)S(1)} %get-tuple-element.105), channel_id=1, source_target_pairs={{0,24},{2,26},{4,28},{6,30},{8,16},{10,18},{12,20},{14,22},{16,8},... | collective-permute-start | bytes 196616 | tf_op jit(solution)/shard_map/ppermute | solution.py:30
  89.8 1.5 %collective-permute-start.26 = (bf16[16,2048]{1,0:T(8,128)(2,1)S(1)}, bf16[16,2048]{1,0:T(8,128)(2,1)S(1)}, u32[]{:S(2)}, u32[]{:S(2)}) collective-permute-start(bf16[16,2048]{1,0:T(8,128)(2,1)S(1)} %get-tuple-element.106), channel_id=1, source_target_pairs={{0,8},{2,10},{4,12},{6,14},{8,0},{10,2},{12,4},{14,6},{16,24},{18,... | collective-permute-start | bytes 196616 | tf_op jit(solution)/shard_map/ppermute | solution.py:30
  91.4 3.3 %collective-permute-done.25 = bf16[16,2048]{1,0:T(8,128)(2,1)S(1)} collective-permute-done((bf16[16,2048]{1,0:T(8,128)(2,1)S(1)}, bf16[16,2048]{1,0:T(8,128)(2,1)S(1)}, u32[]{:S(2)}, u32[]{:S(2)}) %collective-permute-start.25) | collective-permute-done | bytes 65568 | tf_op jit(solution)/shard_map/ppermute | solution.py:30
  94.7 2.1 %collective-permute-done.27 = bf16[16,2048]{1,0:T(8,128)(2,1)S(1)} collective-permute-done((bf16[16,2048]{1,0:T(8,128)(2,1)S(1)}, bf16[16,2048]{1,0:T(8,128)(2,1)S(1)}, u32[]{:S(2)}, u32[]{:S(2)}) %collective-permute-start.27) | collective-permute-done | bytes 65568 | tf_op jit(solution)/shard_map/ppermute | solution.py:30
  96.8 2.9 %collective-permute-start.28 = (bf16[8,2048]{1,0:T(8,128)(2,1)S(1)}, bf16[8,2048]{1,0:T(8,128)(2,1)S(1)}, u32[]{:S(2)}, u32[]{:S(2)}) collective-permute-start(bf16[8,2048]{1,0:T(8,128)(2,1)S(1)} %slice.73), channel_id=1, source_target_pairs={{0,128},{2,130},{4,132},{6,134},{8,136},{10,138},{12,140},{14,142}... | collective-permute-start | bytes 98312 | tf_op jit(solution)/shard_map/ppermute | solution.py:30
  99.7 2.6 %collective-permute-done.28 = bf16[8,2048]{1,0:T(8,128)(2,1)S(1)} collective-permute-done((bf16[8,2048]{1,0:T(8,128)(2,1)S(1)}, bf16[8,2048]{1,0:T(8,128)(2,1)S(1)}, u32[]{:S(2)}, u32[]{:S(2)}) %collective-permute-start.28) | collective-permute-done | bytes 32800 | tf_op jit(solution)/shard_map/ppermute | solution.py:30
  (73 shorter events, 17.3 us)
Async XLA Ops:
  0.6 5.0 %copy-start = (s32[3,128,2,48]{1,3,2,0:T(8,128)S(1)}, s32[3,128,2,48]{1,3,2,0:T(8,128)}, u32[]{:S(2)}) copy-start(s32[3,128,2,48]{1,3,2,0:T(8,128)} %param.12) | copy-start | bytes 442372
  0.6 27.3 %copy-start.1 = (bf16[1,1,48,128,128]{4,3,2,1,0:T(8,128)(2,1)S(1)}, bf16[1,1,48,128,128]{4,3,2,1,0:T(8,128)(2,1)}, u32[]{:S(2)}) copy-start(bf16[1,1,48,128,128]{4,3,2,1,0:T(8,128)(2,1)} %param.9) | copy-start | bytes 4718596
  2.2 5.4 %collective-permute-start = (bf16[8,2048]{1,0:T(8,128)(2,1)S(1)}, bf16[8,2048]{1,0:T(8,128)(2,1)S(1)}, u32[]{:S(2)}, u32[]{:S(2)}) collective-permute-start(bf16[8,2048]{1,0:T(8,128)(2,1)S(1)} %constant_dynamic-update-slice_fusion), channel_id=1, source_target_pairs={{0,128},{2,130},{4,132},{6,134},{8,136},{10,138},{12,140},{14,142}... | collective-permute-start | bytes 98312 | tf_op jit(solution)/shard_map/ppermute | solution.py:30
  7.6 9.3 %collective-permute-start.3 = (bf16[16,2048]{1,0:T(8,128)(2,1)S(1)}, bf16[16,2048]{1,0:T(8,128)(2,1)S(1)}, u32[]{:S(2)}, u32[]{:S(2)}) collective-permute-start(bf16[16,2048]{1,0:T(8,128)(2,1)S(1)} %pad_maximum_fusion.1.p0), channel_id=1, source_target_pairs={{0,16},{2,18},{4,20},{6,22},{8,24},{10,26},{12,28},{14,30},{16,0},... | collective-permute-start | bytes 196616 | tf_op jit(solution)/shard_map/ppermute | solution.py:30
  13.9 7.1 %collective-permute-start.2 = (bf16[16,2048]{1,0:T(8,128)(2,1)S(1)}, bf16[16,2048]{1,0:T(8,128)(2,1)S(1)}, u32[]{:S(2)}, u32[]{:S(2)}) collective-permute-start(bf16[16,2048]{1,0:T(8,128)(2,1)S(1)} %pad_maximum_fusion.1.p0), channel_id=1, source_target_pairs={{0,24},{2,26},{4,28},{6,30},{8,16},{10,18},{12,20},{14,22},{16,8},... | collective-permute-start | bytes 196616 | tf_op jit(solution)/shard_map/ppermute | solution.py:30
  14.5 6.5 %collective-permute-start.1 = (bf16[16,2048]{1,0:T(8,128)(2,1)S(1)}, bf16[16,2048]{1,0:T(8,128)(2,1)S(1)}, u32[]{:S(2)}, u32[]{:S(2)}) collective-permute-start(bf16[16,2048]{1,0:T(8,128)(2,1)S(1)} %pad_maximum_fusion.1.p0), channel_id=1, source_target_pairs={{0,8},{2,10},{4,12},{6,14},{8,0},{10,2},{12,4},{14,6},{16,24},{18,... | collective-permute-start | bytes 196616 | tf_op jit(solution)/shard_map/ppermute | solution.py:30
  21.0 13.5 %collective-permute-start.6 = (bf16[64,2048]{1,0:T(8,128)(2,1)S(1)}, bf16[64,2048]{1,0:T(8,128)(2,1)S(1)}, u32[]{:S(2)}, u32[]{:S(2)}) collective-permute-start(bf16[64,2048]{1,0:T(8,128)(2,1)S(1)} %shard_map.94.p0), channel_id=1, source_target_pairs={{0,64},{2,66},{4,68},{6,70},{8,72},{10,74},{12,76},{14,78},{16,80}... | collective-permute-start | bytes 786440 | tf_op jit(solution)/shard_map/ppermute | solution.py:30
  24.2 10.4 %collective-permute-start.5 = (bf16[64,2048]{1,0:T(8,128)(2,1)S(1)}, bf16[64,2048]{1,0:T(8,128)(2,1)S(1)}, u32[]{:S(2)}, u32[]{:S(2)}) collective-permute-start(bf16[64,2048]{1,0:T(8,128)(2,1)S(1)} %shard_map.94.p0), channel_id=1, source_target_pairs={{0,96},{2,98},{4,100},{6,102},{8,104},{10,106},{12,108},{14,110},{... | collective-permute-start | bytes 786440 | tf_op jit(solution)/shard_map/ppermute | solution.py:30
  25.3 9.2 %collective-permute-start.4 = (bf16[64,2048]{1,0:T(8,128)(2,1)S(1)}, bf16[64,2048]{1,0:T(8,128)(2,1)S(1)}, u32[]{:S(2)}, u32[]{:S(2)}) collective-permute-start(bf16[64,2048]{1,0:T(8,128)(2,1)S(1)} %shard_map.94.p0), channel_id=1, source_target_pairs={{0,32},{2,34},{4,36},{6,38},{8,40},{10,42},{12,44},{14,46},{16,48}... | collective-permute-start | bytes 786440 | tf_op jit(solution)/shard_map/ppermute | solution.py:30
  25.3 9.2 %collective-permute-start.8 = (bf16[32,2048]{1,0:T(8,128)(2,1)S(1)}, bf16[32,2048]{1,0:T(8,128)(2,1)S(1)}, u32[]{:S(2)}, u32[]{:S(2)}) collective-permute-start(bf16[32,2048]{1,0:T(8,128)(2,1)S(1)} %get-tuple-element.107), channel_id=1, source_target_pairs={{0,4},{2,6},{4,0},{6,2},{8,12},{10,14},{12,8},{14,10},{16,20},{18,... | collective-permute-start | bytes 393224 | tf_op jit(solution)/shard_map/ppermute | solution.py:30
  25.9 8.6 %collective-permute-start.7 = (bf16[32,2048]{1,0:T(8,128)(2,1)S(1)}, bf16[32,2048]{1,0:T(8,128)(2,1)S(1)}, u32[]{:S(2)}, u32[]{:S(2)}) collective-permute-start(bf16[32,2048]{1,0:T(8,128)(2,1)S(1)} %get-tuple-element.108), channel_id=1, source_target_pairs={{0,4},{2,6},{4,0},{6,2},{8,12},{10,14},{12,8},{14,10},{16,20},{18,... | collective-permute-start | bytes 393224 | tf_op jit(solution)/shard_map/ppermute | solution.py:30
  27.9 1.4 %copy-start.2 = (bf16[1,1,48,128,128]{4,3,2,1,0:T(8,128)(2,1)S(1)}, bf16[1,1,48,128,128]{4,3,2,1,0:T(8,128)(2,1)}, u32[]{:S(2)}) copy-start(bf16[1,1,48,128,128]{4,3,2,1,0:T(8,128)(2,1)} %param.10) | copy-start | bytes 4718596
  36.4 3.9 %collective-permute-start.9 = (f32[128,2688]{1,0:T(8,128)S(1)}, f32[128,2688]{1,0:T(8,128)S(1)}, u32[]{:S(2)}, u32[]{:S(2)}) collective-permute-start(f32[128,2688]{1,0:T(8,128)S(1)} %shard_map.97), channel_id=1, source_target_pairs={{0,2},{2,0},{4,6},{6,4},{8,10},{10,8},{12,14},{14,12},{16,18},{18,... | collective-permute-start | bytes 4128776 | tf_op jit(solution)/shard_map/ppermute | solution.py:30
  38.4 9.1 %collective-permute-start.13 = (bf16[64,2048]{1,0:T(8,128)(2,1)S(1)}, bf16[64,2048]{1,0:T(8,128)(2,1)S(1)}, u32[]{:S(2)}, u32[]{:S(2)}) collective-permute-start(bf16[64,2048]{1,0:T(8,128)(2,1)S(1)} %pad_maximum_fusion.p0), channel_id=1, source_target_pairs={{0,32},{2,34},{4,36},{6,38},{8,40},{10,42},{12,44},{14,46},{16,48}... | collective-permute-start | bytes 786440 | tf_op jit(solution)/shard_map/ppermute | solution.py:30
  41.2 8.9 %collective-permute-start.10 = (s16[32,2816]{1,0:T(8,128)(2,1)S(1)}, s16[32,2816]{1,0:T(8,128)(2,1)S(1)}, u32[]{:S(2)}, u32[]{:S(2)}) collective-permute-start(s16[32,2816]{1,0:T(8,128)(2,1)S(1)} %get-tuple-element.56), channel_id=1, source_target_pairs={{0,5},{1,4},{2,7},{3,6},{4,1},{5,0},{6,3},{7,2},{8,13},{9,12},{10,... | collective-permute-start | bytes 540680 | tf_op jit(solution)/shard_map/ppermute | solution.py:35
  42.9 9.8 %collective-permute-start.11 = (s16[32,2816]{1,0:T(8,128)(2,1)S(1)}, s16[32,2816]{1,0:T(8,128)(2,1)S(1)}, u32[]{:S(2)}, u32[]{:S(2)}) collective-permute-start(s16[32,2816]{1,0:T(8,128)(2,1)S(1)} %get-tuple-element.57), channel_id=1, source_target_pairs={{0,1},{1,0},{2,3},{3,2},{4,5},{5,4},{6,7},{7,6},{8,9},{9,8},{10,11... | collective-permute-start | bytes 540680 | tf_op jit(solution)/shard_map/ppermute | solution.py:35
  43.5 9.3 %collective-permute-start.12 = (s16[32,2816]{1,0:T(8,128)(2,1)S(1)}, s16[32,2816]{1,0:T(8,128)(2,1)S(1)}, u32[]{:S(2)}, u32[]{:S(2)}) collective-permute-start(s16[32,2816]{1,0:T(8,128)(2,1)S(1)} %get-tuple-element.58), channel_id=1, source_target_pairs={{0,4},{1,5},{2,6},{3,7},{4,0},{5,1},{6,2},{7,3},{8,12},{9,13},{10,... | collective-permute-start | bytes 540680 | tf_op jit(solution)/shard_map/ppermute | solution.py:35
  44.8 11.9 %collective-permute-start.18 = (bf16[64,2048]{1,0:T(8,128)(2,1)S(1)}, bf16[64,2048]{1,0:T(8,128)(2,1)S(1)}, u32[]{:S(2)}, u32[]{:S(2)}) collective-permute-start(bf16[64,2048]{1,0:T(8,128)(2,1)S(1)} %pad_maximum_fusion.p0), channel_id=1, source_target_pairs={{0,64},{2,66},{4,68},{6,70},{8,72},{10,74},{12,76},{14,78},{16,80}... | collective-permute-start | bytes 786440 | tf_op jit(solution)/shard_map/ppermute | solution.py:30
  47.6 12.6 %collective-permute-start.17 = (bf16[64,2048]{1,0:T(8,128)(2,1)S(1)}, bf16[64,2048]{1,0:T(8,128)(2,1)S(1)}, u32[]{:S(2)}, u32[]{:S(2)}) collective-permute-start(bf16[64,2048]{1,0:T(8,128)(2,1)S(1)} %pad_maximum_fusion.p0), channel_id=1, source_target_pairs={{0,96},{2,98},{4,100},{6,102},{8,104},{10,106},{12,108},{14,110},{... | collective-permute-start | bytes 786440 | tf_op jit(solution)/shard_map/ppermute | solution.py:30
  53.1 8.3 %collective-permute-start.16 = (bf16[32,2688]{1,0:T(8,128)(2,1)S(1)}, bf16[32,2688]{1,0:T(8,128)(2,1)S(1)}, u32[]{:S(2)}, u32[]{:S(2)}) collective-permute-start(bf16[32,2688]{1,0:T(8,128)(2,1)S(1)} %shard_map.100), channel_id=1, source_target_pairs={{0,5},{1,4},{2,7},{3,6},{4,1},{5,0},{6,3},{7,2},{8,13},{9,12},{10,... | collective-permute-start | bytes 516104 | tf_op jit(solution)/shard_map/ppermute | solution.py:35
  54.6 8.4 %collective-permute-start.15 = (bf16[32,2688]{1,0:T(8,128)(2,1)S(1)}, bf16[32,2688]{1,0:T(8,128)(2,1)S(1)}, u32[]{:S(2)}, u32[]{:S(2)}) collective-permute-start(bf16[32,2688]{1,0:T(8,128)(2,1)S(1)} %shard_map.100), channel_id=1, source_target_pairs={{0,4},{1,5},{2,6},{3,7},{4,0},{5,1},{6,2},{7,3},{8,12},{9,13},{10,... | collective-permute-start | bytes 516104 | tf_op jit(solution)/shard_map/ppermute | solution.py:35
  55.6 8.3 %collective-permute-start.14 = (bf16[32,2688]{1,0:T(8,128)(2,1)S(1)}, bf16[32,2688]{1,0:T(8,128)(2,1)S(1)}, u32[]{:S(2)}, u32[]{:S(2)}) collective-permute-start(bf16[32,2688]{1,0:T(8,128)(2,1)S(1)} %shard_map.100), channel_id=1, source_target_pairs={{0,1},{1,0},{2,3},{3,2},{4,5},{5,4},{6,7},{7,6},{8,9},{9,8},{10,11... | collective-permute-start | bytes 516104 | tf_op jit(solution)/shard_map/ppermute | solution.py:35
  56.6 9.6 %collective-permute-start.20 = (bf16[16,128,256]{2,1,0:T(8,128)(2,1)S(1)}, bf16[16,128,256]{2,1,0:T(8,128)(2,1)S(1)}, u32[]{:S(2)}, u32[]{:S(2)}) collective-permute-start(bf16[16,128,256]{2,1,0:T(8,128)(2,1)S(1)} %shard_map.99.s0), channel_id=1, source_target_pairs={{0,2},{2,0},{4,6},{6,4},{8,10},{10,8},{12,14},{14,12},{16,18},{18,... | collective-permute-start | bytes 3145736 | tf_op jit(solution)/shard_map/ppermute | solution.py:30
  64.0 2.2 %collective-permute-start.19 = (bf16[128,2688]{1,0:T(8,128)(2,1)S(1)}, bf16[128,2688]{1,0:T(8,128)(2,1)S(1)}, u32[]{:S(2)}, u32[]{:S(2)}) collective-permute-start(bf16[128,2688]{1,0:T(8,128)(2,1)S(1)} %constant_dynamic-update-slice_fusion.2.mine), channel_id=1, source_target_pairs={{0,2},{2,0},{4,6},{6,4},{8,10},{10,8},{12,14},{14,12},{16,18},{18,... | collective-permute-start | bytes 2064392 | tf_op jit(solution)/shard_map/ppermute | solution.py:30
  68.7 4.3 %collective-permute-start.24 = (bf16[16,128,256]{2,1,0:T(8,128)(2,1)S(1)}, bf16[16,128,256]{2,1,0:T(8,128)(2,1)S(1)}, u32[]{:S(2)}, u32[]{:S(2)}) collective-permute-start(bf16[16,128,256]{2,1,0:T(8,128)(2,1)S(1)} %shard_map.101.s2), channel_id=1, source_target_pairs={{0,2},{2,0},{4,6},{6,4},{8,10},{10,8},{12,14},{14,12},{16,18},{18,... | collective-permute-start | bytes 3145736 | tf_op jit(solution)/shard_map/ppermute | solution.py:30
  68.9 10.7 %collective-permute-start.21 = (bf16[64,2048]{1,0:T(8,128)(2,1)S(1)}, bf16[64,2048]{1,0:T(8,128)(2,1)S(1)}, u32[]{:S(2)}, u32[]{:S(2)}) collective-permute-start(bf16[64,2048]{1,0:T(8,128)(2,1)S(1)} %get-tuple-element.80), channel_id=1, source_target_pairs={{0,64},{2,66},{4,68},{6,70},{8,72},{10,74},{12,76},{14,78},{16,80}... | collective-permute-start | bytes 786440 | tf_op jit(solution)/shard_map/ppermute | solution.py:30
  71.7 12.6 %collective-permute-start.22 = (bf16[64,2048]{1,0:T(8,128)(2,1)S(1)}, bf16[64,2048]{1,0:T(8,128)(2,1)S(1)}, u32[]{:S(2)}, u32[]{:S(2)}) collective-permute-start(bf16[64,2048]{1,0:T(8,128)(2,1)S(1)} %get-tuple-element.81), channel_id=1, source_target_pairs={{0,32},{2,34},{4,36},{6,38},{8,40},{10,42},{12,44},{14,46},{16,48}... | collective-permute-start | bytes 786440 | tf_op jit(solution)/shard_map/ppermute | solution.py:30
  72.1 12.5 %collective-permute-start.23 = (bf16[64,2048]{1,0:T(8,128)(2,1)S(1)}, bf16[64,2048]{1,0:T(8,128)(2,1)S(1)}, u32[]{:S(2)}, u32[]{:S(2)}) collective-permute-start(bf16[64,2048]{1,0:T(8,128)(2,1)S(1)} %get-tuple-element.82), channel_id=1, source_target_pairs={{0,96},{2,98},{4,100},{6,102},{8,104},{10,106},{12,108},{14,110},{... | collective-permute-start | bytes 786440 | tf_op jit(solution)/shard_map/ppermute | solution.py:30
  84.8 9.9 %collective-permute-start.25 = (bf16[16,2048]{1,0:T(8,128)(2,1)S(1)}, bf16[16,2048]{1,0:T(8,128)(2,1)S(1)}, u32[]{:S(2)}, u32[]{:S(2)}) collective-permute-start(bf16[16,2048]{1,0:T(8,128)(2,1)S(1)} %get-tuple-element.104), channel_id=1, source_target_pairs={{0,16},{2,18},{4,20},{6,22},{8,24},{10,26},{12,28},{14,30},{16,0},... | collective-permute-start | bytes 196616 | tf_op jit(solution)/shard_map/ppermute | solution.py:30
  88.6 8.2 %collective-permute-start.27 = (bf16[16,2048]{1,0:T(8,128)(2,1)S(1)}, bf16[16,2048]{1,0:T(8,128)(2,1)S(1)}, u32[]{:S(2)}, u32[]{:S(2)}) collective-permute-start(bf16[16,2048]{1,0:T(8,128)(2,1)S(1)} %get-tuple-element.105), channel_id=1, source_target_pairs={{0,24},{2,26},{4,28},{6,30},{8,16},{10,18},{12,20},{14,22},{16,8},... | collective-permute-start | bytes 196616 | tf_op jit(solution)/shard_map/ppermute | solution.py:30
  89.8 7.0 %collective-permute-start.26 = (bf16[16,2048]{1,0:T(8,128)(2,1)S(1)}, bf16[16,2048]{1,0:T(8,128)(2,1)S(1)}, u32[]{:S(2)}, u32[]{:S(2)}) collective-permute-start(bf16[16,2048]{1,0:T(8,128)(2,1)S(1)} %get-tuple-element.106), channel_id=1, source_target_pairs={{0,8},{2,10},{4,12},{6,14},{8,0},{10,2},{12,4},{14,6},{16,24},{18,... | collective-permute-start | bytes 196616 | tf_op jit(solution)/shard_map/ppermute | solution.py:30
  96.8 5.5 %collective-permute-start.28 = (bf16[8,2048]{1,0:T(8,128)(2,1)S(1)}, bf16[8,2048]{1,0:T(8,128)(2,1)S(1)}, u32[]{:S(2)}, u32[]{:S(2)}) collective-permute-start(bf16[8,2048]{1,0:T(8,128)(2,1)S(1)} %slice.73), channel_id=1, source_target_pairs={{0,128},{2,130},{4,132},{6,134},{8,136},{10,138},{12,140},{14,142}... | collective-permute-start | bytes 98312 | tf_op jit(solution)/shard_map/ppermute | solution.py:30
  (1 other events, 1.4 us)

commit v7 on v6

--- a/solution.py
+++ b/solution.py
@@ -223,7 +223,7 @@
     own_index = lax.dynamic_index_in_dim(all_index, row, axis=1, keepdims=False)
 
     tie = lax.optimization_barrier
-    shard = jnp.concatenate([activations, out_grad], axis=1)
+    shard = jnp.pad(activations, ((0, 0), (0, DQ))) + jnp.pad(out_grad, ((0, 0), (DQ, 0)))
     pair = jnp.concatenate([shard, row_swap(shard, Y_MASK)], axis=0)
     near = stack([pair] + [row_swap(pair, z_mask(i)) for i in ORDER])
     pieces = [near] + [row_swap(near, x_mask(i)) for i in ORDER]
@@ -306,8 +306,10 @@
     for at in (3, 1, 2):
         part = total[at * 2 * TG : (at + 1) * 2 * TG].astype(BF)
         last = last + row_swap(part, z_mask(ORDER[at - 1])).astype(F32)
-    got = row_swap(last[TG:].astype(BF), Y_MASK).astype(F32)
-    mixed_rows, input_grad = [(last[:TG, c] + got[:, c]).astype(BF) for c in (slice(0, DQ), slice(DQ, 2 * DQ))]
+    got = row_swap(last[TG:].astype(BF), Y_MASK)
+    mixed_rows, input_grad = [
+        (last[:TG, c] + got[:, c].astype(F32)).astype(BF) for c in (slice(0, DQ), slice(DQ, 2 * DQ))
+    ]
     return mixed_rows, input_grad, grads.reshape(3, 1, 1, CAP, BLK, BLK)
 
 

time: 104 us -> 104 us (level)
  local copies, waits for them, and re-layouts: 6.28 us -> 4.72 us
    unnamed x12 -> x11, local copies, waits for them, and re-layouts: 3.72 us -> 2.88 us
where the time goes in v7:
time: 104 us; the launch traced here: 102 us
  starting transfers between devices  45.2 us (43%)
  waiting for transfers between devices  31.4 us (30%)
  Pallas kernels  17.9 us (17%)
  local copies, waits for them, and re-layouts  4.72 us (5%)
  other arithmetic  1.96 us (2%)
    ppermute x23, starting transfers between devices, row_swap(): return lax.ppermute(value, 'row', [(i, i ^ mask) for i in range(128)])  38.1 us
    ppermute x23, waiting for transfers between devices, row_swap(): return lax.ppermute(value, 'row', [(i, i ^ mask) for i in range(128)])  24.9 us
    ppermute x6, starting transfers between devices, square_swap(): lax.ppermute(value, ('row', 'col'), [(i, i ^ mask) for i in range(256)])  7.15 us
    ppermute x6, waiting for transfers between devices, square_swap(): lax.ppermute(value, ('row', 'col'), [(i, i ^ mask) for i in range(256)])  6.53 us
    pallas_call x1, Pallas kernels, body(): call(grad_kernel, sds((3, CAP, BLK, BLK), BF), [SMEM] + [VMEM] * 5, out_s...  6.21 us
    pallas_call x1, Pallas kernels, body(): call(dense_kernel, wide, [SMEM] + [VMEM] * 3)  3.88 us
    pallas_call x2, Pallas kernels, partial(): call(functools.partial(partial_kernel, other=other), half, [SMEM] + [VMEM...  3.77 us
    unnamed x11, local copies, waits for them, and re-layouts  2.88 us
  transfers between devices with their start and end apart: 29, of which 16 were waited for; matrix products, arithmetic and copies ran while one was open for 2% of the time, Pallas kernels for 13%

profile of v7, /device:TPU:32, one launch (start us, length us, event | category | flops | bytes accessed | tf_op | source)
XLA Modules:
  0.0 102.1 jit_solution(3018517571873826393)
XLA Ops:
  1.5 3.2 %collective-permute-start = (bf16[8,2048]{1,0:T(8,128)(2,1)S(1)}, bf16[8,2048]{1,0:T(8,128)(2,1)S(1)}, u32[]{:S(2)}, u32[]{:S(2)}) collective-permute-start(bf16[8,2048]{1,0:T(8,128)(2,1)S(1)} %pad_add_fusion), channel_id=1, source_target_pairs={{0,128},{2,130},{4,132},{6,134},{8,136},{10,138},{12,140},{14,142}... | collective-permute-start | bytes 98312 | tf_op jit(solution)/shard_map/ppermute | solution.py:30
  6.9 6.3 %collective-permute-start.3 = (bf16[16,2048]{1,0:T(8,128)(2,1)S(1)}, bf16[16,2048]{1,0:T(8,128)(2,1)S(1)}, u32[]{:S(2)}, u32[]{:S(2)}) collective-permute-start(bf16[16,2048]{1,0:T(8,128)(2,1)S(1)} %pad_maximum_fusion.1.p0), channel_id=1, source_target_pairs={{0,16},{2,18},{4,20},{6,22},{8,24},{10,26},{12,28},{14,30},{16,0},... | collective-permute-start | bytes 196616 | tf_op jit(solution)/shard_map/ppermute | solution.py:30
  14.7 1.6 %collective-permute-done.3.p3 = bf16[16,2048]{1,0:T(8,128)(2,1)S(1)} collective-permute-done((bf16[16,2048]{1,0:T(8,128)(2,1)S(1)}, bf16[16,2048]{1,0:T(8,128)(2,1)S(1)}, u32[]{:S(2)}, u32[]{:S(2)}) %collective-permute-start.3) | collective-permute-done | bytes 65568 | tf_op jit(solution)/shard_map/ppermute | solution.py:30
  16.3 4.0 %collective-permute-done.2.p2 = bf16[16,2048]{1,0:T(8,128)(2,1)S(1)} collective-permute-done((bf16[16,2048]{1,0:T(8,128)(2,1)S(1)}, bf16[16,2048]{1,0:T(8,128)(2,1)S(1)}, u32[]{:S(2)}, u32[]{:S(2)}) %collective-permute-start.2) | collective-permute-done | bytes 65568 | tf_op jit(solution)/shard_map/ppermute | solution.py:30
  20.3 3.1 %collective-permute-start.6 = (bf16[64,2048]{1,0:T(8,128)(2,1)S(1)}, bf16[64,2048]{1,0:T(8,128)(2,1)S(1)}, u32[]{:S(2)}, u32[]{:S(2)}) collective-permute-start(bf16[64,2048]{1,0:T(8,128)(2,1)S(1)} %shard_map.94.p0), channel_id=1, source_target_pairs={{0,64},{2,66},{4,68},{6,70},{8,72},{10,74},{12,76},{14,78},{16,80}... | collective-permute-start | bytes 786440 | tf_op jit(solution)/shard_map/ppermute | solution.py:30
  25.2 1.6 %collective-permute-start.7 = (bf16[32,2048]{1,0:T(8,128)(2,1)S(1)}, bf16[32,2048]{1,0:T(8,128)(2,1)S(1)}, u32[]{:S(2)}, u32[]{:S(2)}) collective-permute-start(bf16[32,2048]{1,0:T(8,128)(2,1)S(1)} %get-tuple-element.108), channel_id=1, source_target_pairs={{0,4},{2,6},{4,0},{6,2},{8,12},{10,14},{12,8},{14,10},{16,20},{18,... | collective-permute-start | bytes 393224 | tf_op jit(solution)/shard_map/ppermute | solution.py:30
  27.2 1.4 %copy-done.2 = bf16[1,1,48,128,128]{4,3,2,1,0:T(8,128)(2,1)S(1)} copy-done((bf16[1,1,48,128,128]{4,3,2,1,0:T(8,128)(2,1)S(1)}, bf16[1,1,48,128,128]{4,3,2,1,0:T(8,128)(2,1)}, u32[]{:S(2)}) %copy-start.2) | copy-done | bytes 1572888
  28.6 1.4 %copy-done.3 = bf16[1,1,48,128,128]{4,3,2,1,0:T(8,128)(2,1)S(1)} copy-done((bf16[1,1,48,128,128]{4,3,2,1,0:T(8,128)(2,1)S(1)}, bf16[1,1,48,128,128]{4,3,2,1,0:T(8,128)(2,1)}, u32[]{:S(2)}) %copy-start.3) | copy-done | bytes 1572888
  30.0 3.9 %shard_map.95 = (bf16[1024,896]{1,0:T(8,128)(2,1)S(1)}, bf16[1024,896]{1,0:T(8,128)(2,1)S(1)}, bf16[896,1024]{1,0:T(8,128)(2,1)S(1)}) custom-call(s32[3,48]{1,0:T(4,128)S(1)} %dynamic-slice_reduce_fusion.index_ref, bf16[48,128,128]{2,1,0:T(8,128)(2,1)S(1)} %bitcast.12, bf16[48,128,128]{2,1,0:T(8,128)(2,1)S(1)} %bitcast.13, bf16[48,128,128]{2,1,0:T(8,128)(2,1)S(1)} %bitcast.14), custom_call_target="tpu_custom_call" | custom-call | tf_op jit(solution)/shard_map/pallas_call | solution.py:233
  34.2 1.9 %shard_map.97 = f32[128,2688]{1,0:T(8,128)S(1)} custom-call(s32[2]{0:T(128)S(1)} %pad_add_fusion.1.place_ref, bf16[64,2048]{1,0:T(8,128)(2,1)S(1)} %shard_map.94.p0, bf16[64,2048]{1,0:T(8,128)(2,1)S(1)} %collective-permute-done.4.p1, bf16[64,2048]{1,0:T(8,128)(2,1)S(1)} %collective-permute-done.5.p2, bf16[64,2048]{1,0:T(8,128)(2,1)S(1)} %collective-permute-done.6.p3, ...), custom_call_target="tpu_custom_call" | custom-call | tf_op jit(solution)/shard_map/pallas_call | solution.py:252
  36.2 1.9 %shard_map.96.keep_ref = f32[128,2688]{1,0:T(8,128)S(1)} custom-call(s32[2]{0:T(128)S(1)} %pad_add_fusion.1.place_ref, bf16[64,2048]{1,0:T(8,128)(2,1)S(1)} %shard_map.94.p0, bf16[64,2048]{1,0:T(8,128)(2,1)S(1)} %collective-permute-done.4.p1, bf16[64,2048]{1,0:T(8,128)(2,1)S(1)} %collective-permute-done.5.p2, ...), custom_call_target="tpu_custom_call" | custom-call | tf_op jit(solution)/shard_map/pallas_call | solution.py:252
  38.1 1.8 %collective-permute-start.13 = (bf16[64,2048]{1,0:T(8,128)(2,1)S(1)}, bf16[64,2048]{1,0:T(8,128)(2,1)S(1)}, u32[]{:S(2)}, u32[]{:S(2)}) collective-permute-start(bf16[64,2048]{1,0:T(8,128)(2,1)S(1)} %pad_maximum_fusion.p0), channel_id=1, source_target_pairs={{0,32},{2,34},{4,36},{6,38},{8,40},{10,42},{12,44},{14,46},{16,48}... | collective-permute-start | bytes 786440 | tf_op jit(solution)/shard_map/ppermute | solution.py:30
  40.8 1.4 %collective-permute-start.10 = (s16[32,2816]{1,0:T(8,128)(2,1)S(1)}, s16[32,2816]{1,0:T(8,128)(2,1)S(1)}, u32[]{:S(2)}, u32[]{:S(2)}) collective-permute-start(s16[32,2816]{1,0:T(8,128)(2,1)S(1)} %get-tuple-element.56), channel_id=1, source_target_pairs={{0,5},{1,4},{2,7},{3,6},{4,1},{5,0},{6,3},{7,2},{8,13},{9,12},{10,... | collective-permute-start | bytes 540680 | tf_op jit(solution)/shard_map/ppermute | solution.py:35
  42.8 1.5 %collective-permute-start.12 = (s16[32,2816]{1,0:T(8,128)(2,1)S(1)}, s16[32,2816]{1,0:T(8,128)(2,1)S(1)}, u32[]{:S(2)}, u32[]{:S(2)}) collective-permute-start(s16[32,2816]{1,0:T(8,128)(2,1)S(1)} %get-tuple-element.58), channel_id=1, source_target_pairs={{0,4},{1,5},{2,6},{3,7},{4,0},{5,1},{6,2},{7,3},{8,12},{9,13},{10,... | collective-permute-start | bytes 540680 | tf_op jit(solution)/shard_map/ppermute | solution.py:35
  44.4 2.8 %collective-permute-start.18 = (bf16[64,2048]{1,0:T(8,128)(2,1)S(1)}, bf16[64,2048]{1,0:T(8,128)(2,1)S(1)}, u32[]{:S(2)}, u32[]{:S(2)}) collective-permute-start(bf16[64,2048]{1,0:T(8,128)(2,1)S(1)} %pad_maximum_fusion.p0), channel_id=1, source_target_pairs={{0,64},{2,66},{4,68},{6,70},{8,72},{10,74},{12,76},{14,78},{16,80}... | collective-permute-start | bytes 786440 | tf_op jit(solution)/shard_map/ppermute | solution.py:30
  47.1 2.2 %collective-permute-start.17 = (bf16[64,2048]{1,0:T(8,128)(2,1)S(1)}, bf16[64,2048]{1,0:T(8,128)(2,1)S(1)}, u32[]{:S(2)}, u32[]{:S(2)}) collective-permute-start(bf16[64,2048]{1,0:T(8,128)(2,1)S(1)} %pad_maximum_fusion.p0), channel_id=1, source_target_pairs={{0,96},{2,98},{4,100},{6,102},{8,104},{10,106},{12,108},{14,110},{... | collective-permute-start | bytes 786440 | tf_op jit(solution)/shard_map/ppermute | solution.py:30
  49.6 2.7 %collective-permute-done.11.a2 = s16[32,2816]{1,0:T(8,128)(2,1)S(1)} collective-permute-done((s16[32,2816]{1,0:T(8,128)(2,1)S(1)}, s16[32,2816]{1,0:T(8,128)(2,1)S(1)}, u32[]{:S(2)}, u32[]{:S(2)}) %collective-permute-start.11) | collective-permute-done | bytes 180256 | tf_op jit(solution)/shard_map/ppermute | solution.py:35
  52.6 1.3 %collective-permute-start.16 = (bf16[32,2688]{1,0:T(8,128)(2,1)S(1)}, bf16[32,2688]{1,0:T(8,128)(2,1)S(1)}, u32[]{:S(2)}, u32[]{:S(2)}) collective-permute-start(bf16[32,2688]{1,0:T(8,128)(2,1)S(1)} %shard_map.100), channel_id=1, source_target_pairs={{0,5},{1,4},{2,7},{3,6},{4,1},{5,0},{6,3},{7,2},{8,13},{9,12},{10,... | collective-permute-start | bytes 516104 | tf_op jit(solution)/shard_map/ppermute | solution.py:35
  54.9 1.3 %collective-permute-start.14 = (bf16[32,2688]{1,0:T(8,128)(2,1)S(1)}, bf16[32,2688]{1,0:T(8,128)(2,1)S(1)}, u32[]{:S(2)}, u32[]{:S(2)}) collective-permute-start(bf16[32,2688]{1,0:T(8,128)(2,1)S(1)} %shard_map.100), channel_id=1, source_target_pairs={{0,1},{1,0},{2,3},{3,2},{4,5},{5,4},{6,7},{7,6},{8,9},{9,8},{10,11... | collective-permute-start | bytes 516104 | tf_op jit(solution)/shard_map/ppermute | solution.py:35
  56.2 3.6 %collective-permute-done.17.p2 = bf16[64,2048]{1,0:T(8,128)(2,1)S(1)} collective-permute-done((bf16[64,2048]{1,0:T(8,128)(2,1)S(1)}, bf16[64,2048]{1,0:T(8,128)(2,1)S(1)}, u32[]{:S(2)}, u32[]{:S(2)}) %collective-permute-start.17) | collective-permute-done | bytes 262176 | tf_op jit(solution)/shard_map/ppermute | solution.py:30
  62.1 1.4 %collective-permute-done.14 = bf16[32,2688]{1,0:T(8,128)(2,1)S(1)} collective-permute-done((bf16[32,2688]{1,0:T(8,128)(2,1)S(1)}, bf16[32,2688]{1,0:T(8,128)(2,1)S(1)}, u32[]{:S(2)}, u32[]{:S(2)}) %collective-permute-start.14) | collective-permute-done | bytes 172064 | tf_op jit(solution)/shard_map/ppermute | solution.py:35
  63.9 1.9 %collective-permute-done.19.theirs = bf16[128,2688]{1,0:T(8,128)(2,1)S(1)} collective-permute-done((bf16[128,2688]{1,0:T(8,128)(2,1)S(1)}, bf16[128,2688]{1,0:T(8,128)(2,1)S(1)}, u32[]{:S(2)}, u32[]{:S(2)}) %collective-permute-start.19) | collective-permute-done | bytes 688160 | tf_op jit(solution)/shard_map/ppermute | solution.py:30
  65.8 2.5 %shard_map.102 = (f32[64,2048]{1,0:T(8,128)S(1)}, bf16[64,2048]{1,0:T(8,128)(2,1)S(1)}, bf16[64,2048]{1,0:T(8,128)(2,1)S(1)}, bf16[64,2048]{1,0:T(8,128)(2,1)S(1)}, bf16[256,2688]{1,0:T(8,128)(2,1)S(1)}) custom-call(s32[2]{0:T(128)S(1)} %pad_add_fusion.1.place_ref, bf16[128,2688]{1,0:T(8,128)(2,1)S(1)} %constant_dynamic-update-slice_fusion.mine, ...), custom_call_target="tpu_custom_call" | custom-call | tf_op jit(solution)/shard_map/pallas_call | solution.py:279
  68.5 2.4 %collective-permute-start.21 = (bf16[64,2048]{1,0:T(8,128)(2,1)S(1)}, bf16[64,2048]{1,0:T(8,128)(2,1)S(1)}, u32[]{:S(2)}, u32[]{:S(2)}) collective-permute-start(bf16[64,2048]{1,0:T(8,128)(2,1)S(1)} %get-tuple-element.80), channel_id=1, source_target_pairs={{0,64},{2,66},{4,68},{6,70},{8,72},{10,74},{12,76},{14,78},{16,80}... | collective-permute-start | bytes 786440 | tf_op jit(solution)/shard_map/ppermute | solution.py:30
  72.6 6.2 %shard_map.103 = bf16[3,48,128,128]{3,2,1,0:T(8,128)(2,1)} custom-call(s32[3,48]{1,0:T(4,128)S(1)} %select_reduce_fusion.code_ref, bf16[256,2688]{1,0:T(8,128)(2,1)S(1)} %get-tuple-element.86.full, bf16[16,128,256]{2,1,0:T(8,128)(2,1)S(1)} %shard_map.99.s0, bf16[16,128,256]{2,1,0:T(8,128)(2,1)S(1)} %collective-permute-done.20.s1, ...), custom_call_target="tpu_custom_call" | custom-call | tf_op jit(solution)/shard_map/pallas_call | solution.py:289
  79.2 4.4 %collective-permute-done.22 = bf16[64,2048]{1,0:T(8,128)(2,1)S(1)} collective-permute-done((bf16[64,2048]{1,0:T(8,128)(2,1)S(1)}, bf16[64,2048]{1,0:T(8,128)(2,1)S(1)}, u32[]{:S(2)}, u32[]{:S(2)}) %collective-permute-start.22) | collective-permute-done | bytes 262176 | tf_op jit(solution)/shard_map/ppermute | solution.py:30
  84.4 3.6 %collective-permute-start.25 = (bf16[16,2048]{1,0:T(8,128)(2,1)S(1)}, bf16[16,2048]{1,0:T(8,128)(2,1)S(1)}, u32[]{:S(2)}, u32[]{:S(2)}) collective-permute-start(bf16[16,2048]{1,0:T(8,128)(2,1)S(1)} %get-tuple-element.104), channel_id=1, source_target_pairs={{0,16},{2,18},{4,20},{6,22},{8,24},{10,26},{12,28},{14,30},{16,0},... | collective-permute-start | bytes 196616 | tf_op jit(solution)/shard_map/ppermute | solution.py:30
  89.0 1.9 %collective-permute-start.26 = (bf16[16,2048]{1,0:T(8,128)(2,1)S(1)}, bf16[16,2048]{1,0:T(8,128)(2,1)S(1)}, u32[]{:S(2)}, u32[]{:S(2)}) collective-permute-start(bf16[16,2048]{1,0:T(8,128)(2,1)S(1)} %get-tuple-element.106), channel_id=1, source_target_pairs={{0,8},{2,10},{4,12},{6,14},{8,0},{10,2},{12,4},{14,6},{16,24},{18,... | collective-permute-start | bytes 196616 | tf_op jit(solution)/shard_map/ppermute | solution.py:30
  91.0 3.4 %collective-permute-done.25 = bf16[16,2048]{1,0:T(8,128)(2,1)S(1)} collective-permute-done((bf16[16,2048]{1,0:T(8,128)(2,1)S(1)}, bf16[16,2048]{1,0:T(8,128)(2,1)S(1)}, u32[]{:S(2)}, u32[]{:S(2)}) %collective-permute-start.25) | collective-permute-done | bytes 65568 | tf_op jit(solution)/shard_map/ppermute | solution.py:30
  94.4 1.6 %collective-permute-done.27 = bf16[16,2048]{1,0:T(8,128)(2,1)S(1)} collective-permute-done((bf16[16,2048]{1,0:T(8,128)(2,1)S(1)}, bf16[16,2048]{1,0:T(8,128)(2,1)S(1)}, u32[]{:S(2)}, u32[]{:S(2)}) %collective-permute-start.27) | collective-permute-done | bytes 65568 | tf_op jit(solution)/shard_map/ppermute | solution.py:30
  96.0 2.9 %collective-permute-start.28 = (bf16[8,2048]{1,0:T(8,128)(2,1)S(1)}, bf16[8,2048]{1,0:T(8,128)(2,1)S(1)}, u32[]{:S(2)}, u32[]{:S(2)}) collective-permute-start(bf16[8,2048]{1,0:T(8,128)(2,1)S(1)} %slice.73), channel_id=1, source_target_pairs={{0,128},{2,130},{4,132},{6,134},{8,136},{10,138},{12,140},{14,142}... | collective-permute-start | bytes 98312 | tf_op jit(solution)/shard_map/ppermute | solution.py:30
  98.9 2.6 %collective-permute-done.28 = bf16[8,2048]{1,0:T(8,128)(2,1)S(1)} collective-permute-done((bf16[8,2048]{1,0:T(8,128)(2,1)S(1)}, bf16[8,2048]{1,0:T(8,128)(2,1)S(1)}, u32[]{:S(2)}, u32[]{:S(2)}) %collective-permute-start.28) | collective-permute-done | bytes 32800 | tf_op jit(solution)/shard_map/ppermute | solution.py:30
  (71 shorter events, 17.6 us)
Async XLA Ops:
  0.6 4.2 %copy-start = (s32[3,128,2,48]{1,3,2,0:T(8,128)S(1)}, s32[3,128,2,48]{1,3,2,0:T(8,128)}, u32[]{:S(2)}) copy-start(s32[3,128,2,48]{1,3,2,0:T(8,128)} %param.12) | copy-start | bytes 442372
  0.6 26.6 %copy-start.1 = (bf16[1,1,48,128,128]{4,3,2,1,0:T(8,128)(2,1)S(1)}, bf16[1,1,48,128,128]{4,3,2,1,0:T(8,128)(2,1)}, u32[]{:S(2)}) copy-start(bf16[1,1,48,128,128]{4,3,2,1,0:T(8,128)(2,1)} %param.9) | copy-start | bytes 4718596
  1.5 5.4 %collective-permute-start = (bf16[8,2048]{1,0:T(8,128)(2,1)S(1)}, bf16[8,2048]{1,0:T(8,128)(2,1)S(1)}, u32[]{:S(2)}, u32[]{:S(2)}) collective-permute-start(bf16[8,2048]{1,0:T(8,128)(2,1)S(1)} %pad_add_fusion), channel_id=1, source_target_pairs={{0,128},{2,130},{4,132},{6,134},{8,136},{10,138},{12,140},{14,142}... | collective-permute-start | bytes 98312 | tf_op jit(solution)/shard_map/ppermute | solution.py:30
  6.9 9.3 %collective-permute-start.3 = (bf16[16,2048]{1,0:T(8,128)(2,1)S(1)}, bf16[16,2048]{1,0:T(8,128)(2,1)S(1)}, u32[]{:S(2)}, u32[]{:S(2)}) collective-permute-start(bf16[16,2048]{1,0:T(8,128)(2,1)S(1)} %pad_maximum_fusion.1.p0), channel_id=1, source_target_pairs={{0,16},{2,18},{4,20},{6,22},{8,24},{10,26},{12,28},{14,30},{16,0},... | collective-permute-start | bytes 196616 | tf_op jit(solution)/shard_map/ppermute | solution.py:30
  13.2 7.1 %collective-permute-start.2 = (bf16[16,2048]{1,0:T(8,128)(2,1)S(1)}, bf16[16,2048]{1,0:T(8,128)(2,1)S(1)}, u32[]{:S(2)}, u32[]{:S(2)}) collective-permute-start(bf16[16,2048]{1,0:T(8,128)(2,1)S(1)} %pad_maximum_fusion.1.p0), channel_id=1, source_target_pairs={{0,24},{2,26},{4,28},{6,30},{8,16},{10,18},{12,20},{14,22},{16,8},... | collective-permute-start | bytes 196616 | tf_op jit(solution)/shard_map/ppermute | solution.py:30
  13.8 6.5 %collective-permute-start.1 = (bf16[16,2048]{1,0:T(8,128)(2,1)S(1)}, bf16[16,2048]{1,0:T(8,128)(2,1)S(1)}, u32[]{:S(2)}, u32[]{:S(2)}) collective-permute-start(bf16[16,2048]{1,0:T(8,128)(2,1)S(1)} %pad_maximum_fusion.1.p0), channel_id=1, source_target_pairs={{0,8},{2,10},{4,12},{6,14},{8,0},{10,2},{12,4},{14,6},{16,24},{18,... | collective-permute-start | bytes 196616 | tf_op jit(solution)/shard_map/ppermute | solution.py:30
  20.3 13.8 %collective-permute-start.6 = (bf16[64,2048]{1,0:T(8,128)(2,1)S(1)}, bf16[64,2048]{1,0:T(8,128)(2,1)S(1)}, u32[]{:S(2)}, u32[]{:S(2)}) collective-permute-start(bf16[64,2048]{1,0:T(8,128)(2,1)S(1)} %shard_map.94.p0), channel_id=1, source_target_pairs={{0,64},{2,66},{4,68},{6,70},{8,72},{10,74},{12,76},{14,78},{16,80}... | collective-permute-start | bytes 786440 | tf_op jit(solution)/shard_map/ppermute | solution.py:30
  23.5 10.7 %collective-permute-start.5 = (bf16[64,2048]{1,0:T(8,128)(2,1)S(1)}, bf16[64,2048]{1,0:T(8,128)(2,1)S(1)}, u32[]{:S(2)}, u32[]{:S(2)}) collective-permute-start(bf16[64,2048]{1,0:T(8,128)(2,1)S(1)} %shard_map.94.p0), channel_id=1, source_target_pairs={{0,96},{2,98},{4,100},{6,102},{8,104},{10,106},{12,108},{14,110},{... | collective-permute-start | bytes 786440 | tf_op jit(solution)/shard_map/ppermute | solution.py:30
  24.6 9.6 %collective-permute-start.4 = (bf16[64,2048]{1,0:T(8,128)(2,1)S(1)}, bf16[64,2048]{1,0:T(8,128)(2,1)S(1)}, u32[]{:S(2)}, u32[]{:S(2)}) collective-permute-start(bf16[64,2048]{1,0:T(8,128)(2,1)S(1)} %shard_map.94.p0), channel_id=1, source_target_pairs={{0,32},{2,34},{4,36},{6,38},{8,40},{10,42},{12,44},{14,46},{16,48}... | collective-permute-start | bytes 786440 | tf_op jit(solution)/shard_map/ppermute | solution.py:30
  24.6 9.5 %collective-permute-start.8 = (bf16[32,2048]{1,0:T(8,128)(2,1)S(1)}, bf16[32,2048]{1,0:T(8,128)(2,1)S(1)}, u32[]{:S(2)}, u32[]{:S(2)}) collective-permute-start(bf16[32,2048]{1,0:T(8,128)(2,1)S(1)} %get-tuple-element.107), channel_id=1, source_target_pairs={{0,4},{2,6},{4,0},{6,2},{8,12},{10,14},{12,8},{14,10},{16,20},{18,... | collective-permute-start | bytes 393224 | tf_op jit(solution)/shard_map/ppermute | solution.py:30
  25.2 9.0 %collective-permute-start.7 = (bf16[32,2048]{1,0:T(8,128)(2,1)S(1)}, bf16[32,2048]{1,0:T(8,128)(2,1)S(1)}, u32[]{:S(2)}, u32[]{:S(2)}) collective-permute-start(bf16[32,2048]{1,0:T(8,128)(2,1)S(1)} %get-tuple-element.108), channel_id=1, source_target_pairs={{0,4},{2,6},{4,0},{6,2},{8,12},{10,14},{12,8},{14,10},{16,20},{18,... | collective-permute-start | bytes 393224 | tf_op jit(solution)/shard_map/ppermute | solution.py:30
  27.2 1.4 %copy-start.2 = (bf16[1,1,48,128,128]{4,3,2,1,0:T(8,128)(2,1)S(1)}, bf16[1,1,48,128,128]{4,3,2,1,0:T(8,128)(2,1)}, u32[]{:S(2)}) copy-start(bf16[1,1,48,128,128]{4,3,2,1,0:T(8,128)(2,1)} %param.10) | copy-start | bytes 4718596
  36.1 3.8 %collective-permute-start.9 = (f32[128,2688]{1,0:T(8,128)S(1)}, f32[128,2688]{1,0:T(8,128)S(1)}, u32[]{:S(2)}, u32[]{:S(2)}) collective-permute-start(f32[128,2688]{1,0:T(8,128)S(1)} %shard_map.97), channel_id=1, source_target_pairs={{0,2},{2,0},{4,6},{6,4},{8,10},{10,8},{12,14},{14,12},{16,18},{18,... | collective-permute-start | bytes 4128776 | tf_op jit(solution)/shard_map/ppermute | solution.py:30
  38.1 9.0 %collective-permute-start.13 = (bf16[64,2048]{1,0:T(8,128)(2,1)S(1)}, bf16[64,2048]{1,0:T(8,128)(2,1)S(1)}, u32[]{:S(2)}, u32[]{:S(2)}) collective-permute-start(bf16[64,2048]{1,0:T(8,128)(2,1)S(1)} %pad_maximum_fusion.p0), channel_id=1, source_target_pairs={{0,32},{2,34},{4,36},{6,38},{8,40},{10,42},{12,44},{14,46},{16,48}... | collective-permute-start | bytes 786440 | tf_op jit(solution)/shard_map/ppermute | solution.py:30
  40.8 8.8 %collective-permute-start.10 = (s16[32,2816]{1,0:T(8,128)(2,1)S(1)}, s16[32,2816]{1,0:T(8,128)(2,1)S(1)}, u32[]{:S(2)}, u32[]{:S(2)}) collective-permute-start(s16[32,2816]{1,0:T(8,128)(2,1)S(1)} %get-tuple-element.56), channel_id=1, source_target_pairs={{0,5},{1,4},{2,7},{3,6},{4,1},{5,0},{6,3},{7,2},{8,13},{9,12},{10,... | collective-permute-start | bytes 540680 | tf_op jit(solution)/shard_map/ppermute | solution.py:35
  42.2 10.1 %collective-permute-start.11 = (s16[32,2816]{1,0:T(8,128)(2,1)S(1)}, s16[32,2816]{1,0:T(8,128)(2,1)S(1)}, u32[]{:S(2)}, u32[]{:S(2)}) collective-permute-start(s16[32,2816]{1,0:T(8,128)(2,1)S(1)} %get-tuple-element.57), channel_id=1, source_target_pairs={{0,1},{1,0},{2,3},{3,2},{4,5},{5,4},{6,7},{7,6},{8,9},{9,8},{10,11... | collective-permute-start | bytes 540680 | tf_op jit(solution)/shard_map/ppermute | solution.py:35
  42.8 9.6 %collective-permute-start.12 = (s16[32,2816]{1,0:T(8,128)(2,1)S(1)}, s16[32,2816]{1,0:T(8,128)(2,1)S(1)}, u32[]{:S(2)}, u32[]{:S(2)}) collective-permute-start(s16[32,2816]{1,0:T(8,128)(2,1)S(1)} %get-tuple-element.58), channel_id=1, source_target_pairs={{0,4},{1,5},{2,6},{3,7},{4,0},{5,1},{6,2},{7,3},{8,12},{9,13},{10,... | collective-permute-start | bytes 540680 | tf_op jit(solution)/shard_map/ppermute | solution.py:35
  44.4 11.8 %collective-permute-start.18 = (bf16[64,2048]{1,0:T(8,128)(2,1)S(1)}, bf16[64,2048]{1,0:T(8,128)(2,1)S(1)}, u32[]{:S(2)}, u32[]{:S(2)}) collective-permute-start(bf16[64,2048]{1,0:T(8,128)(2,1)S(1)} %pad_maximum_fusion.p0), channel_id=1, source_target_pairs={{0,64},{2,66},{4,68},{6,70},{8,72},{10,74},{12,76},{14,78},{16,80}... | collective-permute-start | bytes 786440 | tf_op jit(solution)/shard_map/ppermute | solution.py:30
  47.1 12.6 %collective-permute-start.17 = (bf16[64,2048]{1,0:T(8,128)(2,1)S(1)}, bf16[64,2048]{1,0:T(8,128)(2,1)S(1)}, u32[]{:S(2)}, u32[]{:S(2)}) collective-permute-start(bf16[64,2048]{1,0:T(8,128)(2,1)S(1)} %pad_maximum_fusion.p0), channel_id=1, source_target_pairs={{0,96},{2,98},{4,100},{6,102},{8,104},{10,106},{12,108},{14,110},{... | collective-permute-start | bytes 786440 | tf_op jit(solution)/shard_map/ppermute | solution.py:30
  52.6 8.3 %collective-permute-start.16 = (bf16[32,2688]{1,0:T(8,128)(2,1)S(1)}, bf16[32,2688]{1,0:T(8,128)(2,1)S(1)}, u32[]{:S(2)}, u32[]{:S(2)}) collective-permute-start(bf16[32,2688]{1,0:T(8,128)(2,1)S(1)} %shard_map.100), channel_id=1, source_target_pairs={{0,5},{1,4},{2,7},{3,6},{4,1},{5,0},{6,3},{7,2},{8,13},{9,12},{10,... | collective-permute-start | bytes 516104 | tf_op jit(solution)/shard_map/ppermute | solution.py:35
  53.9 8.1 %collective-permute-start.15 = (bf16[32,2688]{1,0:T(8,128)(2,1)S(1)}, bf16[32,2688]{1,0:T(8,128)(2,1)S(1)}, u32[]{:S(2)}, u32[]{:S(2)}) collective-permute-start(bf16[32,2688]{1,0:T(8,128)(2,1)S(1)} %shard_map.100), channel_id=1, source_target_pairs={{0,4},{1,5},{2,6},{3,7},{4,0},{5,1},{6,2},{7,3},{8,12},{9,13},{10,... | collective-permute-start | bytes 516104 | tf_op jit(solution)/shard_map/ppermute | solution.py:35
  54.9 8.6 %collective-permute-start.14 = (bf16[32,2688]{1,0:T(8,128)(2,1)S(1)}, bf16[32,2688]{1,0:T(8,128)(2,1)S(1)}, u32[]{:S(2)}, u32[]{:S(2)}) collective-permute-start(bf16[32,2688]{1,0:T(8,128)(2,1)S(1)} %shard_map.100), channel_id=1, source_target_pairs={{0,1},{1,0},{2,3},{3,2},{4,5},{5,4},{6,7},{7,6},{8,9},{9,8},{10,11... | collective-permute-start | bytes 516104 | tf_op jit(solution)/shard_map/ppermute | solution.py:35
  56.2 9.6 %collective-permute-start.20 = (bf16[16,128,256]{2,1,0:T(8,128)(2,1)S(1)}, bf16[16,128,256]{2,1,0:T(8,128)(2,1)S(1)}, u32[]{:S(2)}, u32[]{:S(2)}) collective-permute-start(bf16[16,128,256]{2,1,0:T(8,128)(2,1)S(1)} %shard_map.99.s0), channel_id=1, source_target_pairs={{0,2},{2,0},{4,6},{6,4},{8,10},{10,8},{12,14},{14,12},{16,18},{18,... | collective-permute-start | bytes 3145736 | tf_op jit(solution)/shard_map/ppermute | solution.py:30
  63.6 2.2 %collective-permute-start.19 = (bf16[128,2688]{1,0:T(8,128)(2,1)S(1)}, bf16[128,2688]{1,0:T(8,128)(2,1)S(1)}, u32[]{:S(2)}, u32[]{:S(2)}) collective-permute-start(bf16[128,2688]{1,0:T(8,128)(2,1)S(1)} %constant_dynamic-update-slice_fusion.mine), channel_id=1, source_target_pairs={{0,2},{2,0},{4,6},{6,4},{8,10},{10,8},{12,14},{14,12},{16,18},{18,... | collective-permute-start | bytes 2064392 | tf_op jit(solution)/shard_map/ppermute | solution.py:30
  68.3 4.3 %collective-permute-start.24 = (bf16[16,128,256]{2,1,0:T(8,128)(2,1)S(1)}, bf16[16,128,256]{2,1,0:T(8,128)(2,1)S(1)}, u32[]{:S(2)}, u32[]{:S(2)}) collective-permute-start(bf16[16,128,256]{2,1,0:T(8,128)(2,1)S(1)} %shard_map.101.s2), channel_id=1, source_target_pairs={{0,2},{2,0},{4,6},{6,4},{8,10},{10,8},{12,14},{14,12},{16,18},{18,... | collective-permute-start | bytes 3145736 | tf_op jit(solution)/shard_map/ppermute | solution.py:30
  68.5 10.7 %collective-permute-start.21 = (bf16[64,2048]{1,0:T(8,128)(2,1)S(1)}, bf16[64,2048]{1,0:T(8,128)(2,1)S(1)}, u32[]{:S(2)}, u32[]{:S(2)}) collective-permute-start(bf16[64,2048]{1,0:T(8,128)(2,1)S(1)} %get-tuple-element.80), channel_id=1, source_target_pairs={{0,64},{2,66},{4,68},{6,70},{8,72},{10,74},{12,76},{14,78},{16,80}... | collective-permute-start | bytes 786440 | tf_op jit(solution)/shard_map/ppermute | solution.py:30
  71.0 12.6 %collective-permute-start.22 = (bf16[64,2048]{1,0:T(8,128)(2,1)S(1)}, bf16[64,2048]{1,0:T(8,128)(2,1)S(1)}, u32[]{:S(2)}, u32[]{:S(2)}) collective-permute-start(bf16[64,2048]{1,0:T(8,128)(2,1)S(1)} %get-tuple-element.81), channel_id=1, source_target_pairs={{0,32},{2,34},{4,36},{6,38},{8,40},{10,42},{12,44},{14,46},{16,48}... | collective-permute-start | bytes 786440 | tf_op jit(solution)/shard_map/ppermute | solution.py:30
  71.4 12.9 %collective-permute-start.23 = (bf16[64,2048]{1,0:T(8,128)(2,1)S(1)}, bf16[64,2048]{1,0:T(8,128)(2,1)S(1)}, u32[]{:S(2)}, u32[]{:S(2)}) collective-permute-start(bf16[64,2048]{1,0:T(8,128)(2,1)S(1)} %get-tuple-element.82), channel_id=1, source_target_pairs={{0,96},{2,98},{4,100},{6,102},{8,104},{10,106},{12,108},{14,110},{... | collective-permute-start | bytes 786440 | tf_op jit(solution)/shard_map/ppermute | solution.py:30
  84.4 10.0 %collective-permute-start.25 = (bf16[16,2048]{1,0:T(8,128)(2,1)S(1)}, bf16[16,2048]{1,0:T(8,128)(2,1)S(1)}, u32[]{:S(2)}, u32[]{:S(2)}) collective-permute-start(bf16[16,2048]{1,0:T(8,128)(2,1)S(1)} %get-tuple-element.104), channel_id=1, source_target_pairs={{0,16},{2,18},{4,20},{6,22},{8,24},{10,26},{12,28},{14,30},{16,0},... | collective-permute-start | bytes 196616 | tf_op jit(solution)/shard_map/ppermute | solution.py:30
  87.9 8.0 %collective-permute-start.27 = (bf16[16,2048]{1,0:T(8,128)(2,1)S(1)}, bf16[16,2048]{1,0:T(8,128)(2,1)S(1)}, u32[]{:S(2)}, u32[]{:S(2)}) collective-permute-start(bf16[16,2048]{1,0:T(8,128)(2,1)S(1)} %get-tuple-element.105), channel_id=1, source_target_pairs={{0,24},{2,26},{4,28},{6,30},{8,16},{10,18},{12,20},{14,22},{16,8},... | collective-permute-start | bytes 196616 | tf_op jit(solution)/shard_map/ppermute | solution.py:30
  89.0 6.9 %collective-permute-start.26 = (bf16[16,2048]{1,0:T(8,128)(2,1)S(1)}, bf16[16,2048]{1,0:T(8,128)(2,1)S(1)}, u32[]{:S(2)}, u32[]{:S(2)}) collective-permute-start(bf16[16,2048]{1,0:T(8,128)(2,1)S(1)} %get-tuple-element.106), channel_id=1, source_target_pairs={{0,8},{2,10},{4,12},{6,14},{8,0},{10,2},{12,4},{14,6},{16,24},{18,... | collective-permute-start | bytes 196616 | tf_op jit(solution)/shard_map/ppermute | solution.py:30
  96.0 5.5 %collective-permute-start.28 = (bf16[8,2048]{1,0:T(8,128)(2,1)S(1)}, bf16[8,2048]{1,0:T(8,128)(2,1)S(1)}, u32[]{:S(2)}, u32[]{:S(2)}) collective-permute-start(bf16[8,2048]{1,0:T(8,128)(2,1)S(1)} %slice.73), channel_id=1, source_target_pairs={{0,128},{2,130},{4,132},{6,134},{8,136},{10,138},{12,140},{14,142}... | collective-permute-start | bytes 98312 | tf_op jit(solution)/shard_map/ppermute | solution.py:30
  (1 other events, 1.4 us)
